TPU v7x, 32 devices: a whole 2x2x4 slice. The times are simulated.
32 devices in a mesh: ctx: 8 (over y, x, core), shard: 4 (over z).
Axes of the slice: x: 2, y: 2, z: 4, core: 2. Of those that a mesh axis runs over, the one named last changes fastest.
Arguments:
- tokens: bfloat16 [4096, 640], P(('ctx', 'shard')), may hold values from -36 to 36
- positions: int32 [4096], replicated, may hold values from 0 to 4095, as said below
- cotangent: bfloat16 [4096, 640], P(('ctx', 'shard')), may hold values from -6 to 6
- query_weight: float32 [640, 1024], P('ctx', 'shard'), may hold values from -0.25 to 0.25
- query_first: float32 [640, 1024], P('ctx', 'shard'), may hold values from -112 to 112
- query_second: float32 [640, 1024], P('ctx', 'shard'), may hold values from 40.96 to 4096
- keyval_weight: float32 [2, 640, 256], P(None, 'ctx', 'shard'), may hold values from -0.25 to 0.25
- keyval_first: float32 [2, 640, 256], P(None, 'ctx', 'shard'), may hold values from -112 to 112
- keyval_second: float32 [2, 640, 256], P(None, 'ctx', 'shard'), may hold values from 40.96 to 4096
- output_weight: float32 [1024, 640], P('shard', 'ctx'), may hold values from -0.1875 to 0.1875
- output_first: float32 [1024, 640], P('shard', 'ctx'), may hold values from -112 to 112
- output_second: float32 [1024, 640], P('shard', 'ctx'), may hold values from 40.96 to 4096
- gateup_weight: float32 [2, 640, 2048], P(None, 'ctx', 'shard'), may hold values from -0.25 to 0.25
- gateup_first: float32 [2, 640, 2048], P(None, 'ctx', 'shard'), may hold values from -112 to 112
- gateup_second: float32 [2, 640, 2048], P(None, 'ctx', 'shard'), may hold values from 40.96 to 4096
- down_weight: float32 [2048, 640], P('shard', 'ctx'), may hold values from -0.125 to 0.125
- down_first: float32 [2048, 640], P('shard', 'ctx'), may hold values from -112 to 112
- down_second: float32 [2048, 640], P('shard', 'ctx'), may hold values from 40.96 to 4096
- norm_scales: float32 [4, 640], replicated, may hold values from -0.3 to 0.3
- norm_first: float32 [4, 640], replicated, may hold values from -112 to 112
- norm_second: float32 [4, 640], replicated, may hold values from 40.96 to 4096
- head_scales: float32 [2, 256], replicated, may hold values from -0.3 to 0.3
- head_first: float32 [2, 256], replicated, may hold values from -112 to 112
- head_second: float32 [2, 256], replicated, may hold values from 40.96 to 4096
Outputs:
- block_out: bfloat16 [4096, 640], P(('ctx', 'shard'))
- tokens_grad: bfloat16 [4096, 640], P(('ctx', 'shard'))
- query_grad: float32 [640, 1024], P('ctx', 'shard')
- query_new: float32 [640, 1024], P('ctx', 'shard')
- query_first_new: float32 [640, 1024], P('ctx', 'shard')
- query_second_new: float32 [640, 1024], P('ctx', 'shard')
- keyval_grad: float32 [2, 640, 256], P(None, 'ctx', 'shard')
- keyval_new: float32 [2, 640, 256], P(None, 'ctx', 'shard')
- keyval_first_new: float32 [2, 640, 256], P(None, 'ctx', 'shard')
- keyval_second_new: float32 [2, 640, 256], P(None, 'ctx', 'shard')
- output_grad: float32 [1024, 640], P('shard', 'ctx')
- output_new: float32 [1024, 640], P('shard', 'ctx')
- output_first_new: float32 [1024, 640], P('shard', 'ctx')
- output_second_new: float32 [1024, 640], P('shard', 'ctx')
- gateup_grad: float32 [2, 640, 2048], P(None, 'ctx', 'shard')
- gateup_new: float32 [2, 640, 2048], P(None, 'ctx', 'shard')
- gateup_first_new: float32 [2, 640, 2048], P(None, 'ctx', 'shard')
- gateup_second_new: float32 [2, 640, 2048], P(None, 'ctx', 'shard')
- down_grad: float32 [2048, 640], P('shard', 'ctx')
- down_new: float32 [2048, 640], P('shard', 'ctx')
- down_first_new: float32 [2048, 640], P('shard', 'ctx')
- down_second_new: float32 [2048, 640], P('shard', 'ctx')
- norm_grad: float32 [4, 640], replicated
- norm_new: float32 [4, 640], replicated
- norm_first_new: float32 [4, 640], replicated
- norm_second_new: float32 [4, 640], replicated
- head_grad: float32 [2, 256], replicated
- head_new: float32 [2, 256], replicated
- head_first_new: float32 [2, 256], replicated
- head_second_new: float32 [2, 256], replicated
Inputs may be any that keep to these rules, and one draw needn't show every extreme that they name: A permutation of the 4096 positions in mirrored pairs of blocks of 256: the device at ctx index c and shard index s holds in its first 64 rows the positions b * 256 + s * 64 + r, r counting up, of one block b below 8, and in its other rows the same offsets in block 15 - b; every ctx index has its own b.
All inputs are finite; a program needn't handle non-finite values.
Results may differ from a plain program's by a relative error of at most 0.023.
Values may be sent and summed in bfloat16 or wider, within the bound.
No kernel may reach another device: no remote copies, remote signals or barrier semaphores. Data moves between devices by JAX's collectives and lax.ppermute only.
A program may use at most 256 MiB of HBM per device.

v0:
```python
import jax
import jax.numpy as jnp
from jax import lax
from jax.experimental import pallas as pl
from jax.experimental.pallas import tpu as pltpu
from jax.sharding import PartitionSpec as P

HEADS = 4
HEAD = 256
STEP = 3


norm_eps = 1e-06
rope_base = 1000000.0
score_scale = 0.0625
learn_rate = 0.02
beta_first = 0.9
beta_second = 0.95
adam_eps = 1e-08
weight_decay = 0.1
gelu_coef = 0.7978845608028654
masked_value = -1e30


def rms_forward(values):
    inverse = lax.rsqrt(jnp.mean(values * values, axis=-1, keepdims=True) + norm_eps)
    return (values * inverse, inverse)


def rms_backward(normed, inverse, upstream):
    return inverse * (upstream - normed * jnp.mean(upstream * normed, axis=-1, keepdims=True))


def rotate(values):
    middle = values.shape[-1] // 2
    return jnp.concatenate([-values[..., middle:], values[..., :middle]], axis=-1)


def rotate_back(values):
    middle = values.shape[-1] // 2
    return jnp.concatenate([values[..., middle:], -values[..., :middle]], axis=-1)


def rope_tables(places):
    middle = HEAD // 2
    freqs = rope_base ** (-(jnp.arange(middle, dtype=jnp.float32) * 2.0 / HEAD))
    angles = places.astype(jnp.float32)[:, None] * freqs[None, :]
    cosine = jnp.cos(angles)
    sine = jnp.sin(angles)
    return (jnp.concatenate([cosine, cosine], axis=-1), jnp.concatenate([sine, sine], axis=-1))


def gelu_parts(values):
    inner = gelu_coef * (values + 0.044715 * values * values * values)
    tangent = jnp.tanh(inner)
    result = 0.5 * values * (1.0 + tangent)
    slope = 0.5 * (1.0 + tangent) + 0.5 * values * (1.0 - tangent * tangent) * gelu_coef * (
        1.0 + 3.0 * 0.044715 * values * values
    )
    return (result, slope)


def adam_update(weight, first, second, grad):
    first_new = beta_first * first + (1.0 - beta_first) * grad
    second_new = beta_second * second + (1.0 - beta_second) * grad * grad
    first_hat = first_new / (1.0 - beta_first**STEP)
    second_hat = second_new / (1.0 - beta_second**STEP)
    weight_new = weight - learn_rate * (
        first_hat / (jnp.sqrt(second_hat) + adam_eps) + weight_decay * weight
    )
    return (grad, weight_new, first_new, second_new)


def swap(piece, axis, distance):
    return lax.ppermute(piece, axis, [(i, i ^ distance) for i in range(lax.axis_size(axis))])


def chip_count():
    return lax.axis_size("ctx") // 2


def gather_shard(piece, dim):
    return jnp.concatenate(
        [piece] + [swap(piece, "shard", j) for j in range(1, lax.axis_size("shard"))], axis=dim
    )


def gather_chips(piece, dim):
    return jnp.concatenate(
        [piece] + [swap(piece, "ctx", 2 * k) for k in range(1, chip_count())], axis=dim
    )


def gather_cores(piece, dim):
    return jnp.concatenate([piece, swap(piece, "ctx", 1)], axis=dim)


def tree_sum(terms):
    while len(terms) > 1:
        terms = [terms[i] + terms[i + 1] for i in range(0, len(terms), 2)]
    return terms[0]


def wide_sum(terms):
    return tree_sum([piece.astype(jnp.float32) for piece in terms])


def scatter_cores(terms, dim):
    keep = lax.index_in_dim(terms, 0, dim, keepdims=False)
    send = lax.index_in_dim(terms, 1, dim, keepdims=False)
    return wide_sum([keep, swap(send, "ctx", 1)])


def scatter_chips(terms, dim):
    parts = jnp.split(terms, chip_count(), axis=dim)
    return wide_sum([parts[0]] + [swap(parts[k], "ctx", 2 * k) for k in range(1, len(parts))])


def scatter_shard(terms, dim):
    parts = jnp.split(terms, lax.axis_size("shard"), axis=dim)
    return wide_sum([parts[0]] + [swap(parts[j], "shard", j) for j in range(1, len(parts))])


def gather_rows(piece):
    rows = gather_chips(piece, -2)
    split = rows.reshape(rows.shape[:-2] + (chip_count(), 1, piece.shape[-2], rows.shape[-1]))
    return gather_cores(split, -3).reshape(
        rows.shape[:-2] + (2 * rows.shape[-2], rows.shape[-1])
    )


def scatter_rows(terms):
    chips = chip_count()
    rows = terms.shape[-2] // (2 * chips)
    split = terms.reshape(terms.shape[:-2] + (chips, 2, rows, terms.shape[-1]))
    summed = scatter_cores(split, split.ndim - 3).astype(jnp.bfloat16)
    return scatter_chips(summed.reshape(terms.shape[:-2] + (chips * rows, terms.shape[-1])), -2)


def scatter_weight(terms):
    return scatter_shard(scatter_rows(terms).astype(jnp.bfloat16), -1)


def reduce_small(values):
    for axis in ("ctx", "shard"):
        distance = 1
        while distance < lax.axis_size(axis):
            values = values + swap(values, axis, distance)
            distance *= 2
    return values


def relative_ctx(index):
    return lax.axis_index("ctx") ^ index


def one_hot(source):
    size = source.shape[0]
    return (jnp.arange(size, dtype=jnp.int32)[:, None] == source[None, :]).astype(jnp.bfloat16)


def nn(left, right):
    return jnp.dot(left, right, preferred_element_type=jnp.float32)


def nt(left, right):
    return lax.dot_general(
        left, right, (((1,), (1,)), ((), ())), preferred_element_type=jnp.float32
    )


def tn(left, right):
    return lax.dot_general(
        left, right, (((0,), (0,)), ((), ())), preferred_element_type=jnp.float32
    )


def stack_heads(rows, half_len):
    return jnp.concatenate(
        [
            rows[side * half_len : (side + 1) * half_len, h * HEAD : (h + 1) * HEAD]
            for side in range(2)
            for h in range(HEADS)
        ],
        axis=0,
    )


def key_block(kv_ref, table_ref, block_index, shard_size, part):
    half_blocks = table_ref.shape[0] - 2
    high = (block_index >= half_blocks).astype(jnp.int32)
    at = table_ref[jnp.where(high == 1, 2 * half_blocks - 1 - block_index, block_index)]
    piece = kv_ref[pl.ds(at * shard_size, shard_size), high, :, part * HEAD : (part + 1) * HEAD]
    return piece.reshape(piece.shape[0] * piece.shape[1], HEAD)


def forward_kernel(table_ref, query_ref, kv_ref, out_ref, log_ref, q_s, acc_s, sum_s):
    half_blocks = table_ref.shape[0] - 2
    shard_size = kv_ref.shape[0] // half_blocks
    half_len = kv_ref.shape[2]
    block_len = shard_size * half_len
    side_rows = half_len * HEADS
    own_block = table_ref[half_blocks]
    own_shard = table_ref[half_blocks + 1]
    far_block = 2 * half_blocks - 1 - own_block
    q_s[...] = stack_heads(query_ref[...], half_len)
    acc_s[...] = jnp.zeros_like(acc_s)
    sum_s[...] = jnp.zeros_like(sum_s)
    key_i = lax.broadcasted_iota(jnp.int32, (1, block_len), 1)
    key_in = ((key_i // half_len) ^ own_shard) * half_len + key_i % half_len
    row_i = lax.broadcasted_iota(jnp.int32, (side_rows, 1), 0)
    query_in = own_shard * half_len + row_i % half_len
    offset_in = key_in - query_in

    def attend(unit):
        far = (unit > own_block).astype(jnp.int32)
        block_index = unit - far * (own_block + 1)
        query_block = jnp.where(far == 1, far_block, own_block)
        rows = pl.ds(pl.multiple_of(far * side_rows, side_rows), side_rows)
        keys = key_block(kv_ref, table_ref, block_index, shard_size, 0)
        values = key_block(kv_ref, table_ref, block_index, shard_size, 1)
        scores = nt(q_s[rows, :], keys) * score_scale
        visible = offset_in <= (query_block - block_index) * block_len
        weights = jnp.where(visible, jnp.exp(scores), 0.0)
        return (
            rows,
            jnp.sum(weights, axis=-1, keepdims=True),
            nn(weights.astype(jnp.bfloat16), values),
        )

    def attend_some(first, count):
        for rows, total, mixed in [attend(first + i) for i in range(count)]:
            sum_s[rows, :] += total
            acc_s[rows, :] += mixed

    unit_count = 2 * half_blocks + 1
    group = 4

    def attend_group(index, carry):
        attend_some(index * group, group)
        return carry

    lax.fori_loop(0, unit_count // group, attend_group, 0)
    attend_some(unit_count - unit_count % group, unit_count % group)
    total = sum_s[...]
    result = acc_s[...] / total
    log_ref[...] = jnp.log(total)
    for side in range(2):
        for h in range(HEADS):
            at = (side * HEADS + h) * half_len
            out_ref[side * half_len : (side + 1) * half_len, h * HEAD : (h + 1) * HEAD] = result[
                at : at + half_len, :
            ]


def backward_kernel(
    table_ref,
    query_ref,
    kv_ref,
    out_ref,
    grad_ref,
    log_ref,
    dq_ref,
    dkv_ref,
    q_s,
    do_s,
    acc_s,
    log_s,
    delta_s,
):
    half_blocks = table_ref.shape[0] - 2
    shard_size = kv_ref.shape[0] // half_blocks
    half_len = kv_ref.shape[2]
    block_len = shard_size * half_len
    side_rows = half_len * HEADS
    own_block = table_ref[half_blocks]
    own_shard = table_ref[half_blocks + 1]
    far_block = 2 * half_blocks - 1 - own_block
    q_s[...] = stack_heads(query_ref[...], half_len)
    grads = stack_heads(grad_ref[...], half_len)
    do_s[...] = grads
    outs = stack_heads(out_ref[...], half_len)
    delta_all = jnp.transpose(
        jnp.sum(grads.astype(jnp.float32) * outs, axis=-1, keepdims=True)
    )
    log_all = jnp.transpose(log_ref[...])
    acc_s[...] = jnp.zeros_like(acc_s)
    shape = (shard_size, half_len, HEAD)
    for side in range(2):
        log_s[side] = log_all[:, side * side_rows : (side + 1) * side_rows]
        delta_s[side] = delta_all[:, side * side_rows : (side + 1) * side_rows]
    key_i = lax.broadcasted_iota(jnp.int32, (block_len, 1), 0)
    key_in = ((key_i // half_len) ^ own_shard) * half_len + key_i % half_len
    row_i = lax.broadcasted_iota(jnp.int32, (1, side_rows), 1)
    query_in = own_shard * half_len + row_i % half_len
    offset_in = key_in - query_in

    def attend(unit):
        far = (unit > own_block).astype(jnp.int32)
        block_index = unit - far * (own_block + 1)
        query_block = jnp.where(far == 1, far_block, own_block)
        rows = pl.ds(pl.multiple_of(far * side_rows, side_rows), side_rows)
        high = (block_index >= half_blocks).astype(jnp.int32)
        at = table_ref[jnp.where(high == 1, 2 * half_blocks - 1 - block_index, block_index)]
        keys = key_block(kv_ref, table_ref, block_index, shard_size, 0)
        values = key_block(kv_ref, table_ref, block_index, shard_size, 1)
        queries = q_s[rows, :]
        grad_rows = do_s[rows, :]
        scores = nt(keys, queries) * score_scale
        visible = offset_in <= (query_block - block_index) * block_len
        weights = jnp.where(visible, jnp.exp(scores - log_s[far]), 0.0)
        grad_weights = nt(values, grad_rows)
        grad_scores = (weights * (grad_weights - delta_s[far])).astype(jnp.bfloat16)
        dq = tn(grad_scores, keys)
        dk = nn(grad_scores, queries) * score_scale
        dv = nn(weights.astype(jnp.bfloat16), grad_rows)
        seen = jnp.logical_and(far == 1, block_index <= own_block)
        return (rows, pl.ds(at * shard_size, shard_size), high, seen, dq, dk, dv)

    def attend_some(first, count):
        for rows, devices, high, seen, dq, dk, dv in [attend(first + i) for i in range(count)]:
            acc_s[rows, :] += dq
            for part, value in enumerate((dk, dv)):
                columns = slice(part * HEAD, (part + 1) * HEAD)
                old = dkv_ref[devices, high, :, columns].astype(jnp.float32)
                dkv_ref[devices, high, :, columns] = (
                    value.reshape(shape) + jnp.where(seen, old, 0.0)
                ).astype(jnp.bfloat16)

    def none(block_index, carry):
        at = table_ref[2 * half_blocks - 1 - block_index]
        dkv_ref[pl.ds(at * shard_size, shard_size), 1] = jnp.zeros(
            (shard_size, half_len, 2 * HEAD), jnp.bfloat16
        )
        return carry

    unit_count = 2 * half_blocks + 1
    group = 4

    def attend_group(index, carry):
        attend_some(index * group, group)
        return carry

    lax.fori_loop(0, unit_count // group, attend_group, 0)
    attend_some(unit_count - unit_count % group, unit_count % group)
    lax.fori_loop(far_block + 1, 2 * half_blocks, none, 0)
    result = acc_s[...] * score_scale
    for side in range(2):
        for h in range(HEADS):
            at = (side * HEADS + h) * half_len
            dq_ref[side * half_len : (side + 1) * half_len, h * HEAD : (h + 1) * HEAD] = result[
                at : at + half_len, :
            ]


def whole_spec(space=pltpu.VMEM):
    return pl.BlockSpec(memory_space=space)


def attention_forward(table, queries, kv):
    rows = queries.shape[0] * HEADS
    room = kv.size * 2 + (24 << 20)
    return pl.pallas_call(
        forward_kernel,
        out_shape=(
            jax.ShapeDtypeStruct(queries.shape, jnp.float32),
            jax.ShapeDtypeStruct((rows, 1), jnp.float32),
        ),
        in_specs=[whole_spec(pltpu.SMEM), whole_spec(), whole_spec()],
        out_specs=(whole_spec(), whole_spec()),
        scratch_shapes=[
            pltpu.VMEM((rows, HEAD), jnp.bfloat16),
            pltpu.VMEM((rows, HEAD), jnp.float32),
            pltpu.VMEM((rows, 1), jnp.float32),
        ],
        compiler_params=pltpu.CompilerParams(vmem_limit_bytes=room),
        cost_estimate=pl.CostEstimate(
            flops=12 * rows * kv.size, transcendentals=0, bytes_accessed=8 * kv.size
        ),
        name="attention_forward",
    )(table, queries, kv)


def attention_backward(table, queries, kv, outs, grads, logs):
    rows = queries.shape[0] * HEADS
    room = kv.size * 4 + (24 << 20)
    return pl.pallas_call(
        backward_kernel,
        out_shape=(
            jax.ShapeDtypeStruct(queries.shape, jnp.float32),
            jax.ShapeDtypeStruct(kv.shape, jnp.bfloat16),
        ),
        in_specs=[whole_spec(pltpu.SMEM)] + [whole_spec()] * 5,
        out_specs=(whole_spec(), whole_spec()),
        scratch_shapes=[
            pltpu.VMEM((rows, HEAD), jnp.bfloat16),
            pltpu.VMEM((rows, HEAD), jnp.bfloat16),
            pltpu.VMEM((rows, HEAD), jnp.float32),
            pltpu.VMEM((2, 1, rows // 2), jnp.float32),
            pltpu.VMEM((2, 1, rows // 2), jnp.float32),
        ],
        compiler_params=pltpu.CompilerParams(vmem_limit_bytes=room),
        cost_estimate=pl.CostEstimate(
            flops=12 * rows * kv.size, transcendentals=0, bytes_accessed=12 * kv.size
        ),
        name="attention_backward",
    )(table, queries, kv, outs, grads, logs)


def shards(
    tokens,
    positions,
    cotangent,
    query_weight,
    query_first,
    query_second,
    keyval_weight,
    keyval_first,
    keyval_second,
    output_weight,
    output_first,
    output_second,
    gateup_weight,
    gateup_first,
    gateup_second,
    down_weight,
    down_first,
    down_second,
    norm_scales,
    norm_first,
    norm_second,
    head_scales,
    head_first,
    head_second,
):
    bfloat = jnp.bfloat16
    single = jnp.float32
    ctx_size = lax.axis_size("ctx")
    shard_size = lax.axis_size("shard")
    ctx_at = lax.axis_index("ctx")
    shard_at = lax.axis_index("shard")
    row_count, width = tokens.shape
    half_len = row_count // 2
    block_len = half_len * shard_size
    piece_len = width // ctx_size
    slice_len = HEAD // shard_size

    group_tokens = gather_shard(tokens, 0)
    attn_pieces = gather_shard(
        jnp.concatenate(
            [
                keyval_weight[0].astype(bfloat),
                keyval_weight[1].astype(bfloat),
                query_weight.astype(bfloat),
                output_weight.astype(bfloat).T,
            ],
            axis=-1,
        )[None],
        0,
    )
    ffn_full = gather_rows(
        jnp.stack(
            [
                gateup_weight[0].astype(bfloat),
                gateup_weight[1].astype(bfloat),
                down_weight.astype(bfloat).T,
            ]
        )
    )
    gate_full, up_full, down_full = (ffn_full[0], ffn_full[1], ffn_full[2])

    def side_by_side(start, size):
        return jnp.concatenate(
            [attn_pieces[j, :, start : start + size] for j in range(shard_size)], axis=-1
        )

    keyval_full = gather_rows(side_by_side(0, 2 * slice_len))
    attn_full = gather_rows(
        jnp.stack([side_by_side(2 * slice_len, HEAD), side_by_side(2 * slice_len + HEAD, HEAD)])
    )
    query_full, output_full = (attn_full[0], attn_full[1])

    feature = jnp.arange(width, dtype=jnp.int32)
    feature_map = one_hot(relative_ctx(feature // piece_len) * piece_len + feature % piece_len)
    channel = jnp.arange(2 * HEAD, dtype=jnp.int32)
    channel_map = one_hot(
        ((channel % HEAD) // slice_len ^ shard_at) * (2 * slice_len)
        + (channel // HEAD) * slice_len
        + channel % slice_len
    )
    keyval_sorted = nn(keyval_full, channel_map).astype(bfloat)

    scales = lax.dot_general(
        norm_scales,
        feature_map.astype(single),
        (((1,), (0,)), ((), ())),
        precision=lax.Precision.HIGHEST,
        preferred_element_type=single,
    )
    group_inputs = nn(group_tokens, feature_map)
    inputs = group_inputs[:row_count]
    upstream = nn(cotangent, feature_map)

    ctx_places = lax.dynamic_slice_in_dim(
        positions, ctx_at * shard_size * row_count, shard_size * row_count
    ).reshape(shard_size, row_count)
    piece = jnp.arange(shard_size, dtype=jnp.int32)
    group_at = jnp.sum(
        jnp.where(
            ((piece ^ shard_at)[:, None] == piece[None, :])[:, :, None], ctx_places[None], 0
        ),
        axis=1,
    ).reshape(-1)
    first_at = positions.reshape(ctx_size, shard_size * row_count)[:, 0] // block_len
    rel = jnp.arange(ctx_size, dtype=jnp.int32)
    blocks_rel = jnp.sum(
        jnp.where(relative_ctx(rel)[:, None] == rel[None, :], first_at[None, :], 0), axis=1
    )
    places = jnp.sum(
        jnp.where(blocks_rel[None, :] == rel[:, None], rel[None, :], 0), axis=1
    )
    table = jnp.concatenate(
        [places, blocks_rel[:1], jnp.full((1,), shard_at, jnp.int32)]
    ).astype(jnp.int32)

    group_normed, group_inverse = rms_forward(group_inputs)
    group_in = (group_normed * (1.0 + scales[0])).astype(bfloat)
    normed_in, inverse_in = (group_normed[:row_count], group_inverse[:row_count])
    attn_in = group_in[:row_count]
    group_cosine, group_sine = rope_tables(group_at)
    cosine, sine = (group_cosine[:row_count], group_sine[:row_count])
    keyval_proj = nn(group_in, keyval_sorted)
    group_key_normed, group_key_inverse = rms_forward(keyval_proj[:, :HEAD])
    key_normed, key_inverse = (group_key_normed[:row_count], group_key_inverse[:row_count])
    key_scaled = group_key_normed * (1.0 + head_scales[1])
    keys_own = (key_scaled * group_cosine + rotate(key_scaled) * group_sine).astype(bfloat)
    values_own = keyval_proj[:, HEAD:].astype(bfloat)
    kv_own = jnp.concatenate([keys_own, values_own], axis=-1).reshape(
        shard_size, 2, half_len, 2 * HEAD
    )
    kv_chips = gather_chips(kv_own, 0).reshape(-1, 1, shard_size, 2, half_len, 2 * HEAD)
    kv_all = gather_cores(kv_chips, 1).reshape(-1, 2, half_len, 2 * HEAD)

    query_proj = nn(attn_in, query_full)
    query_normed, query_inverse = rms_forward(query_proj.reshape(row_count, HEADS, HEAD))
    query_scaled = query_normed * (1.0 + head_scales[0])
    query_rows = (
        (query_scaled * cosine[:, None, :] + rotate(query_scaled) * sine[:, None, :])
        .astype(bfloat)
        .reshape(row_count, HEADS * HEAD)
    )
    attn_rows, attn_logs = attention_forward(table, query_rows, kv_all)
    attn_b = attn_rows.astype(bfloat)
    attn_out = nt(attn_b, output_full)
    out_normed, out_inverse = rms_forward(attn_out)
    hidden_in = inputs + out_normed * (1.0 + scales[1])
    mid_normed, mid_inverse = rms_forward(hidden_in)
    ffn_in = (mid_normed * (1.0 + scales[2])).astype(bfloat)
    group_ffn = gather_shard(ffn_in, 0)
    gate_pre = nn(group_ffn, gate_full)
    up_pre = nn(group_ffn, up_full)
    gate_value, gate_slope = gelu_parts(gate_pre)
    hidden_b = (gate_value * up_pre).astype(bfloat)
    ffn_out = scatter_shard(nt(hidden_b, down_full).astype(bfloat), 0)
    ffn_normed, ffn_inverse = rms_forward(ffn_out)
    block_out = nt(
        (hidden_in + ffn_normed * (1.0 + scales[3])).astype(bfloat), feature_map
    ).astype(bfloat)
    grad_norm3 = jnp.sum(upstream * ffn_normed, axis=0)
    ffn_grad = rms_backward(ffn_normed, ffn_inverse, upstream * (1.0 + scales[3])).astype(bfloat)
    group_grad = gather_shard(ffn_grad, 0)
    hidden_grad = nn(group_grad, down_full)
    gate_grad = (hidden_grad * up_pre * gate_slope).astype(bfloat)
    up_grad = (hidden_grad * gate_value).astype(bfloat)
    ffn_in_grad = scatter_shard(
        (nt(gate_grad, gate_full) + nt(up_grad, up_full)).astype(bfloat), 0
    )
    ffn_owned = scatter_rows(
        jnp.stack(
            [
                tn(group_ffn, gate_grad).astype(bfloat),
                tn(group_ffn, up_grad).astype(bfloat),
                tn(group_grad, hidden_b).astype(bfloat),
            ]
        )
    )
    grad_norm2 = jnp.sum(ffn_in_grad * mid_normed, axis=0)
    residual_grad = upstream + rms_backward(mid_normed, mid_inverse, ffn_in_grad * (1.0 + scales[2]))
    grad_norm1 = jnp.sum(residual_grad * out_normed, axis=0)
    attn_out_grad = rms_backward(
        out_normed, out_inverse, residual_grad * (1.0 + scales[1])
    ).astype(bfloat)
    output_wgrad = tn(attn_out_grad, attn_b).astype(bfloat)
    attn_grad_b = nn(attn_out_grad, output_full).astype(bfloat)
    query_parts, kv_terms = attention_backward(
        table, query_rows, kv_all, attn_rows, attn_grad_b, attn_logs
    )
    kv_terms = kv_terms.reshape(-1, 2, shard_size, 2, half_len, 2 * HEAD)
    kv_terms = scatter_cores(kv_terms, 1).astype(bfloat)
    kv_terms = scatter_chips(kv_terms, 0).astype(bfloat)[0]
    kv_grad = scatter_shard(kv_terms, 0).reshape(row_count, 2 * HEAD)
    query_rot_grad = query_parts.reshape(row_count, HEADS, HEAD)
    query_rope_grad = query_rot_grad * cosine[:, None, :] + rotate_back(
        query_rot_grad * sine[:, None, :]
    )
    grad_head0 = jnp.sum(query_rope_grad * query_normed, axis=(0, 1))
    query_proj_grad = (
        rms_backward(query_normed, query_inverse, query_rope_grad * (1.0 + head_scales[0]))
        .reshape(row_count, HEADS * HEAD)
        .astype(bfloat)
    )
    query_wgrad = tn(attn_in, query_proj_grad).astype(bfloat)
    attn_owned = scatter_weight(jnp.stack([query_wgrad, output_wgrad]))
    key_rot_grad = kv_grad[:, :HEAD]
    value_grad = kv_grad[:, HEAD:]
    key_rope_grad = key_rot_grad * cosine + rotate_back(key_rot_grad * sine)
    grad_head1 = jnp.sum(key_rope_grad * key_normed, axis=0)
    key_proj_grad = rms_backward(
        key_normed, key_inverse, key_rope_grad * (1.0 + head_scales[1])
    ).astype(bfloat)
    keyval_proj_grad = jnp.concatenate([key_proj_grad, value_grad.astype(bfloat)], axis=-1)
    keyval_wgrad = nt(tn(attn_in, keyval_proj_grad).astype(bfloat), channel_map).astype(bfloat)
    keyval_owned = scatter_weight(keyval_wgrad)
    attn_in_grad = nt(query_proj_grad, query_full) + nt(keyval_proj_grad, keyval_sorted)
    grad_norm0 = jnp.sum(attn_in_grad * normed_in, axis=0)
    tokens_grad = nt(
        (
            residual_grad
            + rms_backward(normed_in, inverse_in, attn_in_grad * (1.0 + scales[0]))
        ).astype(bfloat),
        feature_map,
    ).astype(bfloat)
    norm_terms = lax.dot_general(
        jnp.stack([grad_norm0, grad_norm1, grad_norm2, grad_norm3]),
        feature_map.astype(single),
        (((1,), (1,)), ((), ())),
        precision=lax.Precision.HIGHEST,
        preferred_element_type=single,
    )
    small = reduce_small(
        jnp.concatenate([norm_terms.reshape(-1), grad_head0, grad_head1]).reshape(-1, 128)
    ).reshape(-1)
    norm_wgrad = small[: 4 * width].reshape(4, width)
    head_wgrad = small[4 * width :].reshape(2, HEAD)

    query_set = adam_update(query_weight, query_first, query_second, attn_owned[0])
    keyval_set = adam_update(
        keyval_weight,
        keyval_first,
        keyval_second,
        jnp.stack([keyval_owned[:, :slice_len], keyval_owned[:, slice_len:]]),
    )
    output_set = adam_update(output_weight, output_first, output_second, attn_owned[1].T)
    gateup_set = adam_update(
        gateup_weight, gateup_first, gateup_second, ffn_owned[:2]
    )
    down_set = adam_update(down_weight, down_first, down_second, ffn_owned[2].T)
    norm_set = adam_update(norm_scales, norm_first, norm_second, norm_wgrad)
    head_set = adam_update(head_scales, head_first, head_second, head_wgrad)
    return (
        (block_out, tokens_grad)
        + query_set
        + keyval_set
        + output_set
        + gateup_set
        + down_set
        + norm_set
        + head_set
    )


def solution(mesh):
    placed = (
        P(("ctx", "shard"), None),
        P(),
        P(("ctx", "shard"), None),
        P("ctx", "shard"),
        P("ctx", "shard"),
        P("ctx", "shard"),
        P(None, "ctx", "shard"),
        P(None, "ctx", "shard"),
        P(None, "ctx", "shard"),
        P("shard", "ctx"),
        P("shard", "ctx"),
        P("shard", "ctx"),
        P(None, "ctx", "shard"),
        P(None, "ctx", "shard"),
        P(None, "ctx", "shard"),
        P("shard", "ctx"),
        P("shard", "ctx"),
        P("shard", "ctx"),
        P(),
        P(),
        P(),
        P(),
        P(),
        P(),
    )
    return jax.shard_map(
        shards,
        mesh=mesh,
        in_specs=placed,
        out_specs=(
            P(("ctx", "shard"), None),
            P(("ctx", "shard"), None),
            P("ctx", "shard"),
            P("ctx", "shard"),
            P("ctx", "shard"),
            P("ctx", "shard"),
            P(None, "ctx", "shard"),
            P(None, "ctx", "shard"),
            P(None, "ctx", "shard"),
            P(None, "ctx", "shard"),
            P("shard", "ctx"),
            P("shard", "ctx"),
            P("shard", "ctx"),
            P("shard", "ctx"),
            P(None, "ctx", "shard"),
            P(None, "ctx", "shard"),
            P(None, "ctx", "shard"),
            P(None, "ctx", "shard"),
            P("shard", "ctx"),
            P("shard", "ctx"),
            P("shard", "ctx"),
            P("shard", "ctx"),
            P(),
            P(),
            P(),
            P(),
            P(),
            P(),
            P(),
            P(),
        ),
        check_vma=False,
    )
```

profile of v0, /device:TPU:0, one launch (start us, length us, event | category | flops | bytes accessed | tf_op | source)
XLA Modules:
  0.0 300.3 jit_solution(1600872289102672475)
XLA Ops:
  3.6 5.1 %collective-permute-start.5 = (bf16[1,80,640]{2,1,0:T(8,128)(2,1)S(1)}, bf16[1,80,640]{2,1,0:T(8,128)(2,1)S(1)}, u32[]{:S(2)}, u32[]{:S(2)}) collective-permute-start(bf16[1,80,640]{2,1,0:T(8,128)(2,1)S(1)} %maximum_bitcast_fusion.2), channel_id=1, source_target_pairs={{0,3},{1,2},{2,1},{3,0},{4,7},{5,6},{6,5},{7,4},{8,11},{9,10},{10,... | collective-permute-start | bytes 307208 | tf_op jit(solution)/shard_map/ppermute | solution.py:75
  9.3 2.3 collective-permute-start.1
  11.6 2.0 collective-permute-start
  18.5 3.2 %collective-permute-done.4 = bf16[1,80,640]{2,1,0:T(8,128)(2,1)S(1)} collective-permute-done((bf16[1,80,640]{2,1,0:T(8,128)(2,1)S(1)}, bf16[1,80,640]{2,1,0:T(8,128)(2,1)S(1)}, u32[]{:S(2)}, u32[]{:S(2)}) %collective-permute-start.4) | collective-permute-done | bytes 102432 | tf_op jit(solution)/shard_map/ppermute | solution.py:75
  21.8 2.5 collective-permute-start.12
  25.0 3.9 %collective-permute-done.1 = bf16[128,640]{1,0:T(8,128)(2,1)S(1)} collective-permute-done((bf16[128,640]{1,0:T(8,128)(2,1)}, bf16[128,640]{1,0:T(8,128)(2,1)S(1)}, u32[]{:S(2)}, u32[]{:S(2)}) %collective-permute-start.1) | collective-permute-done | bytes 163872 | tf_op jit(solution)/shard_map/ppermute | solution.py:75
  36.2 6.0 %collective-permute-done.8 = bf16[2,80,1024]{2,1,0:T(8,128)(2,1)S(1)} collective-permute-done((bf16[2,80,1024]{2,1,0:T(8,128)(2,1)S(1)}, bf16[2,80,1024]{2,1,0:T(8,128)(2,1)S(1)}, u32[]{:S(2)}, u32[]{:S(2)}) %collective-permute-start.8) | collective-permute-done | bytes 327712 | tf_op jit(solution)/shard_map/ppermute | solution.py:75
  42.2 3.6 %collective-permute-done.7 = bf16[2,80,1024]{2,1,0:T(8,128)(2,1)S(1)} collective-permute-done((bf16[2,80,1024]{2,1,0:T(8,128)(2,1)S(1)}, bf16[2,80,1024]{2,1,0:T(8,128)(2,1)S(1)}, u32[]{:S(2)}, u32[]{:S(2)}) %collective-permute-start.7) | collective-permute-done | bytes 327712 | tf_op jit(solution)/shard_map/ppermute | solution.py:75
  56.5 9.5 %collective-permute-done.16 = bf16[4,2,64,512]{3,2,1,0:T(8,128)(2,1)} collective-permute-done((bf16[4,2,64,512]{3,2,1,0:T(8,128)(2,1)S(1)}, bf16[4,2,64,512]{3,2,1,0:T(8,128)(2,1)}, u32[]{:S(2)}, u32[]{:S(2)}) %collective-permute-start.16) | collective-permute-done | bytes 524320 | tf_op jit(solution)/shard_map/ppermute | solution.py:75
  66.5 10.8 %collective-permute-done.15 = bf16[4,2,64,512]{3,2,1,0:T(8,128)(2,1)} collective-permute-done((bf16[4,2,64,512]{3,2,1,0:T(8,128)(2,1)S(1)}, bf16[4,2,64,512]{3,2,1,0:T(8,128)(2,1)}, u32[]{:S(2)}, u32[]{:S(2)}) %collective-permute-start.15) | collective-permute-done | bytes 524320 | tf_op jit(solution)/shard_map/ppermute | solution.py:75
  77.9 3.0 pad_maximum_fusion.1
  82.5 4.5 %collective-permute-done.22 = bf16[3,80,512]{2,1,0:T(8,128)(2,1)} collective-permute-done((bf16[3,80,512]{2,1,0:T(8,128)(2,1)}, bf16[3,80,512]{2,1,0:T(8,128)(2,1)}, u32[]{:S(2)}, u32[]{:S(2)}) %collective-permute-start.22) | collective-permute-done | bytes 245792 | tf_op jit(solution)/shard_map/ppermute | solution.py:75
  87.0 2.1 pad_maximum_fusion.6
  89.1 1.9 fusion.12
  91.0 1.6 copy.107
  92.6 2.0 multiply_reduce_fusion.4
  95.1 2.6 pad_maximum_fusion
  97.7 4.0 %attention_forward.1 = (f32[128,1024]{1,0:T(8,128)S(1)}, f32[512,1]{1,0:T(8,128)S(1)}) custom-call(s32[10]{0:T(128)S(1)} %pad_add_fusion.table_ref, bf16[128,1024]{1,0:T(8,128)(2,1)S(1)} %bitcast.207, bf16[32,2,64,512]{3,2,1,0:T(8,128)(2,1)S(1)} %bitcast.203), custom_call_target="tpu_custom_call" | custom-call | flops 12884901888 | bytes 16777216 | tf_op jit(solution)/shard_map/attention_forward/pallas_call | solution.py:363
  103.9 4.2 %collective-permute-start.18 = (bf16[128,640]{1,0:T(8,128)(2,1)S(1)}, bf16[128,640]{1,0:T(8,128)(2,1)S(1)}, u32[]{:S(2)}, u32[]{:S(2)}) collective-permute-start(bf16[128,640]{1,0:T(8,128)(2,1)S(1)} %multiply_convert_fusion.6), channel_id=1, source_target_pairs={{0,1},{1,0},{2,3},{3,2},{4,5},{5,4},{6,7},{7,6},{8,9},{9,8},{10,11... | collective-permute-start | bytes 491528 | tf_op jit(solution)/shard_map/ppermute | solution.py:75
  108.2 1.6 pad_maximum_fusion.7
  109.8 2.9 collective-permute-done.20
  112.7 6.4 %collective-permute-done.19 = bf16[128,640]{1,0:T(8,128)(2,1)S(1)} collective-permute-done((bf16[128,640]{1,0:T(8,128)(2,1)S(1)}, bf16[128,640]{1,0:T(8,128)(2,1)S(1)}, u32[]{:S(2)}, u32[]{:S(2)}) %collective-permute-start.19) | collective-permute-done | bytes 163872 | tf_op jit(solution)/shard_map/ppermute | solution.py:75
  121.1 2.2 collective-permute-start.27
  124.6 3.9 %collective-permute-done.25 = bf16[128,640]{1,0:T(8,128)(2,1)S(1)} collective-permute-done((bf16[128,640]{1,0:T(8,128)(2,1)S(1)}, bf16[128,640]{1,0:T(8,128)(2,1)S(1)}, u32[]{:S(2)}, u32[]{:S(2)}) %collective-permute-start.25) | collective-permute-done | bytes 163872 | tf_op jit(solution)/shard_map/ppermute | solution.py:75
  128.5 3.5 %collective-permute-done.27 = bf16[128,640]{1,0:T(8,128)(2,1)S(1)} collective-permute-done((bf16[128,640]{1,0:T(8,128)(2,1)S(1)}, bf16[128,640]{1,0:T(8,128)(2,1)S(1)}, u32[]{:S(2)}, u32[]{:S(2)}) %collective-permute-start.27) | collective-permute-done | bytes 163872 | tf_op jit(solution)/shard_map/ppermute | solution.py:75
  132.1 6.6 %collective-permute-done.26 = bf16[128,640]{1,0:T(8,128)(2,1)S(1)} collective-permute-done((bf16[128,640]{1,0:T(8,128)(2,1)S(1)}, bf16[128,640]{1,0:T(8,128)(2,1)S(1)}, u32[]{:S(2)}, u32[]{:S(2)}) %collective-permute-start.26) | collective-permute-done | bytes 163872 | tf_op jit(solution)/shard_map/ppermute | solution.py:75
  141.4 3.2 %collective-permute-start.28 = (bf16[128,640]{1,0:T(8,128)(2,1)S(1)}, bf16[128,640]{1,0:T(8,128)(2,1)S(1)}, u32[]{:S(2)}, u32[]{:S(2)}) collective-permute-start(bf16[128,640]{1,0:T(8,128)(2,1)S(1)} %multiply_convert_fusion.5), channel_id=1, source_target_pairs={{0,1},{1,0},{2,3},{3,2},{4,5},{5,4},{6,7},{7,6},{8,9},{9,8},{10,11... | collective-permute-start | bytes 491528 | tf_op jit(solution)/shard_map/ppermute | solution.py:75
  144.6 4.6 %collective-permute-done.30 = bf16[128,640]{1,0:T(8,128)(2,1)S(1)} collective-permute-done((bf16[128,640]{1,0:T(8,128)(2,1)S(1)}, bf16[128,640]{1,0:T(8,128)(2,1)S(1)}, u32[]{:S(2)}, u32[]{:S(2)}) %collective-permute-start.30) | collective-permute-done | bytes 163872 | tf_op jit(solution)/shard_map/ppermute | solution.py:75
  149.2 4.8 %collective-permute-done.29 = bf16[128,640]{1,0:T(8,128)(2,1)S(1)} collective-permute-done((bf16[128,640]{1,0:T(8,128)(2,1)S(1)}, bf16[128,640]{1,0:T(8,128)(2,1)S(1)}, u32[]{:S(2)}, u32[]{:S(2)}) %collective-permute-start.29) | collective-permute-done | bytes 163872 | tf_op jit(solution)/shard_map/ppermute | solution.py:75
  156.5 2.5 collective-permute-start.33
  163.1 1.9 collective-permute-done.31
  165.0 2.3 collective-permute-done.33
  167.3 7.1 %collective-permute-done.32 = bf16[128,640]{1,0:T(8,128)(2,1)S(1)} collective-permute-done((bf16[128,640]{1,0:T(8,128)(2,1)S(1)}, bf16[128,640]{1,0:T(8,128)(2,1)S(1)}, u32[]{:S(2)}, u32[]{:S(2)}) %collective-permute-start.32) | collective-permute-done | bytes 163872 | tf_op jit(solution)/shard_map/ppermute | solution.py:75
  176.0 8.6 %attention_backward.1 = (f32[128,1024]{1,0:T(8,128)S(1)}, bf16[32,2,64,512]{3,2,1,0:T(8,128)(2,1)S(1)}) custom-call(s32[10]{0:T(128)S(1)} %pad_add_fusion.table_ref, bf16[128,1024]{1,0:T(8,128)(2,1)S(1)} %bitcast.208, bf16[32,2,64,512]{3,2,1,0:T(8,128)(2,1)S(1)} %bitcast.204, f32[128,1024]{1,0:T(8,128)S(1)} %get-tuple-element.34.out_ref, ...), custom_call_target="tpu_custom_call" | custom-call | flops 12884901888 | bytes 25165824 | tf_op jit(solution)/shard_map/attention_backward/pallas_call | solution.py:387
  185.0 1.6 copy-done.2
  188.7 1.6 convolution_convert_fusion.1
  194.6 1.7 collective-permute-start.58
  198.8 4.1 %collective-permute-done.56 = bf16[3,80,512]{2,1,0:T(8,128)(2,1)S(1)} collective-permute-done((bf16[3,80,512]{2,1,0:T(8,128)(2,1)S(1)}, bf16[3,80,512]{2,1,0:T(8,128)(2,1)S(1)}, u32[]{:S(2)}, u32[]{:S(2)}) %collective-permute-start.56) | collective-permute-done | bytes 245792 | tf_op jit(solution)/shard_map/ppermute | solution.py:75
  204.1 4.3 %collective-permute-done.58 = bf16[3,80,512]{2,1,0:T(8,128)(2,1)S(1)} collective-permute-done((bf16[3,80,512]{2,1,0:T(8,128)(2,1)S(1)}, bf16[3,80,512]{2,1,0:T(8,128)(2,1)S(1)}, u32[]{:S(2)}, u32[]{:S(2)}) %collective-permute-start.58) | collective-permute-done | bytes 245792 | tf_op jit(solution)/shard_map/ppermute | solution.py:75
  211.1 4.2 %collective-permute-done.42 = bf16[2,80,1024]{2,1,0:T(8,128)(2,1)S(1)} collective-permute-done((bf16[2,80,1024]{2,1,0:T(8,128)(2,1)S(1)}, bf16[2,80,1024]{2,1,0:T(8,128)(2,1)S(1)}, u32[]{:S(2)}, u32[]{:S(2)}) %collective-permute-start.42) | collective-permute-done | bytes 327712 | tf_op jit(solution)/shard_map/ppermute | solution.py:75
  215.3 6.4 %collective-permute-done.44 = bf16[2,80,1024]{2,1,0:T(8,128)(2,1)S(1)} collective-permute-done((bf16[2,80,1024]{2,1,0:T(8,128)(2,1)S(1)}, bf16[2,80,1024]{2,1,0:T(8,128)(2,1)S(1)}, u32[]{:S(2)}, u32[]{:S(2)}) %collective-permute-start.44) | collective-permute-done | bytes 327712 | tf_op jit(solution)/shard_map/ppermute | solution.py:75
  221.7 1.7 collective-permute-done.43
  225.8 1.7 collective-permute-start.37
  229.4 1.6 collective-permute-start.47
  231.0 1.9 collective-permute-start.46
  233.8 2.0 collective-permute-done.47
  235.8 2.2 collective-permute-done.46
  238.0 1.6 collective-permute-done.35
  239.6 8.5 %collective-permute-done.37 = bf16[1,4,2,64,512]{4,3,2,1,0:T(8,128)(2,1)S(1)} collective-permute-done((bf16[1,4,2,64,512]{4,3,2,1,0:T(8,128)(2,1)S(1)}, bf16[1,4,2,64,512]{4,3,2,1,0:T(8,128)(2,1)S(1)}, u32[]{:S(2)}, u32[]{:S(2)}) %collective-permute-start.37) | collective-permute-done | bytes 524320 | tf_op jit(solution)/shard_map/ppermute | solution.py:75
  249.8 1.8 collective-permute-start.38
  251.6 1.6 collective-permute-start.40
  254.1 2.0 collective-permute-done.38
  256.1 2.3 collective-permute-done.40
  258.4 2.7 collective-permute-done.39
  263.8 1.7 multiply_reduce_fusion.8
  268.3 1.6 convolution_convert_fusion.3
  272.7 2.5 collective-permute-done.61
  275.2 3.7 %collective-permute-done.62 = f32[24,128]{1,0:T(8,128)S(1)} collective-permute-done((f32[24,128]{1,0:T(8,128)S(1)}, f32[24,128]{1,0:T(8,128)S(1)}, u32[]{:S(2)}, u32[]{:S(2)}) %collective-permute-start.62) | collective-permute-done | bytes 12320 | tf_op jit(solution)/shard_map/ppermute | solution.py:75
  279.0 2.2 fusion.16
  281.5 2.0 collective-permute-done.63
  284.4 1.7 collective-permute-start.51
  288.8 1.7 collective-permute-done.51
  292.1 2.2 collective-permute-start.54
  296.1 1.7 collective-permute-done.54
  (358 shorter events, 84.2 us)
Async XLA Ops:
  3.6 14.8 %collective-permute-start.5 = (bf16[1,80,640]{2,1,0:T(8,128)(2,1)S(1)}, bf16[1,80,640]{2,1,0:T(8,128)(2,1)S(1)}, u32[]{:S(2)}, u32[]{:S(2)}) collective-permute-start(bf16[1,80,640]{2,1,0:T(8,128)(2,1)S(1)} %maximum_bitcast_fusion.2), channel_id=1, source_target_pairs={{0,3},{1,2},{2,1},{3,0},{4,7},{5,6},{6,5},{7,4},{8,11},{9,10},{10,... | collective-permute-start | bytes 307208 | tf_op jit(solution)/shard_map/ppermute | solution.py:75
  8.7 13.1 %collective-permute-start.4 = (bf16[1,80,640]{2,1,0:T(8,128)(2,1)S(1)}, bf16[1,80,640]{2,1,0:T(8,128)(2,1)S(1)}, u32[]{:S(2)}, u32[]{:S(2)}) collective-permute-start(bf16[1,80,640]{2,1,0:T(8,128)(2,1)S(1)} %maximum_bitcast_fusion.2), channel_id=1, source_target_pairs={{0,2},{1,3},{2,0},{3,1},{4,6},{5,7},{6,4},{7,5},{8,10},{9,11},{10,... | collective-permute-start | bytes 307208 | tf_op jit(solution)/shard_map/ppermute | solution.py:75
  8.7 13.1 %collective-permute-start.3 = (bf16[1,80,640]{2,1,0:T(8,128)(2,1)S(1)}, bf16[1,80,640]{2,1,0:T(8,128)(2,1)S(1)}, u32[]{:S(2)}, u32[]{:S(2)}) collective-permute-start(bf16[1,80,640]{2,1,0:T(8,128)(2,1)S(1)} %maximum_bitcast_fusion.2), channel_id=1, source_target_pairs={{0,1},{1,0},{2,3},{3,2},{4,5},{5,4},{6,7},{7,6},{8,9},{9,8},{10,11... | collective-permute-start | bytes 307208 | tf_op jit(solution)/shard_map/ppermute | solution.py:75
  9.3 19.5 %collective-permute-start.1 = (bf16[128,640]{1,0:T(8,128)(2,1)}, bf16[128,640]{1,0:T(8,128)(2,1)S(1)}, u32[]{:S(2)}, u32[]{:S(2)}) collective-permute-start(bf16[128,640]{1,0:T(8,128)(2,1)} %param.24), channel_id=1, source_target_pairs={{0,2},{1,3},{2,0},{3,1},{4,6},{5,7},{6,4},{7,5},{8,10},{9,11},{10,... | collective-permute-start | bytes 491528 | tf_op jit(solution)/shard_map/ppermute | solution.py:75
  11.6 18.7 %collective-permute-start = (bf16[128,640]{1,0:T(8,128)(2,1)}, bf16[128,640]{1,0:T(8,128)(2,1)S(1)}, u32[]{:S(2)}, u32[]{:S(2)}) collective-permute-start(bf16[128,640]{1,0:T(8,128)(2,1)} %param.24), channel_id=1, source_target_pairs={{0,1},{1,0},{2,3},{3,2},{4,5},{5,4},{6,7},{7,6},{8,9},{9,8},{10,11... | collective-permute-start | bytes 491528 | tf_op jit(solution)/shard_map/ppermute | solution.py:75
  18.4 13.4 %collective-permute-start.2 = (bf16[128,640]{1,0:T(8,128)(2,1)S(1)}, bf16[128,640]{1,0:T(8,128)(2,1)S(1)}, u32[]{:S(2)}, u32[]{:S(2)}) collective-permute-start(bf16[128,640]{1,0:T(8,128)(2,1)S(1)} %copy-done.60), channel_id=1, source_target_pairs={{0,3},{1,2},{2,1},{3,0},{4,7},{5,6},{6,5},{7,4},{8,11},{9,10},{10,... | collective-permute-start | bytes 491528 | tf_op jit(solution)/shard_map/ppermute | solution.py:75
  21.8 11.4 %collective-permute-start.12 = (bf16[80,512]{1,0:T(8,128)(2,1)S(1)}, bf16[80,512]{1,0:T(8,128)(2,1)S(1)}, u32[]{:S(2)}, u32[]{:S(2)}) collective-permute-start(bf16[80,512]{1,0:T(8,128)(2,1)S(1)} %pad_maximum_fusion.23), channel_id=1, source_target_pairs={{0,24},{4,28},{8,16},{12,20},{16,8},{20,12},{24,0},{28,4},{1,25},{... | collective-permute-start | bytes 245768 | tf_op jit(solution)/shard_map/ppermute | solution.py:75
  24.3 10.4 %collective-permute-start.11 = (bf16[80,512]{1,0:T(8,128)(2,1)S(1)}, bf16[80,512]{1,0:T(8,128)(2,1)S(1)}, u32[]{:S(2)}, u32[]{:S(2)}) collective-permute-start(bf16[80,512]{1,0:T(8,128)(2,1)S(1)} %pad_maximum_fusion.23), channel_id=1, source_target_pairs={{0,16},{4,20},{8,24},{12,28},{16,0},{20,4},{24,8},{28,12},{1,17},{... | collective-permute-start | bytes 245768 | tf_op jit(solution)/shard_map/ppermute | solution.py:75
  28.8 6.0 %collective-permute-start.10 = (bf16[80,512]{1,0:T(8,128)(2,1)S(1)}, bf16[80,512]{1,0:T(8,128)(2,1)S(1)}, u32[]{:S(2)}, u32[]{:S(2)}) collective-permute-start(bf16[80,512]{1,0:T(8,128)(2,1)S(1)} %pad_maximum_fusion.23), channel_id=1, source_target_pairs={{0,8},{4,12},{8,0},{12,4},{16,24},{20,28},{24,16},{28,20},{1,9},{5... | collective-permute-start | bytes 245768 | tf_op jit(solution)/shard_map/ppermute | solution.py:75
  30.3 11.9 %collective-permute-start.8 = (bf16[2,80,1024]{2,1,0:T(8,128)(2,1)S(1)}, bf16[2,80,1024]{2,1,0:T(8,128)(2,1)S(1)}, u32[]{:S(2)}, u32[]{:S(2)}) collective-permute-start(bf16[2,80,1024]{2,1,0:T(8,128)(2,1)S(1)} %pad_maximum_fusion.14), channel_id=1, source_target_pairs={{0,24},{4,28},{8,16},{12,20},{16,8},{20,12},{24,0},{28,4},{1,25},{... | collective-permute-start | bytes 983048 | tf_op jit(solution)/shard_map/ppermute | solution.py:75
  31.8 14.0 %collective-permute-start.7 = (bf16[2,80,1024]{2,1,0:T(8,128)(2,1)S(1)}, bf16[2,80,1024]{2,1,0:T(8,128)(2,1)S(1)}, u32[]{:S(2)}, u32[]{:S(2)}) collective-permute-start(bf16[2,80,1024]{2,1,0:T(8,128)(2,1)S(1)} %pad_maximum_fusion.14), channel_id=1, source_target_pairs={{0,16},{4,20},{8,24},{12,28},{16,0},{20,4},{24,8},{28,12},{1,17},{... | collective-permute-start | bytes 983048 | tf_op jit(solution)/shard_map/ppermute | solution.py:75
  33.2 13.5 %collective-permute-start.6 = (bf16[2,80,1024]{2,1,0:T(8,128)(2,1)S(1)}, bf16[2,80,1024]{2,1,0:T(8,128)(2,1)S(1)}, u32[]{:S(2)}, u32[]{:S(2)}) collective-permute-start(bf16[2,80,1024]{2,1,0:T(8,128)(2,1)S(1)} %pad_maximum_fusion.14), channel_id=1, source_target_pairs={{0,8},{4,12},{8,0},{12,4},{16,24},{20,28},{24,16},{28,20},{1,9},{5... | collective-permute-start | bytes 983048 | tf_op jit(solution)/shard_map/ppermute | solution.py:75
  34.8 12.1 %collective-permute-start.13 = (bf16[4,1,80,512]{3,2,1,0:T(8,128)(2,1)S(1)}, bf16[4,1,80,512]{3,2,1,0:T(8,128)(2,1)S(1)}, u32[]{:S(2)}, u32[]{:S(2)}) collective-permute-start(bf16[4,1,80,512]{3,2,1,0:T(8,128)(2,1)S(1)} %bitcast.234), channel_id=1, source_target_pairs={{0,4},{4,0},{8,12},{12,8},{16,20},{20,16},{24,28},{28,24},{1,5},{5... | collective-permute-start | bytes 983048 | tf_op jit(solution)/shard_map/ppermute | solution.py:75
  46.8 42.3 %collective-permute-start.9 = (bf16[2,4,1,80,1024]{4,3,2,1,0:T(8,128)(2,1)S(1)}, bf16[2,4,1,80,1024]{4,3,2,1,0:T(8,128)(2,1)}, u32[]{:S(2)}, u32[]{:S(2)}) collective-permute-start(bf16[2,4,1,80,1024]{4,3,2,1,0:T(8,128)(2,1)S(1)} %bitcast.217), channel_id=1, source_target_pairs={{0,4},{4,0},{8,12},{12,8},{16,20},{20,16},{24,28},{28,24},{1,5},{5... | collective-permute-start | bytes 3932168 | tf_op jit(solution)/shard_map/ppermute | solution.py:75
  50.2 15.9 %collective-permute-start.16 = (bf16[4,2,64,512]{3,2,1,0:T(8,128)(2,1)S(1)}, bf16[4,2,64,512]{3,2,1,0:T(8,128)(2,1)}, u32[]{:S(2)}, u32[]{:S(2)}) collective-permute-start(bf16[4,2,64,512]{3,2,1,0:T(8,128)(2,1)S(1)} %bitcast.230), channel_id=1, source_target_pairs={{0,24},{4,28},{8,16},{12,20},{16,8},{20,12},{24,0},{28,4},{1,25},{... | collective-permute-start | bytes 1572872 | tf_op jit(solution)/shard_map/ppermute | solution.py:75
  51.4 26.0 %collective-permute-start.15 = (bf16[4,2,64,512]{3,2,1,0:T(8,128)(2,1)S(1)}, bf16[4,2,64,512]{3,2,1,0:T(8,128)(2,1)}, u32[]{:S(2)}, u32[]{:S(2)}) collective-permute-start(bf16[4,2,64,512]{3,2,1,0:T(8,128)(2,1)S(1)} %bitcast.231), channel_id=1, source_target_pairs={{0,16},{4,20},{8,24},{12,28},{16,0},{20,4},{24,8},{28,12},{1,17},{... | collective-permute-start | bytes 1572872 | tf_op jit(solution)/shard_map/ppermute | solution.py:75
  52.2 25.7 %collective-permute-start.14 = (bf16[4,2,64,512]{3,2,1,0:T(8,128)(2,1)S(1)}, bf16[4,2,64,512]{3,2,1,0:T(8,128)(2,1)}, u32[]{:S(2)}, u32[]{:S(2)}) collective-permute-start(bf16[4,2,64,512]{3,2,1,0:T(8,128)(2,1)S(1)} %bitcast.232), channel_id=1, source_target_pairs={{0,8},{4,12},{8,0},{12,4},{16,24},{20,28},{24,16},{28,20},{1,9},{5... | collective-permute-start | bytes 1572872 | tf_op jit(solution)/shard_map/ppermute | solution.py:75
  54.5 28.0 %collective-permute-start.23 = (bf16[3,80,512]{2,1,0:T(8,128)(2,1)}, bf16[3,80,512]{2,1,0:T(8,128)(2,1)S(1)}, u32[]{:S(2)}, u32[]{:S(2)}) collective-permute-start(bf16[3,80,512]{2,1,0:T(8,128)(2,1)} %pad_maximum_fusion.16), channel_id=1, source_target_pairs={{0,24},{4,28},{8,16},{12,20},{16,8},{20,12},{24,0},{28,4},{1,25},{... | collective-permute-start | bytes 737288 | tf_op jit(solution)/shard_map/ppermute | solution.py:75
  66.0 20.9 %collective-permute-start.22 = (bf16[3,80,512]{2,1,0:T(8,128)(2,1)}, bf16[3,80,512]{2,1,0:T(8,128)(2,1)}, u32[]{:S(2)}, u32[]{:S(2)}) collective-permute-start(bf16[3,80,512]{2,1,0:T(8,128)(2,1)} %pad_maximum_fusion.16), channel_id=1, source_target_pairs={{0,16},{4,20},{8,24},{12,28},{16,0},{20,4},{24,8},{28,12},{1,17},{... | collective-permute-start | bytes 737288 | tf_op jit(solution)/shard_map/ppermute | solution.py:75
  77.3 9.6 %collective-permute-start.21 = (bf16[3,80,512]{2,1,0:T(8,128)(2,1)}, bf16[3,80,512]{2,1,0:T(8,128)(2,1)}, u32[]{:S(2)}, u32[]{:S(2)}) collective-permute-start(bf16[3,80,512]{2,1,0:T(8,128)(2,1)} %pad_maximum_fusion.16), channel_id=1, source_target_pairs={{0,8},{4,12},{8,0},{12,4},{16,24},{20,28},{24,16},{28,20},{1,9},{5... | collective-permute-start | bytes 737288 | tf_op jit(solution)/shard_map/ppermute | solution.py:75
  80.9 14.2 %collective-permute-start.17 = (bf16[4,1,4,2,64,512]{5,4,3,2,1,0:T(8,128)(2,1)}, bf16[4,1,4,2,64,512]{5,4,3,2,1,0:T(8,128)(2,1)}, u32[]{:S(2)}, u32[]{:S(2)}) collective-permute-start(bf16[4,1,4,2,64,512]{5,4,3,2,1,0:T(8,128)(2,1)} %bitcast.33), channel_id=1, source_target_pairs={{0,4},{4,0},{8,12},{12,8},{16,20},{20,16},{24,28},{28,24},{1,5},{5... | collective-permute-start | bytes 6291464 | tf_op jit(solution)/shard_map/ppermute | solution.py:75
  89.1 19.1 %collective-permute-start.24 = (bf16[3,4,1,80,512]{4,3,2,1,0:T(8,128)(2,1)}, bf16[3,4,1,80,512]{4,3,2,1,0:T(8,128)(2,1)}, u32[]{:S(2)}, u32[]{:S(2)}) collective-permute-start(bf16[3,4,1,80,512]{4,3,2,1,0:T(8,128)(2,1)} %bitcast.39), channel_id=1, source_target_pairs={{0,4},{4,0},{8,12},{12,8},{16,20},{20,16},{24,28},{28,24},{1,5},{5... | collective-permute-start | bytes 2949128 | tf_op jit(solution)/shard_map/ppermute | solution.py:75
  103.7 9.0 %collective-permute-start.20 = (bf16[128,640]{1,0:T(8,128)(2,1)S(1)}, bf16[128,640]{1,0:T(8,128)(2,1)S(1)}, u32[]{:S(2)}, u32[]{:S(2)}) collective-permute-start(bf16[128,640]{1,0:T(8,128)(2,1)S(1)} %multiply_convert_fusion.6), channel_id=1, source_target_pairs={{0,3},{1,2},{2,1},{3,0},{4,7},{5,6},{6,5},{7,4},{8,11},{9,10},{10,... | collective-permute-start | bytes 491528 | tf_op jit(solution)/shard_map/ppermute | solution.py:75
  103.8 15.3 %collective-permute-start.19 = (bf16[128,640]{1,0:T(8,128)(2,1)S(1)}, bf16[128,640]{1,0:T(8,128)(2,1)S(1)}, u32[]{:S(2)}, u32[]{:S(2)}) collective-permute-start(bf16[128,640]{1,0:T(8,128)(2,1)S(1)} %multiply_convert_fusion.6), channel_id=1, source_target_pairs={{0,2},{1,3},{2,0},{3,1},{4,6},{5,7},{6,4},{7,5},{8,10},{9,11},{10,... | collective-permute-start | bytes 491528 | tf_op jit(solution)/shard_map/ppermute | solution.py:75
  103.9 15.1 %collective-permute-start.18 = (bf16[128,640]{1,0:T(8,128)(2,1)S(1)}, bf16[128,640]{1,0:T(8,128)(2,1)S(1)}, u32[]{:S(2)}, u32[]{:S(2)}) collective-permute-start(bf16[128,640]{1,0:T(8,128)(2,1)S(1)} %multiply_convert_fusion.6), channel_id=1, source_target_pairs={{0,1},{1,0},{2,3},{3,2},{4,5},{5,4},{6,7},{7,6},{8,9},{9,8},{10,11... | collective-permute-start | bytes 491528 | tf_op jit(solution)/shard_map/ppermute | solution.py:75
  121.1 7.5 %collective-permute-start.25 = (bf16[128,640]{1,0:T(8,128)(2,1)S(1)}, bf16[128,640]{1,0:T(8,128)(2,1)S(1)}, u32[]{:S(2)}, u32[]{:S(2)}) collective-permute-start(bf16[128,640]{1,0:T(8,128)(2,1)S(1)} %get-tuple-element.112), channel_id=1, source_target_pairs={{0,1},{1,0},{2,3},{3,2},{4,5},{5,4},{6,7},{7,6},{8,9},{9,8},{10,11... | collective-permute-start | bytes 491528 | tf_op jit(solution)/shard_map/ppermute | solution.py:75
  121.1 10.9 %collective-permute-start.27 = (bf16[128,640]{1,0:T(8,128)(2,1)S(1)}, bf16[128,640]{1,0:T(8,128)(2,1)S(1)}, u32[]{:S(2)}, u32[]{:S(2)}) collective-permute-start(bf16[128,640]{1,0:T(8,128)(2,1)S(1)} %get-tuple-element.113), channel_id=1, source_target_pairs={{0,3},{1,2},{2,1},{3,0},{4,7},{5,6},{6,5},{7,4},{8,11},{9,10},{10,... | collective-permute-start | bytes 491528 | tf_op jit(solution)/shard_map/ppermute | solution.py:75
  123.4 15.3 %collective-permute-start.26 = (bf16[128,640]{1,0:T(8,128)(2,1)S(1)}, bf16[128,640]{1,0:T(8,128)(2,1)S(1)}, u32[]{:S(2)}, u32[]{:S(2)}) collective-permute-start(bf16[128,640]{1,0:T(8,128)(2,1)S(1)} %get-tuple-element.114), channel_id=1, source_target_pairs={{0,2},{1,3},{2,0},{3,1},{4,6},{5,7},{6,4},{7,5},{8,10},{9,11},{10,... | collective-permute-start | bytes 491528 | tf_op jit(solution)/shard_map/ppermute | solution.py:75
  140.1 9.1 %collective-permute-start.30 = (bf16[128,640]{1,0:T(8,128)(2,1)S(1)}, bf16[128,640]{1,0:T(8,128)(2,1)S(1)}, u32[]{:S(2)}, u32[]{:S(2)}) collective-permute-start(bf16[128,640]{1,0:T(8,128)(2,1)S(1)} %multiply_convert_fusion.5), channel_id=1, source_target_pairs={{0,3},{1,2},{2,1},{3,0},{4,7},{5,6},{6,5},{7,4},{8,11},{9,10},{10,... | collective-permute-start | bytes 491528 | tf_op jit(solution)/shard_map/ppermute | solution.py:75
  141.4 12.6 %collective-permute-start.29 = (bf16[128,640]{1,0:T(8,128)(2,1)S(1)}, bf16[128,640]{1,0:T(8,128)(2,1)S(1)}, u32[]{:S(2)}, u32[]{:S(2)}) collective-permute-start(bf16[128,640]{1,0:T(8,128)(2,1)S(1)} %multiply_convert_fusion.5), channel_id=1, source_target_pairs={{0,2},{1,3},{2,0},{3,1},{4,6},{5,7},{6,4},{7,5},{8,10},{9,11},{10,... | collective-permute-start | bytes 491528 | tf_op jit(solution)/shard_map/ppermute | solution.py:75
  141.4 12.6 %collective-permute-start.28 = (bf16[128,640]{1,0:T(8,128)(2,1)S(1)}, bf16[128,640]{1,0:T(8,128)(2,1)S(1)}, u32[]{:S(2)}, u32[]{:S(2)}) collective-permute-start(bf16[128,640]{1,0:T(8,128)(2,1)S(1)} %multiply_convert_fusion.5), channel_id=1, source_target_pairs={{0,1},{1,0},{2,3},{3,2},{4,5},{5,4},{6,7},{7,6},{8,9},{9,8},{10,11... | collective-permute-start | bytes 491528 | tf_op jit(solution)/shard_map/ppermute | solution.py:75
  156.4 8.5 %collective-permute-start.31 = (bf16[128,640]{1,0:T(8,128)(2,1)S(1)}, bf16[128,640]{1,0:T(8,128)(2,1)S(1)}, u32[]{:S(2)}, u32[]{:S(2)}) collective-permute-start(bf16[128,640]{1,0:T(8,128)(2,1)S(1)} %get-tuple-element.109), channel_id=1, source_target_pairs={{0,1},{1,0},{2,3},{3,2},{4,5},{5,4},{6,7},{7,6},{8,9},{9,8},{10,11... | collective-permute-start | bytes 491528 | tf_op jit(solution)/shard_map/ppermute | solution.py:75
  156.5 10.7 %collective-permute-start.33 = (bf16[128,640]{1,0:T(8,128)(2,1)S(1)}, bf16[128,640]{1,0:T(8,128)(2,1)S(1)}, u32[]{:S(2)}, u32[]{:S(2)}) collective-permute-start(bf16[128,640]{1,0:T(8,128)(2,1)S(1)} %get-tuple-element.110), channel_id=1, source_target_pairs={{0,3},{1,2},{2,1},{3,0},{4,7},{5,6},{6,5},{7,4},{8,11},{9,10},{10,... | collective-permute-start | bytes 491528 | tf_op jit(solution)/shard_map/ppermute | solution.py:75
  159.1 15.2 %collective-permute-start.32 = (bf16[128,640]{1,0:T(8,128)(2,1)S(1)}, bf16[128,640]{1,0:T(8,128)(2,1)S(1)}, u32[]{:S(2)}, u32[]{:S(2)}) collective-permute-start(bf16[128,640]{1,0:T(8,128)(2,1)S(1)} %get-tuple-element.111), channel_id=1, source_target_pairs={{0,2},{1,3},{2,0},{3,1},{4,6},{5,7},{6,4},{7,5},{8,10},{9,11},{10,... | collective-permute-start | bytes 491528 | tf_op jit(solution)/shard_map/ppermute | solution.py:75
  163.1 28.2 %collective-permute-start.55 = (bf16[3,4,80,512]{3,2,1,0:T(8,128)(2,1)}, bf16[3,4,80,512]{3,2,1,0:T(8,128)(2,1)}, u32[]{:S(2)}, u32[]{:S(2)}) collective-permute-start(bf16[3,4,80,512]{3,2,1,0:T(8,128)(2,1)} %slice_bitcast_fusion.2), channel_id=1, source_target_pairs={{0,4},{4,0},{8,12},{12,8},{16,20},{20,16},{24,28},{28,24},{1,5},{5... | collective-permute-start | bytes 2949128 | tf_op jit(solution)/shard_map/ppermute | solution.py:75
  190.4 7.2 %collective-permute-start.41 = (bf16[2,4,80,1024]{3,2,1,0:T(8,128)(2,1)S(1)}, bf16[2,4,80,1024]{3,2,1,0:T(8,128)(2,1)S(1)}, u32[]{:S(2)}, u32[]{:S(2)}) collective-permute-start(bf16[2,4,80,1024]{3,2,1,0:T(8,128)(2,1)S(1)} %fusion.13), channel_id=1, source_target_pairs={{0,4},{4,0},{8,12},{12,8},{16,20},{20,16},{24,28},{28,24},{1,5},{5... | collective-permute-start | bytes 3932168 | tf_op jit(solution)/shard_map/ppermute | solution.py:75
  191.2 32.5 %collective-permute-start.34 = (bf16[4,4,2,64,512]{4,3,2,1,0:T(8,128)(2,1)S(1)}, bf16[4,4,2,64,512]{4,3,2,1,0:T(8,128)(2,1)S(1)}, u32[]{:S(2)}, u32[]{:S(2)}) collective-permute-start(bf16[4,4,2,64,512]{4,3,2,1,0:T(8,128)(2,1)S(1)} %slice_bitcast_fusion), channel_id=1, source_target_pairs={{0,4},{4,0},{8,12},{12,8},{16,20},{20,16},{24,28},{28,24},{1,5},{5... | collective-permute-start | bytes 6291464 | tf_op jit(solution)/shard_map/ppermute | solution.py:75
  194.0 8.9 %collective-permute-start.56 = (bf16[3,80,512]{2,1,0:T(8,128)(2,1)S(1)}, bf16[3,80,512]{2,1,0:T(8,128)(2,1)S(1)}, u32[]{:S(2)}, u32[]{:S(2)}) collective-permute-start(bf16[3,80,512]{2,1,0:T(8,128)(2,1)S(1)} %get-tuple-element.104), channel_id=1, source_target_pairs={{0,8},{4,12},{8,0},{12,4},{16,24},{20,28},{24,16},{28,20},{1,9},{5... | collective-permute-start | bytes 737288 | tf_op jit(solution)/shard_map/ppermute | solution.py:75
  194.6 13.8 %collective-permute-start.58 = (bf16[3,80,512]{2,1,0:T(8,128)(2,1)S(1)}, bf16[3,80,512]{2,1,0:T(8,128)(2,1)S(1)}, u32[]{:S(2)}, u32[]{:S(2)}) collective-permute-start(bf16[3,80,512]{2,1,0:T(8,128)(2,1)S(1)} %get-tuple-element.105), channel_id=1, source_target_pairs={{0,24},{4,28},{8,16},{12,20},{16,8},{20,12},{24,0},{28,4},{1,25},{... | collective-permute-start | bytes 737288 | tf_op jit(solution)/shard_map/ppermute | solution.py:75
  196.3 14.6 %collective-permute-start.57 = (bf16[3,80,512]{2,1,0:T(8,128)(2,1)S(1)}, bf16[3,80,512]{2,1,0:T(8,128)(2,1)S(1)}, u32[]{:S(2)}, u32[]{:S(2)}) collective-permute-start(bf16[3,80,512]{2,1,0:T(8,128)(2,1)S(1)} %get-tuple-element.106), channel_id=1, source_target_pairs={{0,16},{4,20},{8,24},{12,28},{16,0},{20,4},{24,8},{28,12},{1,17},{... | collective-permute-start | bytes 737288 | tf_op jit(solution)/shard_map/ppermute | solution.py:75
  198.3 17.0 %collective-permute-start.42 = (bf16[2,80,1024]{2,1,0:T(8,128)(2,1)S(1)}, bf16[2,80,1024]{2,1,0:T(8,128)(2,1)S(1)}, u32[]{:S(2)}, u32[]{:S(2)}) collective-permute-start(bf16[2,80,1024]{2,1,0:T(8,128)(2,1)S(1)} %get-tuple-element.101), channel_id=1, source_target_pairs={{0,8},{4,12},{8,0},{12,4},{16,24},{20,28},{24,16},{28,20},{1,9},{5... | collective-permute-start | bytes 983048 | tf_op jit(solution)/shard_map/ppermute | solution.py:75
  202.9 18.7 %collective-permute-start.44 = (bf16[2,80,1024]{2,1,0:T(8,128)(2,1)S(1)}, bf16[2,80,1024]{2,1,0:T(8,128)(2,1)S(1)}, u32[]{:S(2)}, u32[]{:S(2)}) collective-permute-start(bf16[2,80,1024]{2,1,0:T(8,128)(2,1)S(1)} %get-tuple-element.102), channel_id=1, source_target_pairs={{0,24},{4,28},{8,16},{12,20},{16,8},{20,12},{24,0},{28,4},{1,25},{... | collective-permute-start | bytes 983048 | tf_op jit(solution)/shard_map/ppermute | solution.py:75
  208.4 14.9 %collective-permute-start.43 = (bf16[2,80,1024]{2,1,0:T(8,128)(2,1)S(1)}, bf16[2,80,1024]{2,1,0:T(8,128)(2,1)S(1)}, u32[]{:S(2)}, u32[]{:S(2)}) collective-permute-start(bf16[2,80,1024]{2,1,0:T(8,128)(2,1)S(1)} %get-tuple-element.103), channel_id=1, source_target_pairs={{0,16},{4,20},{8,24},{12,28},{16,0},{20,4},{24,8},{28,12},{1,17},{... | collective-permute-start | bytes 983048 | tf_op jit(solution)/shard_map/ppermute | solution.py:75
  223.6 7.4 %collective-permute-start.45 = (bf16[2,80,256]{2,1,0:T(8,128)(2,1)S(1)}, bf16[2,80,256]{2,1,0:T(8,128)(2,1)S(1)}, u32[]{:S(2)}, u32[]{:S(2)}) collective-permute-start(bf16[2,80,256]{2,1,0:T(8,128)(2,1)S(1)} %get-tuple-element.127), channel_id=1, source_target_pairs={{0,1},{1,0},{2,3},{3,2},{4,5},{5,4},{6,7},{7,6},{8,9},{9,8},{10,11... | collective-permute-start | bytes 245768 | tf_op jit(solution)/shard_map/ppermute | solution.py:75
  224.7 14.9 %collective-permute-start.35 = (bf16[1,4,2,64,512]{4,3,2,1,0:T(8,128)(2,1)S(1)}, bf16[1,4,2,64,512]{4,3,2,1,0:T(8,128)(2,1)S(1)}, u32[]{:S(2)}, u32[]{:S(2)}) collective-permute-start(bf16[1,4,2,64,512]{4,3,2,1,0:T(8,128)(2,1)S(1)} %get-tuple-element.93), channel_id=1, source_target_pairs={{0,8},{4,12},{8,0},{12,4},{16,24},{20,28},{24,16},{28,20},{1,9},{5... | collective-permute-start | bytes 1572872 | tf_op jit(solution)/shard_map/ppermute | solution.py:75
  225.8 22.3 %collective-permute-start.37 = (bf16[1,4,2,64,512]{4,3,2,1,0:T(8,128)(2,1)S(1)}, bf16[1,4,2,64,512]{4,3,2,1,0:T(8,128)(2,1)S(1)}, u32[]{:S(2)}, u32[]{:S(2)}) collective-permute-start(bf16[1,4,2,64,512]{4,3,2,1,0:T(8,128)(2,1)S(1)} %get-tuple-element.94), channel_id=1, source_target_pairs={{0,24},{4,28},{8,16},{12,20},{16,8},{20,12},{24,0},{28,4},{1,25},{... | collective-permute-start | bytes 1572872 | tf_op jit(solution)/shard_map/ppermute | solution.py:75
  227.5 22.0 %collective-permute-start.36 = (bf16[1,4,2,64,512]{4,3,2,1,0:T(8,128)(2,1)S(1)}, bf16[1,4,2,64,512]{4,3,2,1,0:T(8,128)(2,1)S(1)}, u32[]{:S(2)}, u32[]{:S(2)}) collective-permute-start(bf16[1,4,2,64,512]{4,3,2,1,0:T(8,128)(2,1)S(1)} %get-tuple-element.95), channel_id=1, source_target_pairs={{0,16},{4,20},{8,24},{12,28},{16,0},{20,4},{24,8},{28,12},{1,17},{... | collective-permute-start | bytes 1572872 | tf_op jit(solution)/shard_map/ppermute | solution.py:75
  229.4 6.3 %collective-permute-start.47 = (bf16[2,80,256]{2,1,0:T(8,128)(2,1)S(1)}, bf16[2,80,256]{2,1,0:T(8,128)(2,1)S(1)}, u32[]{:S(2)}, u32[]{:S(2)}) collective-permute-start(bf16[2,80,256]{2,1,0:T(8,128)(2,1)S(1)} %get-tuple-element.128), channel_id=1, source_target_pairs={{0,3},{1,2},{2,1},{3,0},{4,7},{5,6},{6,5},{7,4},{8,11},{9,10},{10,... | collective-permute-start | bytes 245768 | tf_op jit(solution)/shard_map/ppermute | solution.py:75
  231.0 6.9 %collective-permute-start.46 = (bf16[2,80,256]{2,1,0:T(8,128)(2,1)S(1)}, bf16[2,80,256]{2,1,0:T(8,128)(2,1)S(1)}, u32[]{:S(2)}, u32[]{:S(2)}) collective-permute-start(bf16[2,80,256]{2,1,0:T(8,128)(2,1)S(1)} %get-tuple-element.129), channel_id=1, source_target_pairs={{0,2},{1,3},{2,0},{3,1},{4,6},{5,7},{6,4},{7,5},{8,10},{9,11},{10,... | collective-permute-start | bytes 245768 | tf_op jit(solution)/shard_map/ppermute | solution.py:75
  249.8 6.3 %collective-permute-start.38 = (bf16[1,2,64,512]{3,2,1,0:T(8,128)(2,1)S(1)}, bf16[1,2,64,512]{3,2,1,0:T(8,128)(2,1)S(1)}, u32[]{:S(2)}, u32[]{:S(2)}) collective-permute-start(bf16[1,2,64,512]{3,2,1,0:T(8,128)(2,1)S(1)} %get-tuple-element.120), channel_id=1, source_target_pairs={{0,1},{1,0},{2,3},{3,2},{4,5},{5,4},{6,7},{7,6},{8,9},{9,8},{10,11... | collective-permute-start | bytes 393224 | tf_op jit(solution)/shard_map/ppermute | solution.py:75
  251.6 6.8 %collective-permute-start.40 = (bf16[1,2,64,512]{3,2,1,0:T(8,128)(2,1)S(1)}, bf16[1,2,64,512]{3,2,1,0:T(8,128)(2,1)S(1)}, u32[]{:S(2)}, u32[]{:S(2)}) collective-permute-start(bf16[1,2,64,512]{3,2,1,0:T(8,128)(2,1)S(1)} %get-tuple-element.121), channel_id=1, source_target_pairs={{0,3},{1,2},{2,1},{3,0},{4,7},{5,6},{6,5},{7,4},{8,11},{9,10},{10,... | collective-permute-start | bytes 393224 | tf_op jit(solution)/shard_map/ppermute | solution.py:75
  253.2 8.0 %collective-permute-start.39 = (bf16[1,2,64,512]{3,2,1,0:T(8,128)(2,1)S(1)}, bf16[1,2,64,512]{3,2,1,0:T(8,128)(2,1)S(1)}, u32[]{:S(2)}, u32[]{:S(2)}) collective-permute-start(bf16[1,2,64,512]{3,2,1,0:T(8,128)(2,1)S(1)} %get-tuple-element.122), channel_id=1, source_target_pairs={{0,2},{1,3},{2,0},{3,1},{4,6},{5,7},{6,4},{7,5},{8,10},{9,11},{10,... | collective-permute-start | bytes 393224 | tf_op jit(solution)/shard_map/ppermute | solution.py:75
  266.4 1.2 collective-permute-start.59
  267.7 3.8 %collective-permute-start.60 = (f32[24,128]{1,0:T(8,128)S(1)}, f32[24,128]{1,0:T(8,128)S(1)}, u32[]{:S(2)}, u32[]{:S(2)}) collective-permute-start(f32[24,128]{1,0:T(8,128)S(1)} %fusion.171), channel_id=1, source_target_pairs={{0,8},{4,12},{8,0},{12,4},{16,24},{20,28},{24,16},{28,20},{1,9},{5... | collective-permute-start | bytes 36872 | tf_op jit(solution)/shard_map/ppermute | solution.py:75
  271.4 3.8 %collective-permute-start.61 = (f32[24,128]{1,0:T(8,128)S(1)}, f32[24,128]{1,0:T(8,128)S(1)}, u32[]{:S(2)}, u32[]{:S(2)}) collective-permute-start(f32[24,128]{1,0:T(8,128)S(1)} %fusion.172), channel_id=1, source_target_pairs={{0,16},{4,20},{8,24},{12,28},{16,0},{20,4},{24,8},{28,12},{1,17},{... | collective-permute-start | bytes 36872 | tf_op jit(solution)/shard_map/ppermute | solution.py:75
  272.6 11.0 %collective-permute-start.48 = (bf16[4,80,512]{1,2,0:T(8,128)(2,1)S(1)}, bf16[4,80,512]{1,2,0:T(8,128)(2,1)S(1)}, u32[]{:S(2)}, u32[]{:S(2)}) collective-permute-start(bf16[4,80,512]{1,2,0:T(8,128)(2,1)S(1)} %bitcast.245), channel_id=1, source_target_pairs={{0,4},{4,0},{8,12},{12,8},{16,20},{20,16},{24,28},{28,24},{1,5},{5... | collective-permute-start | bytes 983048 | tf_op jit(solution)/shard_map/ppermute | solution.py:75
  275.2 3.7 %collective-permute-start.62 = (f32[24,128]{1,0:T(8,128)S(1)}, f32[24,128]{1,0:T(8,128)S(1)}, u32[]{:S(2)}, u32[]{:S(2)}) collective-permute-start(f32[24,128]{1,0:T(8,128)S(1)} %add.518), channel_id=1, source_target_pairs={{0,1},{1,0},{2,3},{3,2},{4,5},{5,4},{6,7},{7,6},{8,9},{9,8},{10,11... | collective-permute-start | bytes 36872 | tf_op jit(solution)/shard_map/ppermute | solution.py:75
  278.9 4.6 %collective-permute-start.63 = (f32[24,128]{1,0:T(8,128)S(1)}, f32[24,128]{1,0:T(8,128)S(1)}, u32[]{:S(2)}, u32[]{:S(2)}) collective-permute-start(f32[24,128]{1,0:T(8,128)S(1)} %add.519), channel_id=1, source_target_pairs={{0,2},{1,3},{2,0},{3,1},{4,6},{5,7},{6,4},{7,5},{8,10},{9,11},{10,... | collective-permute-start | bytes 36872 | tf_op jit(solution)/shard_map/ppermute | solution.py:75
  283.8 5.0 %collective-permute-start.49 = (bf16[80,512]{0,1:T(8,128)(2,1)S(1)}, bf16[80,512]{0,1:T(8,128)(2,1)S(1)}, u32[]{:S(2)}, u32[]{:S(2)}) collective-permute-start(bf16[80,512]{0,1:T(8,128)(2,1)S(1)} %get-tuple-element.115), channel_id=1, source_target_pairs={{0,8},{4,12},{8,0},{12,4},{16,24},{20,28},{24,16},{28,20},{1,9},{5... | collective-permute-start | bytes 245768 | tf_op jit(solution)/shard_map/ppermute | solution.py:75
  284.4 6.1 %collective-permute-start.51 = (bf16[80,512]{0,1:T(8,128)(2,1)S(1)}, bf16[80,512]{0,1:T(8,128)(2,1)S(1)}, u32[]{:S(2)}, u32[]{:S(2)}) collective-permute-start(bf16[80,512]{0,1:T(8,128)(2,1)S(1)} %get-tuple-element.116), channel_id=1, source_target_pairs={{0,24},{4,28},{8,16},{12,20},{16,8},{20,12},{24,0},{28,4},{1,25},{... | collective-permute-start | bytes 245768 | tf_op jit(solution)/shard_map/ppermute | solution.py:75
  286.1 5.8 %collective-permute-start.50 = (bf16[80,512]{0,1:T(8,128)(2,1)S(1)}, bf16[80,512]{0,1:T(8,128)(2,1)S(1)}, u32[]{:S(2)}, u32[]{:S(2)}) collective-permute-start(bf16[80,512]{0,1:T(8,128)(2,1)S(1)} %get-tuple-element.117), channel_id=1, source_target_pairs={{0,16},{4,20},{8,24},{12,28},{16,0},{20,4},{24,8},{28,12},{1,17},{... | collective-permute-start | bytes 245768 | tf_op jit(solution)/shard_map/ppermute | solution.py:75
  291.9 4.2 %collective-permute-start.52 = (bf16[80,128]{0,1:T(8,128)(2,1)S(1)}, bf16[80,128]{0,1:T(8,128)(2,1)S(1)}, u32[]{:S(2)}, u32[]{:S(2)}) collective-permute-start(bf16[80,128]{0,1:T(8,128)(2,1)S(1)} %get-tuple-element.130), channel_id=1, source_target_pairs={{0,1},{1,0},{2,3},{3,2},{4,5},{5,4},{6,7},{7,6},{8,9},{9,8},{10,11... | collective-permute-start | bytes 61448 | tf_op jit(solution)/shard_map/ppermute | solution.py:75
  292.1 5.7 %collective-permute-start.54 = (bf16[80,128]{0,1:T(8,128)(2,1)S(1)}, bf16[80,128]{0,1:T(8,128)(2,1)S(1)}, u32[]{:S(2)}, u32[]{:S(2)}) collective-permute-start(bf16[80,128]{0,1:T(8,128)(2,1)S(1)} %get-tuple-element.131), channel_id=1, source_target_pairs={{0,3},{1,2},{2,1},{3,0},{4,7},{5,6},{6,5},{7,4},{8,11},{9,10},{10,... | collective-permute-start | bytes 61448 | tf_op jit(solution)/shard_map/ppermute | solution.py:75
  294.3 5.0 %collective-permute-start.53 = (bf16[80,128]{0,1:T(8,128)(2,1)S(1)}, bf16[80,128]{0,1:T(8,128)(2,1)S(1)}, u32[]{:S(2)}, u32[]{:S(2)}) collective-permute-start(bf16[80,128]{0,1:T(8,128)(2,1)S(1)} %get-tuple-element.132), channel_id=1, source_target_pairs={{0,2},{1,3},{2,0},{3,1},{4,6},{5,7},{6,4},{7,5},{8,10},{9,11},{10,... | collective-permute-start | bytes 61448 | tf_op jit(solution)/shard_map/ppermute | solution.py:75
  (63 other events, 730.4 us)
where the time goes:
time: 301 us; the launch traced here: 300 us
  waiting for transfers between devices  148 us (49%)
  starting transfers between devices  66.3 us (22%)
  other arithmetic  33.6 us (11%)
  matrix products  23.3 us (8%)
  local copies, waits for them, and re-layouts  14.1 us (5%)
  Pallas kernels  12.6 us (4%)
    ppermute x64, waiting for transfers between devices, swap(): lax.ppermute(piece, axis, [(i, i ^ distance) for i in range(lax.axis_size...  148 us
    ppermute x64, starting transfers between devices, swap(): lax.ppermute(piece, axis, [(i, i ^ distance) for i in range(lax.axis_size...  66.3 us
    dot_general x9, matrix products, nt(): lax.dot_general(left, right, (((1,), (1,)), ((), ())), preferred_element_...  9.49 us
    pallas_call x1, Pallas kernels, attention_backward(): pl.pallas_call(backward_kernel, out_shape=(jax.ShapeDtypeStruct(queries.s...  8.56 us
    dot_general x9, matrix products, nn(): return jnp.dot(left, right, preferred_element_type=jnp.float32)  7.98 us
    unnamed x127, local copies, waits for them, and re-layouts  6.68 us
    concatenate x4, other arithmetic, gather_cores(): return jnp.concatenate([piece, swap(piece, 'ctx', 1)], axis=dim)  6.23 us
  transfers between devices with their start and end apart: 64, of which 42 were waited for; matrix products, arithmetic and copies ran while one was open for 17% of the time, Pallas kernels for 4%

commit v1 on v0

--- a/solution.py
+++ b/solution.py
@@ -79,16 +79,22 @@
     return lax.axis_size("ctx") // 2
 
 
+def after(value, marks):
+    return lax.optimization_barrier((value, marks))[0]
+
+
 def gather_shard(piece, dim):
-    return jnp.concatenate(
-        [piece] + [swap(piece, "shard", j) for j in range(1, lax.axis_size("shard"))], axis=dim
-    )
-
-
-def gather_chips(piece, dim):
-    return jnp.concatenate(
-        [piece] + [swap(piece, "ctx", 2 * k) for k in range(1, chip_count())], axis=dim
-    )
+    got = [swap(piece, "shard", j) for j in range(1, lax.axis_size("shard"))]
+    return (jnp.concatenate([piece] + got, axis=dim), got)
+
+
+def gather_pair(piece, dim):
+    return jnp.concatenate([piece, swap(piece, "shard", 1)], axis=dim)
+
+
+def scatter_pair(terms):
+    keep, send = jnp.split(terms, 2, axis=0)
+    return keep + swap(send.astype(jnp.bfloat16), "shard", 1).astype(jnp.float32)
 
 
 def gather_cores(piece, dim):
@@ -113,7 +119,8 @@
 
 def scatter_chips(terms, dim):
     parts = jnp.split(terms, chip_count(), axis=dim)
-    return wide_sum([parts[0]] + [swap(parts[k], "ctx", 2 * k) for k in range(1, len(parts))])
+    got = [swap(parts[k], "ctx", 2 * k) for k in range(1, len(parts))]
+    return (wide_sum([parts[0]] + got), got)
 
 
 def scatter_shard(terms, dim):
@@ -121,33 +128,83 @@
     return wide_sum([parts[0]] + [swap(parts[j], "shard", j) for j in range(1, len(parts))])
 
 
-def gather_rows(piece):
-    rows = gather_chips(piece, -2)
+def gather_rows(piece, begin, end):
+    piece = after(piece, begin)
+    marks = [swap(piece, "ctx", 2 * k) for k in range(1, chip_count())]
+    rows = jnp.concatenate(after([piece] + marks, end), axis=-2)
     split = rows.reshape(rows.shape[:-2] + (chip_count(), 1, piece.shape[-2], rows.shape[-1]))
+    whole = gather_cores(split, -3).reshape(
+        rows.shape[:-2] + (2 * rows.shape[-2], rows.shape[-1])
+    )
+    return (whole, marks)
+
+
+def core_rows(rows):
+    split = rows.reshape(rows.shape[:-2] + (chip_count(), 1, -1, rows.shape[-1]))
     return gather_cores(split, -3).reshape(
         rows.shape[:-2] + (2 * rows.shape[-2], rows.shape[-1])
     )
 
 
-def scatter_rows(terms):
+def scatter_rows(terms, begin):
     chips = chip_count()
     rows = terms.shape[-2] // (2 * chips)
     split = terms.reshape(terms.shape[:-2] + (chips, 2, rows, terms.shape[-1]))
     summed = scatter_cores(split, split.ndim - 3).astype(jnp.bfloat16)
-    return scatter_chips(summed.reshape(terms.shape[:-2] + (chips * rows, terms.shape[-1])), -2)
-
-
-def scatter_weight(terms):
-    return scatter_shard(scatter_rows(terms).astype(jnp.bfloat16), -1)
-
-
-def reduce_small(values):
-    for axis in ("ctx", "shard"):
-        distance = 1
-        while distance < lax.axis_size(axis):
-            values = values + swap(values, axis, distance)
-            distance *= 2
-    return values
+    summed = summed.reshape(terms.shape[:-2] + (chips * rows, terms.shape[-1]))
+    return scatter_chips(after(summed, begin), -2)
+
+
+def split_wide(values):
+    high = lax.reduce_precision(values, 8, 7)
+    low = lax.reduce_precision(values - high, 8, 7)
+    return (high + low, jnp.concatenate([high, low], axis=0).astype(jnp.bfloat16))
+
+
+def join_wide(packed, shape):
+    high, low = jnp.split(packed.reshape((2,) + shape).astype(jnp.float32), 2, axis=0)
+    return (high + low)[0]
+
+
+def scatter_last(terms, small, attn_terms):
+    chips = chip_count()
+    shards_n = lax.axis_size("shard")
+    rows = terms.shape[0] // (2 * chips)
+    shape = small.shape
+    split = terms.reshape(chips, 2, rows, terms.shape[1])
+    summed = scatter_cores(split, 1).astype(jnp.bfloat16)
+    small = small + swap(small, "ctx", 1)
+    own, packed = split_wide(small)
+    packed = packed.reshape(-1, terms.shape[1])
+    got = [
+        swap(jnp.concatenate([summed[k], packed], axis=0), "ctx", 2 * k)
+        for k in range(1, chips)
+    ]
+    small = tree_sum([own] + [join_wide(piece[rows:], shape) for piece in got])
+    summed = wide_sum([summed[0]] + [piece[:rows] for piece in got]).astype(jnp.bfloat16)
+    own, packed = split_wide(small)
+    attn_parts = jnp.split(attn_terms.astype(jnp.bfloat16), shards_n, axis=-1)
+    parts = jnp.split(summed, shards_n, axis=1)
+    width = attn_parts[0].shape[-1]
+
+    def flat(value):
+        return value.reshape(-1, width)
+
+    def message(j):
+        return jnp.concatenate([flat(packed), flat(attn_parts[j]), flat(parts[j])], axis=0)
+
+    mine = message(0)
+    got = [swap(message(j), "shard", j) for j in range(1, shards_n)]
+    small_rows = packed.size // width
+    attn_rows = small_rows + attn_parts[0].size // width
+    term_rows = attn_rows + parts[0].size // width
+    small = tree_sum([own] + [join_wide(piece[:small_rows], shape) for piece in got])
+    total = wide_sum([mine[small_rows:term_rows]] + [piece[small_rows:term_rows] for piece in got])
+    return (
+        total[: attn_rows - small_rows].reshape(attn_parts[0].shape),
+        total[attn_rows - small_rows :].reshape(parts[0].shape),
+        small,
+    )
 
 
 def relative_ctx(index):
@@ -190,14 +247,27 @@
     half_blocks = table_ref.shape[0] - 2
     high = (block_index >= half_blocks).astype(jnp.int32)
     at = table_ref[jnp.where(high == 1, 2 * half_blocks - 1 - block_index, block_index)]
-    piece = kv_ref[pl.ds(at * shard_size, shard_size), high, :, part * HEAD : (part + 1) * HEAD]
+    piece = kv_ref[at, :, high, :, part * HEAD : (part + 1) * HEAD]
     return piece.reshape(piece.shape[0] * piece.shape[1], HEAD)
 
 
-def forward_kernel(table_ref, query_ref, kv_ref, out_ref, log_ref, q_s, acc_s, sum_s):
+def start_keys(piece_refs, kv_ref, sem_ref):
+    copies = [
+        pltpu.make_async_copy(piece_ref, kv_ref.at[i], sem_ref.at[i])
+        for i, piece_ref in enumerate(piece_refs)
+    ]
+    for copy in copies:
+        copy.start()
+    return copies
+
+
+def forward_kernel(table_ref, query_ref, *refs):
     half_blocks = table_ref.shape[0] - 2
-    shard_size = kv_ref.shape[0] // half_blocks
-    half_len = kv_ref.shape[2]
+    piece_refs = refs[:half_blocks]
+    out_ref, log_ref, q_s, acc_s, sum_s, kv_ref, sem_ref = refs[half_blocks:]
+    copies = start_keys(piece_refs, kv_ref, sem_ref)
+    shard_size = kv_ref.shape[1]
+    half_len = kv_ref.shape[3]
     block_len = shard_size * half_len
     side_rows = half_len * HEADS
     own_block = table_ref[half_blocks]
@@ -211,6 +281,8 @@
     row_i = lax.broadcasted_iota(jnp.int32, (side_rows, 1), 0)
     query_in = own_shard * half_len + row_i % half_len
     offset_in = key_in - query_in
+    for copy in copies:
+        copy.wait()
 
     def attend(unit):
         far = (unit > own_block).astype(jnp.int32)
@@ -254,23 +326,15 @@
 
 
 def backward_kernel(
-    table_ref,
-    query_ref,
-    kv_ref,
-    out_ref,
-    grad_ref,
-    log_ref,
-    dq_ref,
-    dkv_ref,
-    q_s,
-    do_s,
-    acc_s,
-    log_s,
-    delta_s,
+    table_ref, query_ref, out_ref, grad_ref, log_ref, *refs
 ):
     half_blocks = table_ref.shape[0] - 2
-    shard_size = kv_ref.shape[0] // half_blocks
-    half_len = kv_ref.shape[2]
+    piece_refs = refs[:half_blocks]
+    dq_ref, keep_ref, send_ref = refs[half_blocks : half_blocks + 3]
+    q_s, do_s, acc_s, log_s, delta_s, kv_ref, dkv_ref, sem_ref = refs[half_blocks + 3 :]
+    copies = start_keys(piece_refs, kv_ref, sem_ref)
+    shard_size = kv_ref.shape[1]
+    half_len = kv_ref.shape[3]
     block_len = shard_size * half_len
     side_rows = half_len * HEADS
     own_block = table_ref[half_blocks]
@@ -294,6 +358,8 @@
     row_i = lax.broadcasted_iota(jnp.int32, (1, side_rows), 1)
     query_in = own_shard * half_len + row_i % half_len
     offset_in = key_in - query_in
+    for copy in copies:
+        copy.wait()
 
     def attend(unit):
         far = (unit > own_block).astype(jnp.int32)
@@ -315,21 +381,21 @@
         dk = nn(grad_scores, queries) * score_scale
         dv = nn(weights.astype(jnp.bfloat16), grad_rows)
         seen = jnp.logical_and(far == 1, block_index <= own_block)
-        return (rows, pl.ds(at * shard_size, shard_size), high, seen, dq, dk, dv)
+        return (rows, (at % 2, at // 2), high, seen, dq, dk, dv)
 
     def attend_some(first, count):
-        for rows, devices, high, seen, dq, dk, dv in [attend(first + i) for i in range(count)]:
+        for rows, (core, chip), high, seen, dq, dk, dv in [attend(first + i) for i in range(count)]:
             acc_s[rows, :] += dq
             for part, value in enumerate((dk, dv)):
                 columns = slice(part * HEAD, (part + 1) * HEAD)
-                old = dkv_ref[devices, high, :, columns].astype(jnp.float32)
-                dkv_ref[devices, high, :, columns] = (
+                old = dkv_ref[core, chip, :, high, :, columns].astype(jnp.float32)
+                dkv_ref[core, chip, :, high, :, columns] = (
                     value.reshape(shape) + jnp.where(seen, old, 0.0)
                 ).astype(jnp.bfloat16)
 
     def none(block_index, carry):
         at = table_ref[2 * half_blocks - 1 - block_index]
-        dkv_ref[pl.ds(at * shard_size, shard_size), 1] = jnp.zeros(
+        dkv_ref[at % 2, at // 2, :, 1] = jnp.zeros(
             (shard_size, half_len, 2 * HEAD), jnp.bfloat16
         )
         return carry
@@ -344,6 +410,12 @@
     lax.fori_loop(0, unit_count // group, attend_group, 0)
     attend_some(unit_count - unit_count % group, unit_count % group)
     lax.fori_loop(far_block + 1, 2 * half_blocks, none, 0)
+    copies = [
+        pltpu.make_async_copy(dkv_ref.at[i], target_ref, sem_ref.at[i])
+        for i, target_ref in enumerate((keep_ref, send_ref))
+    ]
+    for copy in copies:
+        copy.start()
     result = acc_s[...] * score_scale
     for side in range(2):
         for h in range(HEADS):
@@ -351,60 +423,65 @@
             dq_ref[side * half_len : (side + 1) * half_len, h * HEAD : (h + 1) * HEAD] = result[
                 at : at + half_len, :
             ]
+    for copy in copies:
+        copy.wait()
 
 
 def whole_spec(space=pltpu.VMEM):
     return pl.BlockSpec(memory_space=space)
 
 
-def attention_forward(table, queries, kv):
+def attention_forward(table, queries, pieces):
     rows = queries.shape[0] * HEADS
-    room = kv.size * 2 + (24 << 20)
+    kv_size = len(pieces) * pieces[0].size
     return pl.pallas_call(
         forward_kernel,
         out_shape=(
             jax.ShapeDtypeStruct(queries.shape, jnp.float32),
             jax.ShapeDtypeStruct((rows, 1), jnp.float32),
         ),
-        in_specs=[whole_spec(pltpu.SMEM), whole_spec(), whole_spec()],
+        in_specs=[whole_spec(pltpu.SMEM), whole_spec()] + [whole_spec(pl.ANY)] * len(pieces),
         out_specs=(whole_spec(), whole_spec()),
         scratch_shapes=[
             pltpu.VMEM((rows, HEAD), jnp.bfloat16),
             pltpu.VMEM((rows, HEAD), jnp.float32),
             pltpu.VMEM((rows, 1), jnp.float32),
+            pltpu.VMEM((len(pieces),) + pieces[0].shape, jnp.bfloat16),
+            pltpu.SemaphoreType.DMA((len(pieces),)),
         ],
-        compiler_params=pltpu.CompilerParams(vmem_limit_bytes=room),
-        cost_estimate=pl.CostEstimate(
-            flops=12 * rows * kv.size, transcendentals=0, bytes_accessed=8 * kv.size
-        ),
+        compiler_params=pltpu.CompilerParams(vmem_limit_bytes=2 * kv_size + (24 << 20)),
         name="attention_forward",
-    )(table, queries, kv)
-
-
-def attention_backward(table, queries, kv, outs, grads, logs):
+    )(table, queries, *pieces)
+
+
+def attention_backward(table, queries, pieces, outs, grads, logs):
     rows = queries.shape[0] * HEADS
-    room = kv.size * 4 + (24 << 20)
+    kv_size = len(pieces) * pieces[0].size
+    half = (len(pieces) // 2,) + pieces[0].shape
     return pl.pallas_call(
         backward_kernel,
         out_shape=(
             jax.ShapeDtypeStruct(queries.shape, jnp.float32),
-            jax.ShapeDtypeStruct(kv.shape, jnp.bfloat16),
+            jax.ShapeDtypeStruct(half, jnp.bfloat16),
+            jax.ShapeDtypeStruct(half, jnp.bfloat16),
         ),
-        in_specs=[whole_spec(pltpu.SMEM)] + [whole_spec()] * 5,
-        out_specs=(whole_spec(), whole_spec()),
+        in_specs=[whole_spec(pltpu.SMEM)]
+        + [whole_spec()] * 4
+        + [whole_spec(pl.ANY)] * len(pieces),
+        out_specs=(whole_spec(), whole_spec(pl.ANY), whole_spec(pl.ANY)),
         scratch_shapes=[
             pltpu.VMEM((rows, HEAD), jnp.bfloat16),
             pltpu.VMEM((rows, HEAD), jnp.bfloat16),
             pltpu.VMEM((rows, HEAD), jnp.float32),
             pltpu.VMEM((2, 1, rows // 2), jnp.float32),
             pltpu.VMEM((2, 1, rows // 2), jnp.float32),
+            pltpu.VMEM((len(pieces),) + pieces[0].shape, jnp.bfloat16),
+            pltpu.VMEM((2,) + half, jnp.bfloat16),
+            pltpu.SemaphoreType.DMA((len(pieces),)),
         ],
-        compiler_params=pltpu.CompilerParams(vmem_limit_bytes=room),
-        cost_estimate=pl.CostEstimate(
-            flops=12 * rows * kv.size, transcendentals=0, bytes_accessed=12 * kv.size
-        ),
+        compiler_params=pltpu.CompilerParams(vmem_limit_bytes=4 * kv_size + (24 << 20)),
         name="attention_backward",
-    )(table, queries, kv, outs, grads, logs)
+    )(table, queries, outs, grads, logs, *pieces)
 
 
 def shards(
@@ -445,8 +522,8 @@
     piece_len = width // ctx_size
     slice_len = HEAD // shard_size
 
-    group_tokens = gather_shard(tokens, 0)
-    attn_pieces = gather_shard(
+    group_tokens, token_marks = gather_shard(tokens, 0)
+    attn_pieces, _ = gather_shard(
         jnp.concatenate(
             [
                 keyval_weight[0].astype(bfloat),
@@ -458,27 +535,26 @@
         )[None],
         0,
     )
-    ffn_full = gather_rows(
+    ffn_piece = after(
         jnp.stack(
             [
                 gateup_weight[0].astype(bfloat),
                 gateup_weight[1].astype(bfloat),
                 down_weight.astype(bfloat).T,
             ]
-        )
-    )
-    gate_full, up_full, down_full = (ffn_full[0], ffn_full[1], ffn_full[2])
+        ),
+        token_marks,
+    )
+    ffn_z = jnp.concatenate(
+        [ffn_piece] + [swap(ffn_piece, "shard", j) for j in range(2, shard_size, 2)], axis=-1
+    )
 
     def side_by_side(start, size):
         return jnp.concatenate(
             [attn_pieces[j, :, start : start + size] for j in range(shard_size)], axis=-1
         )
 
-    keyval_full = gather_rows(side_by_side(0, 2 * slice_len))
-    attn_full = gather_rows(
-        jnp.stack([side_by_side(2 * slice_len, HEAD), side_by_side(2 * slice_len + HEAD, HEAD)])
-    )
-    query_full, output_full = (attn_full[0], attn_full[1])
+    keyval_full, keyval_marks = gather_rows(side_by_side(0, 2 * slice_len), [], [])
 
     feature = jnp.arange(width, dtype=jnp.int32)
     feature_map = one_hot(relative_ctx(feature // piece_len) * piece_len + feature % piece_len)
@@ -538,9 +614,15 @@
     kv_own = jnp.concatenate([keys_own, values_own], axis=-1).reshape(
         shard_size, 2, half_len, 2 * HEAD
     )
-    kv_chips = gather_chips(kv_own, 0).reshape(-1, 1, shard_size, 2, half_len, 2 * HEAD)
-    kv_all = gather_cores(kv_chips, 1).reshape(-1, 2, half_len, 2 * HEAD)
-
+    attn_own = after(
+        jnp.stack([side_by_side(2 * slice_len, HEAD), side_by_side(2 * slice_len + HEAD, HEAD)]),
+        keyval_marks,
+    )
+    attn_got = [attn_own] + [swap(attn_own, "ctx", 2 * k) for k in range(1, chip_count())]
+    kv_marks = [swap(kv_own, "ctx", 2 * k) for k in range(1, chip_count())]
+    attn_got = after(attn_got, (kv_marks, ffn_z))
+    attn_full = core_rows(jnp.concatenate(attn_got, axis=-2))
+    query_full, output_full = (attn_full[0], attn_full[1])
     query_proj = nn(attn_in, query_full)
     query_normed, query_inverse = rms_forward(query_proj.reshape(row_count, HEADS, HEAD))
     query_scaled = query_normed * (1.0 + head_scales[0])
@@ -549,40 +631,51 @@
         .astype(bfloat)
         .reshape(row_count, HEADS * HEAD)
     )
-    attn_rows, attn_logs = attention_forward(table, query_rows, kv_all)
+    kv_pieces = [
+        piece
+        for own in [kv_own] + kv_marks
+        for piece in (own, swap(own, "ctx", 1))
+    ]
+
+    attn_rows, attn_logs = attention_forward(table, query_rows, kv_pieces)
+    ffn_full, _ = gather_rows(ffn_z, kv_marks, attn_rows)
+    gate_full, up_full, down_full = (ffn_full[0], ffn_full[1], ffn_full[2])
     attn_b = attn_rows.astype(bfloat)
     attn_out = nt(attn_b, output_full)
     out_normed, out_inverse = rms_forward(attn_out)
     hidden_in = inputs + out_normed * (1.0 + scales[1])
     mid_normed, mid_inverse = rms_forward(hidden_in)
     ffn_in = (mid_normed * (1.0 + scales[2])).astype(bfloat)
-    group_ffn = gather_shard(ffn_in, 0)
+    group_ffn = gather_pair(ffn_in, 0)
     gate_pre = nn(group_ffn, gate_full)
     up_pre = nn(group_ffn, up_full)
     gate_value, gate_slope = gelu_parts(gate_pre)
     hidden_b = (gate_value * up_pre).astype(bfloat)
-    ffn_out = scatter_shard(nt(hidden_b, down_full).astype(bfloat), 0)
+    ffn_out = scatter_pair(nt(hidden_b, down_full))
     ffn_normed, ffn_inverse = rms_forward(ffn_out)
     block_out = nt(
         (hidden_in + ffn_normed * (1.0 + scales[3])).astype(bfloat), feature_map
     ).astype(bfloat)
     grad_norm3 = jnp.sum(upstream * ffn_normed, axis=0)
     ffn_grad = rms_backward(ffn_normed, ffn_inverse, upstream * (1.0 + scales[3])).astype(bfloat)
-    group_grad = gather_shard(ffn_grad, 0)
+    group_grad = gather_pair(ffn_grad, 0)
     hidden_grad = nn(group_grad, down_full)
     gate_grad = (hidden_grad * up_pre * gate_slope).astype(bfloat)
     up_grad = (hidden_grad * gate_value).astype(bfloat)
-    ffn_in_grad = scatter_shard(
-        (nt(gate_grad, gate_full) + nt(up_grad, up_full)).astype(bfloat), 0
-    )
-    ffn_owned = scatter_rows(
+    ffn_in_grad = scatter_pair(nt(gate_grad, gate_full) + nt(up_grad, up_full))
+    ffn_rows, ffn_marks = scatter_rows(
         jnp.stack(
             [
                 tn(group_ffn, gate_grad).astype(bfloat),
                 tn(group_ffn, up_grad).astype(bfloat),
                 tn(group_grad, hidden_b).astype(bfloat),
             ]
-        )
+        ),
+        [],
+    )
+    ffn_parts = jnp.split(ffn_rows.astype(bfloat), shard_size // 2, axis=-1)
+    ffn_owned = wide_sum(
+        [ffn_parts[0]] + [swap(ffn_parts[j], "shard", 2 * j) for j in range(1, len(ffn_parts))]
     )
     grad_norm2 = jnp.sum(ffn_in_grad * mid_normed, axis=0)
     residual_grad = upstream + rms_backward(mid_normed, mid_inverse, ffn_in_grad * (1.0 + scales[2]))
@@ -590,15 +683,15 @@
     attn_out_grad = rms_backward(
         out_normed, out_inverse, residual_grad * (1.0 + scales[1])
     ).astype(bfloat)
-    output_wgrad = tn(attn_out_grad, attn_b).astype(bfloat)
     attn_grad_b = nn(attn_out_grad, output_full).astype(bfloat)
-    query_parts, kv_terms = attention_backward(
-        table, query_rows, kv_all, attn_rows, attn_grad_b, attn_logs
-    )
-    kv_terms = kv_terms.reshape(-1, 2, shard_size, 2, half_len, 2 * HEAD)
-    kv_terms = scatter_cores(kv_terms, 1).astype(bfloat)
-    kv_terms = scatter_chips(kv_terms, 0).astype(bfloat)[0]
-    kv_grad = scatter_shard(kv_terms, 0).reshape(row_count, 2 * HEAD)
+    query_parts, kv_keep, kv_send = attention_backward(
+        table, query_rows, kv_pieces, attn_rows, attn_grad_b, attn_logs
+    )
+    kv_keep, kv_send = after((kv_keep, kv_send), ffn_marks)
+    kv_terms = wide_sum([kv_keep, swap(kv_send, "ctx", 1)]).astype(bfloat)
+    kv_core = kv_terms
+    kv_terms, kv_marks = scatter_chips(kv_terms, 0)
+    kv_grad = scatter_shard(kv_terms.astype(bfloat)[0], 0).reshape(row_count, 2 * HEAD)
     query_rot_grad = query_parts.reshape(row_count, HEADS, HEAD)
     query_rope_grad = query_rot_grad * cosine[:, None, :] + rotate_back(
         query_rot_grad * sine[:, None, :]
@@ -609,8 +702,11 @@
         .reshape(row_count, HEADS * HEAD)
         .astype(bfloat)
     )
-    query_wgrad = tn(attn_in, query_proj_grad).astype(bfloat)
-    attn_owned = scatter_weight(jnp.stack([query_wgrad, output_wgrad]))
+    late_grad, late_out_grad = after((query_proj_grad, attn_out_grad), kv_core)
+    query_wgrad = tn(attn_in, late_grad).astype(bfloat)
+    output_wgrad = tn(late_out_grad, attn_b).astype(bfloat)
+    attn_terms, attn_marks = scatter_rows(jnp.stack([query_wgrad, output_wgrad]), kv_marks)
+    kv_grad = after(kv_grad, attn_marks)
     key_rot_grad = kv_grad[:, :HEAD]
     value_grad = kv_grad[:, HEAD:]
     key_rope_grad = key_rot_grad * cosine + rotate_back(key_rot_grad * sine)
@@ -620,7 +716,6 @@
     ).astype(bfloat)
     keyval_proj_grad = jnp.concatenate([key_proj_grad, value_grad.astype(bfloat)], axis=-1)
     keyval_wgrad = nt(tn(attn_in, keyval_proj_grad).astype(bfloat), channel_map).astype(bfloat)
-    keyval_owned = scatter_weight(keyval_wgrad)
     attn_in_grad = nt(query_proj_grad, query_full) + nt(keyval_proj_grad, keyval_sorted)
     grad_norm0 = jnp.sum(attn_in_grad * normed_in, axis=0)
     tokens_grad = nt(
@@ -637,9 +732,12 @@
         precision=lax.Precision.HIGHEST,
         preferred_element_type=single,
     )
-    small = reduce_small(
-        jnp.concatenate([norm_terms.reshape(-1), grad_head0, grad_head1]).reshape(-1, 128)
-    ).reshape(-1)
+    attn_owned, keyval_owned, small = scatter_last(
+        keyval_wgrad,
+        jnp.concatenate([norm_terms.reshape(-1), grad_head0, grad_head1]).reshape(-1, 128),
+        attn_terms,
+    )
+    small = small.reshape(-1)
     norm_wgrad = small[: 4 * width].reshape(4, width)
     head_wgrad = small[4 * width :].reshape(2, HEAD)
 

time: 301 us -> 266 us (0.88)
  waiting for transfers between devices: 148 us -> 120 us
  starting transfers between devices: 66.3 us -> 57.1 us
  Pallas kernels: 12.6 us -> 16.3 us
    ppermute x64 -> x54, waiting for transfers between devices: 148 us -> 120 us  [swap(): lax.ppermute(piece, axis, [(i, i ^ distance) for i in range(lax.axis_size...]
    ppermute x64 -> x54, starting transfers between devices: 66.3 us -> 57.1 us  [swap(): lax.ppermute(piece, axis, [(i, i ^ distance) for i in range(lax.axis_size...]
    convert_element_type x4 -> x12, other arithmetic: 1.4 us -> 4.9 us  [the longest x1 2.35 us: shards(): kv_terms = wide_sum([kv_keep, swap(kv_send, 'ctx', 1)]).astype(bfloat)]
    concatenate x4 -> x3, other arithmetic: 6.23 us -> 3.9 us  [gather_cores(): return jnp.concatenate([piece, swap(piece, 'ctx', 1)], axis=dim)]
    unnamed x127 -> x146, local copies, waits for them, and re-layouts: 6.68 us -> 5.88 us
  transfers between devices with their start and end apart: 64 -> 54, of which waited for: 42 -> 26; matrix products, arithmetic and copies ran while one was open for 17% -> 14% of each run, Pallas kernels for 4% -> 6%
where the time goes in v1:
time: 266 us; the launch traced here: 265 us
  waiting for transfers between devices  120 us (45%)
  starting transfers between devices  57.1 us (21%)
  other arithmetic  31.7 us (12%)
  matrix products  24.5 us (9%)
  Pallas kernels  16.3 us (6%)
  local copies, waits for them, and re-layouts  13.5 us (5%)
    ppermute x54, waiting for transfers between devices, swap(): lax.ppermute(piece, axis, [(i, i ^ distance) for i in range(lax.axis_size...  120 us
    ppermute x54, starting transfers between devices, swap(): lax.ppermute(piece, axis, [(i, i ^ distance) for i in range(lax.axis_size...  57.1 us
    dot_general x9, matrix products, nt(): lax.dot_general(left, right, (((1,), (1,)), ((), ())), preferred_element_...  12.2 us
    pallas_call x1, Pallas kernels, attention_backward(): pl.pallas_call(backward_kernel, out_shape=(jax.ShapeDtypeStruct(queries.s...  11 us
    dot_general x9, matrix products, nn(): return jnp.dot(left, right, preferred_element_type=jnp.float32)  7.48 us
    unnamed x146, local copies, waits for them, and re-layouts  5.88 us
    sub x7, other arithmetic, adam_update(): weight - learn_rate * (first_hat / (jnp.sqrt(second_hat) + adam_eps) + we...  5.46 us
    pallas_call x1, Pallas kernels, attention_forward(): pl.pallas_call(forward_kernel, out_shape=(jax.ShapeDtypeStruct(queries.sh...  5.33 us
  transfers between devices with their start and end apart: 54, of which 26 were waited for; matrix products, arithmetic and copies ran while one was open for 14% of the time, Pallas kernels for 6%

profile of v1, /device:TPU:0, one launch (start us, length us, event | category | flops | bytes accessed | tf_op | source)
XLA Modules:
  0.0 265.3 jit_solution(15943865251027767205)
XLA Ops:
  3.6 5.1 %collective-permute-start.5 = (bf16[1,80,640]{2,1,0:T(8,128)(2,1)S(1)}, bf16[1,80,640]{2,1,0:T(8,128)(2,1)S(1)}, u32[]{:S(2)}, u32[]{:S(2)}) collective-permute-start(bf16[1,80,640]{2,1,0:T(8,128)(2,1)S(1)} %maximum_bitcast_fusion.2), channel_id=1, source_target_pairs={{0,3},{1,2},{2,1},{3,0},{4,7},{5,6},{6,5},{7,4},{8,11},{9,10},{10,... | collective-permute-start | bytes 307208 | tf_op jit(solution)/shard_map/ppermute | solution.py:75
  9.4 2.3 collective-permute-start.1
  11.6 2.0 collective-permute-start
  15.4 1.3 fusion.17
  18.1 3.7 %collective-permute-done.4 = bf16[1,80,640]{2,1,0:T(8,128)(2,1)S(1)} collective-permute-done((bf16[1,80,640]{2,1,0:T(8,128)(2,1)S(1)}, bf16[1,80,640]{2,1,0:T(8,128)(2,1)S(1)}, u32[]{:S(2)}, u32[]{:S(2)}) %collective-permute-start.4) | collective-permute-done | bytes 102432 | tf_op jit(solution)/shard_map/ppermute | solution.py:75
  21.8 2.5 collective-permute-start.8
  25.0 3.9 %collective-permute-done.1 = bf16[128,640]{1,0:T(8,128)(2,1)S(1)} collective-permute-done((bf16[128,640]{1,0:T(8,128)(2,1)}, bf16[128,640]{1,0:T(8,128)(2,1)S(1)}, u32[]{:S(2)}, u32[]{:S(2)}) %collective-permute-start.1) | collective-permute-done | bytes 163872 | tf_op jit(solution)/shard_map/ppermute | solution.py:75
  28.8 1.5 collective-permute-start.6
  30.3 2.6 collective-permute-start.16
  34.0 1.3 multiply_convert_fusion
  35.3 2.4 collective-permute-start.11
  41.2 1.5 collective-permute-start.14
  42.7 1.5 collective-permute-start.13
  44.9 2.0 collective-permute-done.11
  46.9 1.5 collective-permute-start.9
  49.4 26.3 %collective-permute-done.10 = bf16[2,80,1024]{2,1,0:T(8,128)(2,1)S(1)} collective-permute-done((bf16[2,80,1024]{2,1,0:T(8,128)(2,1)S(1)}, bf16[2,80,1024]{2,1,0:T(8,128)(2,1)S(1)}, u32[]{:S(2)}, u32[]{:S(2)}) %collective-permute-start.10) | collective-permute-done | bytes 327712 | tf_op jit(solution)/shard_map/ppermute | solution.py:75
  75.9 2.4 pad_maximum_fusion.5
  80.3 2.4 collective-permute-start.25
  83.2 3.5 %fusion.10 = (bf16[1,4,2,80,1024]{4,3,2,1,0:T(8,128)(2,1)}, bf16[1,4,2,80,1024]{4,3,2,1,0:T(8,128)(2,1)}) fusion(bf16[2,4,1,80,1024]{4,3,2,1,0:T(8,128)(2,1)} %bitcast.29, bf16[2,4,1,80,1024]{4,3,2,1,0:T(8,128)(2,1)} %collective-permute-done.17), kind=kLoop, calls=%fused_computation.36 | loop fusion | flops 1310720 | bytes 5242880 | tf_op jit(solution)/shard_map/concatenate | solution.py:101
  86.6 2.4 copy.103
  89.1 2.1 multiply_reduce_fusion.3
  94.4 5.3 %attention_forward.1 = (f32[128,1024]{1,0:T(8,128)S(1)}, f32[512,1]{1,0:T(8,128)S(1)}) custom-call(s32[10]{0:T(128)S(1)} %pad_add_fusion.table_ref, bf16[128,1024]{1,0:T(8,128)(2,1)S(1)} %bitcast.192, bf16[4,2,64,512]{3,2,1,0:T(8,128)(2,1)S(1)} %bitcast.190, bf16[4,2,64,512]{3,2,1,0:T(8,128)(2,1)S(1)} %collective-permute-done.18.refs_1_, ...), custom_call_target="tpu_custom_call" | custom-call | tf_op jit(solution)/shard_map/attention_forward/pallas_call | solution.py:437
  99.7 5.4 %collective-permute-done.24 = bf16[3,80,1024]{2,1,0:T(8,128)(2,1)S(1)} collective-permute-done((bf16[3,80,1024]{2,1,0:T(8,128)(2,1)S(1)}, bf16[3,80,1024]{2,1,0:T(8,128)(2,1)S(1)}, u32[]{:S(2)}, u32[]{:S(2)}) %collective-permute-start.24) | collective-permute-done | bytes 491552 | tf_op jit(solution)/shard_map/ppermute | solution.py:75
  105.4 1.3 pad_maximum_fusion.1
  107.5 1.2 multiply_reduce_fusion.14
  109.2 1.5 collective-permute-done.26
  111.1 4.3 %collective-permute-done.22 = bf16[128,640]{1,0:T(8,128)(2,1)S(1)} collective-permute-done((bf16[128,640]{1,0:T(8,128)(2,1)S(1)}, bf16[128,640]{1,0:T(8,128)(2,1)S(1)}, u32[]{:S(2)}, u32[]{:S(2)}) %collective-permute-start.22) | collective-permute-done | bytes 163872 | tf_op jit(solution)/shard_map/ppermute | solution.py:75
  117.8 5.4 %collective-permute-done.27 = bf16[128,640]{1,0:T(8,128)(2,1)S(1)} collective-permute-done((bf16[128,640]{1,0:T(8,128)(2,1)S(1)}, bf16[128,640]{1,0:T(8,128)(2,1)S(1)}, u32[]{:S(2)}, u32[]{:S(2)}) %collective-permute-start.27) | collective-permute-done | bytes 163872 | tf_op jit(solution)/shard_map/ppermute | solution.py:75
  124.5 5.0 %collective-permute-done.28 = bf16[128,640]{1,0:T(8,128)(2,1)S(1)} collective-permute-done((bf16[128,640]{1,0:T(8,128)(2,1)S(1)}, bf16[128,640]{1,0:T(8,128)(2,1)S(1)}, u32[]{:S(2)}, u32[]{:S(2)}) %collective-permute-start.28) | collective-permute-done | bytes 163872 | tf_op jit(solution)/shard_map/ppermute | solution.py:75
  130.0 1.1 fusion.24
  134.6 6.2 %collective-permute-done.29 = bf16[128,640]{1,0:T(8,128)(2,1)S(1)} collective-permute-done((bf16[128,640]{1,0:T(8,128)(2,1)S(1)}, bf16[128,640]{1,0:T(8,128)(2,1)S(1)}, u32[]{:S(2)}, u32[]{:S(2)}) %collective-permute-start.29) | collective-permute-done | bytes 163872 | tf_op jit(solution)/shard_map/ppermute | solution.py:75
  142.6 1.1 copy-done.15
  143.7 2.2 collective-permute-start.33
  147.8 11.0 %attention_backward.1 = (f32[128,1024]{1,0:T(8,128)S(1)}, bf16[4,4,2,64,512]{4,3,2,1,0:T(8,128)(2,1)S(1)}, bf16[4,4,2,64,512]{4,3,2,1,0:T(8,128)(2,1)}) custom-call(s32[10]{0:T(128)S(1)} %pad_add_fusion.table_ref, bf16[128,1024]{1,0:T(8,128)(2,1)S(1)} %bitcast.193, f32[128,1024]{1,0:T(8,128)S(1)} %get-tuple-element.66.out_ref, ...), custom_call_target="tpu_custom_call" | custom-call | tf_op jit(solution)/shard_map/attention_backward/pallas_call | solution.py:461
  158.8 9.2 %collective-permute-done.32 = bf16[3,80,1024]{2,1,0:T(8,128)(2,1)S(1)} collective-permute-done((bf16[3,80,1024]{2,1,0:T(8,128)(2,1)S(1)}, bf16[3,80,1024]{2,1,0:T(8,128)(2,1)S(1)}, u32[]{:S(2)}, u32[]{:S(2)}) %collective-permute-start.32) | collective-permute-done | bytes 491552 | tf_op jit(solution)/shard_map/ppermute | solution.py:75
  168.1 1.2 fusion.15
  170.1 1.9 add_convert_fusion.2
  172.1 1.1 collective-permute-start.53
  173.2 2.3 add_convert_fusion
  177.7 1.3 collective-permute-start.35
  179.0 1.6 collective-permute-start.37
  181.2 5.2 %collective-permute-done.53 = bf16[3,80,512]{2,1,0:T(8,128)(2,1)S(1)} collective-permute-done((bf16[3,80,512]{2,1,0:T(8,128)(2,1)S(1)}, bf16[3,80,512]{2,1,0:T(8,128)(2,1)S(1)}, u32[]{:S(2)}, u32[]{:S(2)}) %collective-permute-start.53) | collective-permute-done | bytes 245792 | tf_op jit(solution)/shard_map/ppermute | solution.py:75
  186.5 1.1 multiply_subtract_fusion
  187.7 4.8 %collective-permute-done.35 = bf16[1,4,2,64,512]{4,3,2,1,0:T(8,128)(2,1)S(1)} collective-permute-done((bf16[1,4,2,64,512]{4,3,2,1,0:T(8,128)(2,1)S(1)}, bf16[1,4,2,64,512]{4,3,2,1,0:T(8,128)(2,1)S(1)}, u32[]{:S(2)}, u32[]{:S(2)}) %collective-permute-start.35) | collective-permute-done | bytes 524320 | tf_op jit(solution)/shard_map/ppermute | solution.py:75
  192.5 11.6 %collective-permute-done.37 = bf16[1,4,2,64,512]{4,3,2,1,0:T(8,128)(2,1)S(1)} collective-permute-done((bf16[1,4,2,64,512]{4,3,2,1,0:T(8,128)(2,1)S(1)}, bf16[1,4,2,64,512]{4,3,2,1,0:T(8,128)(2,1)S(1)}, u32[]{:S(2)}, u32[]{:S(2)}) %collective-permute-start.37) | collective-permute-done | bytes 524320 | tf_op jit(solution)/shard_map/ppermute | solution.py:75
  204.1 1.4 collective-permute-done.36
  205.8 1.6 collective-permute-start.38
  207.4 1.8 collective-permute-start.40
  210.0 1.4 collective-permute-start.44
  212.4 1.1 collective-permute-start.42
  214.5 1.7 collective-permute-done.40
  216.1 4.2 %collective-permute-done.39 = bf16[1,2,64,512]{3,2,1,0:T(8,128)(2,1)S(1)} collective-permute-done((bf16[1,2,64,512]{3,2,1,0:T(8,128)(2,1)S(1)}, bf16[1,2,64,512]{3,2,1,0:T(8,128)(2,1)S(1)}, u32[]{:S(2)}, u32[]{:S(2)}) %collective-permute-start.39) | collective-permute-done | bytes 131104 | tf_op jit(solution)/shard_map/ppermute | solution.py:75
  221.6 4.2 %collective-permute-done.43 = bf16[2,80,1024]{2,1,0:T(8,128)(2,1)S(1)} collective-permute-done((bf16[2,80,1024]{2,1,0:T(8,128)(2,1)S(1)}, bf16[2,80,1024]{2,1,0:T(8,128)(2,1)S(1)}, u32[]{:S(2)}, u32[]{:S(2)}) %collective-permute-start.43) | collective-permute-done | bytes 327712 | tf_op jit(solution)/shard_map/ppermute | solution.py:75
  227.3 1.1 copy.112
  228.7 2.3 fusion.74
  231.0 1.5 convolution_convert_fusion.6
  232.6 2.5 multiply_reduce_fusion.8
  240.3 1.6 collective-permute-start.49
  241.9 1.9 collective-permute-done.47
  243.8 2.4 collective-permute-done.48
  246.5 2.4 collective-permute-start.50
  249.0 2.2 fusion.16
  251.6 2.0 collective-permute-start.52
  253.7 7.3 %collective-permute-done.51 = bf16[224,256]{1,0:T(8,128)(2,1)S(1)} collective-permute-done((bf16[224,256]{1,0:T(8,128)(2,1)S(1)}, bf16[224,256]{1,0:T(8,128)(2,1)S(1)}, u32[]{:S(2)}, u32[]{:S(2)}) %collective-permute-start.51) | collective-permute-done | bytes 114720 | tf_op jit(solution)/shard_map/ppermute | solution.py:75
  (381 shorter events, 51.4 us)
Async XLA Ops:
  0.7 122.6 %copy-start = (bf16[128,640]{1,0:T(8,128)(2,1)S(1)}, bf16[128,640]{1,0:T(8,128)(2,1)}, u32[]{:S(2)}) copy-start(bf16[128,640]{1,0:T(8,128)(2,1)} %param.26) | copy-start | bytes 491524
  0.7 16.1 %copy-start.33 = (f32[512,80]{0,1:T(8,128)S(1)}, f32[512,80]{0,1:T(8,128)}, u32[]{:S(2)}) copy-start(f32[512,80]{0,1:T(8,128)} %param.39) | copy-start | bytes 491524
  0.7 16.1 %copy-start.21 = (f32[2,80,512]{2,1,0:T(8,128)S(1)}, f32[2,80,512]{2,1,0:T(8,128)}, u32[]{:S(2)}) copy-start(f32[2,80,512]{2,1,0:T(8,128)} %param.36) | copy-start | bytes 983044
  3.6 14.3 %collective-permute-start.5 = (bf16[1,80,640]{2,1,0:T(8,128)(2,1)S(1)}, bf16[1,80,640]{2,1,0:T(8,128)(2,1)S(1)}, u32[]{:S(2)}, u32[]{:S(2)}) collective-permute-start(bf16[1,80,640]{2,1,0:T(8,128)(2,1)S(1)} %maximum_bitcast_fusion.2), channel_id=1, source_target_pairs={{0,3},{1,2},{2,1},{3,0},{4,7},{5,6},{6,5},{7,4},{8,11},{9,10},{10,... | collective-permute-start | bytes 307208 | tf_op jit(solution)/shard_map/ppermute | solution.py:75
  8.7 13.1 %collective-permute-start.4 = (bf16[1,80,640]{2,1,0:T(8,128)(2,1)S(1)}, bf16[1,80,640]{2,1,0:T(8,128)(2,1)S(1)}, u32[]{:S(2)}, u32[]{:S(2)}) collective-permute-start(bf16[1,80,640]{2,1,0:T(8,128)(2,1)S(1)} %maximum_bitcast_fusion.2), channel_id=1, source_target_pairs={{0,2},{1,3},{2,0},{3,1},{4,6},{5,7},{6,4},{7,5},{8,10},{9,11},{10,... | collective-permute-start | bytes 307208 | tf_op jit(solution)/shard_map/ppermute | solution.py:75
  8.7 13.1 %collective-permute-start.3 = (bf16[1,80,640]{2,1,0:T(8,128)(2,1)S(1)}, bf16[1,80,640]{2,1,0:T(8,128)(2,1)S(1)}, u32[]{:S(2)}, u32[]{:S(2)}) collective-permute-start(bf16[1,80,640]{2,1,0:T(8,128)(2,1)S(1)} %maximum_bitcast_fusion.2), channel_id=1, source_target_pairs={{0,1},{1,0},{2,3},{3,2},{4,5},{5,4},{6,7},{7,6},{8,9},{9,8},{10,11... | collective-permute-start | bytes 307208 | tf_op jit(solution)/shard_map/ppermute | solution.py:75
  9.4 19.5 %collective-permute-start.1 = (bf16[128,640]{1,0:T(8,128)(2,1)}, bf16[128,640]{1,0:T(8,128)(2,1)S(1)}, u32[]{:S(2)}, u32[]{:S(2)}) collective-permute-start(bf16[128,640]{1,0:T(8,128)(2,1)} %param.24), channel_id=1, source_target_pairs={{0,2},{1,3},{2,0},{3,1},{4,6},{5,7},{6,4},{7,5},{8,10},{9,11},{10,... | collective-permute-start | bytes 491528 | tf_op jit(solution)/shard_map/ppermute | solution.py:75
  11.6 18.7 %collective-permute-start = (bf16[128,640]{1,0:T(8,128)(2,1)}, bf16[128,640]{1,0:T(8,128)(2,1)S(1)}, u32[]{:S(2)}, u32[]{:S(2)}) collective-permute-start(bf16[128,640]{1,0:T(8,128)(2,1)} %param.24), channel_id=1, source_target_pairs={{0,1},{1,0},{2,3},{3,2},{4,5},{5,4},{6,7},{7,6},{8,9},{9,8},{10,11... | collective-permute-start | bytes 491528 | tf_op jit(solution)/shard_map/ppermute | solution.py:75
  17.9 12.4 %collective-permute-start.2 = (bf16[128,640]{1,0:T(8,128)(2,1)S(1)}, bf16[128,640]{1,0:T(8,128)(2,1)S(1)}, u32[]{:S(2)}, u32[]{:S(2)}) collective-permute-start(bf16[128,640]{1,0:T(8,128)(2,1)S(1)} %copy-done.70), channel_id=1, source_target_pairs={{0,3},{1,2},{2,1},{3,0},{4,7},{5,6},{6,5},{7,4},{8,11},{9,10},{10,... | collective-permute-start | bytes 491528 | tf_op jit(solution)/shard_map/ppermute | solution.py:75
  21.8 12.0 %collective-permute-start.8 = (bf16[80,512]{1,0:T(8,128)(2,1)S(1)}, bf16[80,512]{1,0:T(8,128)(2,1)S(1)}, u32[]{:S(2)}, u32[]{:S(2)}) collective-permute-start(bf16[80,512]{1,0:T(8,128)(2,1)S(1)} %pad_maximum_fusion.27), channel_id=1, source_target_pairs={{0,24},{4,28},{8,16},{12,20},{16,8},{20,12},{24,0},{28,4},{1,25},{... | collective-permute-start | bytes 245768 | tf_op jit(solution)/shard_map/ppermute | solution.py:75
  24.4 9.5 %collective-permute-start.7 = (bf16[80,512]{1,0:T(8,128)(2,1)S(1)}, bf16[80,512]{1,0:T(8,128)(2,1)S(1)}, u32[]{:S(2)}, u32[]{:S(2)}) collective-permute-start(bf16[80,512]{1,0:T(8,128)(2,1)S(1)} %pad_maximum_fusion.27), channel_id=1, source_target_pairs={{0,16},{4,20},{8,24},{12,28},{16,0},{20,4},{24,8},{28,12},{1,17},{... | collective-permute-start | bytes 245768 | tf_op jit(solution)/shard_map/ppermute | solution.py:75
  28.8 5.0 %collective-permute-start.6 = (bf16[80,512]{1,0:T(8,128)(2,1)S(1)}, bf16[80,512]{1,0:T(8,128)(2,1)S(1)}, u32[]{:S(2)}, u32[]{:S(2)}) collective-permute-start(bf16[80,512]{1,0:T(8,128)(2,1)S(1)} %pad_maximum_fusion.27), channel_id=1, source_target_pairs={{0,8},{4,12},{8,0},{12,4},{16,24},{20,28},{24,16},{28,20},{1,9},{5... | collective-permute-start | bytes 245768 | tf_op jit(solution)/shard_map/ppermute | solution.py:75
  30.3 13.9 %collective-permute-start.16 = (bf16[3,80,512]{2,1,0:T(8,128)(2,1)S(1)}, bf16[3,80,512]{2,1,0:T(8,128)(2,1)}, u32[]{:S(2)}, u32[]{:S(2)}) collective-permute-start(bf16[3,80,512]{2,1,0:T(8,128)(2,1)S(1)} %pad_maximum_fusion.14), channel_id=1, source_target_pairs={{0,2},{1,3},{2,0},{3,1},{4,6},{5,7},{6,4},{7,5},{8,10},{9,11},{10,... | collective-permute-start | bytes 737288 | tf_op jit(solution)/shard_map/ppermute | solution.py:75
  33.9 3.9 %collective-permute-start.12 = (bf16[4,1,80,512]{3,2,1,0:T(8,128)(2,1)S(1)}, bf16[4,1,80,512]{3,2,1,0:T(8,128)(2,1)S(1)}, u32[]{:S(2)}, u32[]{:S(2)}) collective-permute-start(bf16[4,1,80,512]{3,2,1,0:T(8,128)(2,1)S(1)} %bitcast.222), channel_id=1, source_target_pairs={{0,4},{4,0},{8,12},{12,8},{16,20},{20,16},{24,28},{28,24},{1,5},{5... | collective-permute-start | bytes 983048 | tf_op jit(solution)/shard_map/ppermute | solution.py:75
  34.0 134.1 %copy-start.67 = (f32[512]{0:T(512)}, f32[512]{0:T(512)S(1)}, u32[]{:S(2)}) copy-start(f32[512]{0:T(512)S(1)} %add_rsqrt_fusion.2) | copy-start | bytes 6148
  35.3 11.6 %collective-permute-start.11 = (bf16[2,80,1024]{2,1,0:T(8,128)(2,1)S(1)}, bf16[2,80,1024]{2,1,0:T(8,128)(2,1)}, u32[]{:S(2)}, u32[]{:S(2)}) collective-permute-start(bf16[2,80,1024]{2,1,0:T(8,128)(2,1)S(1)} %pad_maximum_fusion.10), channel_id=1, source_target_pairs={{0,24},{4,28},{8,16},{12,20},{16,8},{20,12},{24,0},{28,4},{1,25},{... | collective-permute-start | bytes 983048 | tf_op jit(solution)/shard_map/ppermute | solution.py:75
  39.2 128.8 %copy-start.64 = (f32[512]{0:T(512)}, f32[512]{0:T(512)S(1)}, u32[]{:S(2)}) copy-start(f32[512]{0:T(512)S(1)} %add_rsqrt_fusion.1) | copy-start | bytes 6148
  40.6 35.2 %collective-permute-start.15 = (bf16[4,2,64,512]{3,2,1,0:T(8,128)(2,1)S(1)}, bf16[4,2,64,512]{3,2,1,0:T(8,128)(2,1)S(1)}, u32[]{:S(2)}, u32[]{:S(2)}) collective-permute-start(bf16[4,2,64,512]{3,2,1,0:T(8,128)(2,1)S(1)} %bitcast.186), channel_id=1, source_target_pairs={{0,24},{4,28},{8,16},{12,20},{16,8},{20,12},{24,0},{28,4},{1,25},{... | collective-permute-start | bytes 1572872 | tf_op jit(solution)/shard_map/ppermute | solution.py:75
  41.2 34.7 %collective-permute-start.14 = (bf16[4,2,64,512]{3,2,1,0:T(8,128)(2,1)S(1)}, bf16[4,2,64,512]{3,2,1,0:T(8,128)(2,1)S(1)}, u32[]{:S(2)}, u32[]{:S(2)}) collective-permute-start(bf16[4,2,64,512]{3,2,1,0:T(8,128)(2,1)S(1)} %bitcast.187), channel_id=1, source_target_pairs={{0,16},{4,20},{8,24},{12,28},{16,0},{20,4},{24,8},{28,12},{1,17},{... | collective-permute-start | bytes 1572872 | tf_op jit(solution)/shard_map/ppermute | solution.py:75
  42.7 33.2 %collective-permute-start.13 = (bf16[4,2,64,512]{3,2,1,0:T(8,128)(2,1)S(1)}, bf16[4,2,64,512]{3,2,1,0:T(8,128)(2,1)S(1)}, u32[]{:S(2)}, u32[]{:S(2)}) collective-permute-start(bf16[4,2,64,512]{3,2,1,0:T(8,128)(2,1)S(1)} %bitcast.188), channel_id=1, source_target_pairs={{0,8},{4,12},{8,0},{12,4},{16,24},{20,28},{24,16},{28,20},{1,9},{5... | collective-permute-start | bytes 1572872 | tf_op jit(solution)/shard_map/ppermute | solution.py:75
  44.2 31.6 %collective-permute-start.10 = (bf16[2,80,1024]{2,1,0:T(8,128)(2,1)S(1)}, bf16[2,80,1024]{2,1,0:T(8,128)(2,1)S(1)}, u32[]{:S(2)}, u32[]{:S(2)}) collective-permute-start(bf16[2,80,1024]{2,1,0:T(8,128)(2,1)S(1)} %pad_maximum_fusion.10), channel_id=1, source_target_pairs={{0,16},{4,20},{8,24},{12,28},{16,0},{20,4},{24,8},{28,12},{1,17},{... | collective-permute-start | bytes 983048 | tf_op jit(solution)/shard_map/ppermute | solution.py:75
  46.9 28.9 %collective-permute-start.9 = (bf16[2,80,1024]{2,1,0:T(8,128)(2,1)S(1)}, bf16[2,80,1024]{2,1,0:T(8,128)(2,1)S(1)}, u32[]{:S(2)}, u32[]{:S(2)}) collective-permute-start(bf16[2,80,1024]{2,1,0:T(8,128)(2,1)S(1)} %pad_maximum_fusion.10), channel_id=1, source_target_pairs={{0,8},{4,12},{8,0},{12,4},{16,24},{20,28},{24,16},{28,20},{1,9},{5... | collective-permute-start | bytes 983048 | tf_op jit(solution)/shard_map/ppermute | solution.py:75
  49.4 26.5 %copy-start.31 = (bf16[3,80,1024]{2,1,0:T(8,128)(2,1)}, bf16[3,80,1024]{2,1,0:T(8,128)(2,1)S(1)}, u32[]{:S(2)}) copy-start(bf16[3,80,1024]{2,1,0:T(8,128)(2,1)S(1)} %constant_dynamic-update-slice_fusion) | copy-start | bytes 1474564
  49.4 28.9 %copy-start.60 = (s32[4096]{0:T(1024)S(1)}, s32[4096]{0:T(1024)}, u32[]{:S(2)}) copy-start(s32[4096]{0:T(1024)} %param.25) | copy-start | bytes 49156
  75.9 17.4 %copy-start.2 = (bf16[4,2,64,512]{3,2,1,0:T(8,128)(2,1)}, bf16[4,2,64,512]{3,2,1,0:T(8,128)(2,1)S(1)}, u32[]{:S(2)}) copy-start(bf16[4,2,64,512]{3,2,1,0:T(8,128)(2,1)S(1)} %collective-permute-done.15.refs_6_) | copy-start | bytes 1572868
  75.9 17.4 %copy-start.4 = (bf16[4,2,64,512]{3,2,1,0:T(8,128)(2,1)}, bf16[4,2,64,512]{3,2,1,0:T(8,128)(2,1)S(1)}, u32[]{:S(2)}) copy-start(bf16[4,2,64,512]{3,2,1,0:T(8,128)(2,1)S(1)} %collective-permute-done.14.refs_4_) | copy-start | bytes 1572868
  75.9 17.4 %copy-start.6 = (bf16[4,2,64,512]{3,2,1,0:T(8,128)(2,1)}, bf16[4,2,64,512]{3,2,1,0:T(8,128)(2,1)S(1)}, u32[]{:S(2)}) copy-start(bf16[4,2,64,512]{3,2,1,0:T(8,128)(2,1)S(1)} %collective-permute-done.13.refs_2_) | copy-start | bytes 1572868
  78.3 4.8 %collective-permute-start.17 = (bf16[2,4,1,80,1024]{4,3,2,1,0:T(8,128)(2,1)}, bf16[2,4,1,80,1024]{4,3,2,1,0:T(8,128)(2,1)}, u32[]{:S(2)}, u32[]{:S(2)}) collective-permute-start(bf16[2,4,1,80,1024]{4,3,2,1,0:T(8,128)(2,1)} %bitcast.29), channel_id=1, source_target_pairs={{0,4},{4,0},{8,12},{12,8},{16,20},{20,16},{24,28},{28,24},{1,5},{5... | collective-permute-start | bytes 3932168 | tf_op jit(solution)/shard_map/ppermute | solution.py:75
  79.8 11.5 %collective-permute-start.18 = (bf16[4,2,64,512]{3,2,1,0:T(8,128)(2,1)S(1)}, bf16[4,2,64,512]{3,2,1,0:T(8,128)(2,1)S(1)}, u32[]{:S(2)}, u32[]{:S(2)}) collective-permute-start(bf16[4,2,64,512]{3,2,1,0:T(8,128)(2,1)S(1)} %bitcast.189), channel_id=1, source_target_pairs={{0,4},{4,0},{8,12},{12,8},{16,20},{20,16},{24,28},{28,24},{1,5},{5... | collective-permute-start | bytes 1572872 | tf_op jit(solution)/shard_map/ppermute | solution.py:75
  80.3 19.4 %collective-permute-start.25 = (bf16[3,80,1024]{2,1,0:T(8,128)(2,1)}, bf16[3,80,1024]{2,1,0:T(8,128)(2,1)}, u32[]{:S(2)}, u32[]{:S(2)}) collective-permute-start(bf16[3,80,1024]{2,1,0:T(8,128)(2,1)} %copy-done.31), channel_id=1, source_target_pairs={{0,24},{4,28},{8,16},{12,20},{16,8},{20,12},{24,0},{28,4},{1,25},{... | collective-permute-start | bytes 1474568 | tf_op jit(solution)/shard_map/ppermute | solution.py:75
  82.7 9.4 %collective-permute-start.21 = (bf16[4,2,64,512]{3,2,1,0:T(8,128)(2,1)S(1)}, bf16[4,2,64,512]{3,2,1,0:T(8,128)(2,1)S(1)}, u32[]{:S(2)}, u32[]{:S(2)}) collective-permute-start(bf16[4,2,64,512]{3,2,1,0:T(8,128)(2,1)S(1)} %collective-permute-done.15.refs_6_), channel_id=1, source_target_pairs={{0,4},{4,0},{8,12},{12,8},{16,20},{20,16},{24,28},{28,24},{1,5},{5... | collective-permute-start | bytes 1572872 | tf_op jit(solution)/shard_map/ppermute | solution.py:75
  82.7 10.6 %collective-permute-start.20 = (bf16[4,2,64,512]{3,2,1,0:T(8,128)(2,1)S(1)}, bf16[4,2,64,512]{3,2,1,0:T(8,128)(2,1)}, u32[]{:S(2)}, u32[]{:S(2)}) collective-permute-start(bf16[4,2,64,512]{3,2,1,0:T(8,128)(2,1)S(1)} %collective-permute-done.14.refs_4_), channel_id=1, source_target_pairs={{0,4},{4,0},{8,12},{12,8},{16,20},{20,16},{24,28},{28,24},{1,5},{5... | collective-permute-start | bytes 1572872 | tf_op jit(solution)/shard_map/ppermute | solution.py:75
  83.2 10.1 %collective-permute-start.19 = (bf16[4,2,64,512]{3,2,1,0:T(8,128)(2,1)S(1)}, bf16[4,2,64,512]{3,2,1,0:T(8,128)(2,1)}, u32[]{:S(2)}, u32[]{:S(2)}) collective-permute-start(bf16[4,2,64,512]{3,2,1,0:T(8,128)(2,1)S(1)} %collective-permute-done.13.refs_2_), channel_id=1, source_target_pairs={{0,4},{4,0},{8,12},{12,8},{16,20},{20,16},{24,28},{28,24},{1,5},{5... | collective-permute-start | bytes 1572872 | tf_op jit(solution)/shard_map/ppermute | solution.py:75
  91.4 13.8 %collective-permute-start.24 = (bf16[3,80,1024]{2,1,0:T(8,128)(2,1)S(1)}, bf16[3,80,1024]{2,1,0:T(8,128)(2,1)S(1)}, u32[]{:S(2)}, u32[]{:S(2)}) collective-permute-start(bf16[3,80,1024]{2,1,0:T(8,128)(2,1)S(1)} %copy-done.32), channel_id=1, source_target_pairs={{0,16},{4,20},{8,24},{12,28},{16,0},{20,4},{24,8},{28,12},{1,17},{... | collective-permute-start | bytes 1474568 | tf_op jit(solution)/shard_map/ppermute | solution.py:75
  92.0 13.4 %collective-permute-start.23 = (bf16[3,80,1024]{2,1,0:T(8,128)(2,1)S(1)}, bf16[3,80,1024]{2,1,0:T(8,128)(2,1)S(1)}, u32[]{:S(2)}, u32[]{:S(2)}) collective-permute-start(bf16[3,80,1024]{2,1,0:T(8,128)(2,1)S(1)} %copy-done.32), channel_id=1, source_target_pairs={{0,8},{4,12},{8,0},{12,4},{16,24},{20,28},{24,16},{28,20},{1,9},{5... | collective-permute-start | bytes 1474568 | tf_op jit(solution)/shard_map/ppermute | solution.py:75
  106.7 4.0 %collective-permute-start.26 = (bf16[3,4,1,80,1024]{4,3,2,1,0:T(8,128)(2,1)S(1)}, bf16[3,4,1,80,1024]{4,3,2,1,0:T(8,128)(2,1)S(1)}, u32[]{:S(2)}, u32[]{:S(2)}) collective-permute-start(bf16[3,4,1,80,1024]{4,3,2,1,0:T(8,128)(2,1)S(1)} %bitcast.208), channel_id=1, source_target_pairs={{0,4},{4,0},{8,12},{12,8},{16,20},{20,16},{24,28},{28,24},{1,5},{5... | collective-permute-start | bytes 5898248 | tf_op jit(solution)/shard_map/ppermute | solution.py:75
  108.8 6.6 %collective-permute-start.22 = (bf16[128,640]{1,0:T(8,128)(2,1)S(1)}, bf16[128,640]{1,0:T(8,128)(2,1)S(1)}, u32[]{:S(2)}, u32[]{:S(2)}) collective-permute-start(bf16[128,640]{1,0:T(8,128)(2,1)S(1)} %multiply_convert_fusion.6), channel_id=1, source_target_pairs={{0,1},{1,0},{2,3},{3,2},{4,5},{5,4},{6,7},{7,6},{8,9},{9,8},{10,11... | collective-permute-start | bytes 491528 | tf_op jit(solution)/shard_map/ppermute | solution.py:75
  117.4 5.8 %collective-permute-start.27 = (bf16[128,640]{1,0:T(8,128)(2,1)S(1)}, bf16[128,640]{1,0:T(8,128)(2,1)S(1)}, u32[]{:S(2)}, u32[]{:S(2)}) collective-permute-start(bf16[128,640]{1,0:T(8,128)(2,1)S(1)} %split.269), channel_id=1, source_target_pairs={{0,1},{1,0},{2,3},{3,2},{4,5},{5,4},{6,7},{7,6},{8,9},{9,8},{10,11... | collective-permute-start | bytes 491528 | tf_op jit(solution)/shard_map/ppermute | solution.py:75
  124.0 5.4 %collective-permute-start.28 = (bf16[128,640]{1,0:T(8,128)(2,1)S(1)}, bf16[128,640]{1,0:T(8,128)(2,1)S(1)}, u32[]{:S(2)}, u32[]{:S(2)}) collective-permute-start(bf16[128,640]{1,0:T(8,128)(2,1)S(1)} %multiply_convert_fusion.5), channel_id=1, source_target_pairs={{0,1},{1,0},{2,3},{3,2},{4,5},{5,4},{6,7},{7,6},{8,9},{9,8},{10,11... | collective-permute-start | bytes 491528 | tf_op jit(solution)/shard_map/ppermute | solution.py:75
  132.8 8.6 %collective-permute-start.30 = (bf16[3,4,80,1024]{3,2,1,0:T(8,128)(2,1)S(1)}, bf16[3,4,80,1024]{3,2,1,0:T(8,128)(2,1)S(1)}, u32[]{:S(2)}, u32[]{:S(2)}) collective-permute-start(bf16[3,4,80,1024]{3,2,1,0:T(8,128)(2,1)S(1)} %slice_bitcast_fusion), channel_id=1, source_target_pairs={{0,4},{4,0},{8,12},{12,8},{16,20},{20,16},{24,28},{28,24},{1,5},{5... | collective-permute-start | bytes 5898248 | tf_op jit(solution)/shard_map/ppermute | solution.py:75
  134.2 6.7 %collective-permute-start.29 = (bf16[128,640]{1,0:T(8,128)(2,1)S(1)}, bf16[128,640]{1,0:T(8,128)(2,1)S(1)}, u32[]{:S(2)}, u32[]{:S(2)}) collective-permute-start(bf16[128,640]{1,0:T(8,128)(2,1)S(1)} %split.268), channel_id=1, source_target_pairs={{0,1},{1,0},{2,3},{3,2},{4,5},{5,4},{6,7},{7,6},{8,9},{9,8},{10,11... | collective-permute-start | bytes 491528 | tf_op jit(solution)/shard_map/ppermute | solution.py:75
  143.7 15.1 %collective-permute-start.33 = (bf16[3,80,1024]{2,1,0:T(8,128)(2,1)S(1)}, bf16[3,80,1024]{2,1,0:T(8,128)(2,1)S(1)}, u32[]{:S(2)}, u32[]{:S(2)}) collective-permute-start(bf16[3,80,1024]{2,1,0:T(8,128)(2,1)S(1)} %get-tuple-element.145), channel_id=1, source_target_pairs={{0,24},{4,28},{8,16},{12,20},{16,8},{20,12},{24,0},{28,4},{1,25},{... | collective-permute-start | bytes 1474568 | tf_op jit(solution)/shard_map/ppermute | solution.py:75
  145.8 22.2 %collective-permute-start.32 = (bf16[3,80,1024]{2,1,0:T(8,128)(2,1)S(1)}, bf16[3,80,1024]{2,1,0:T(8,128)(2,1)S(1)}, u32[]{:S(2)}, u32[]{:S(2)}) collective-permute-start(bf16[3,80,1024]{2,1,0:T(8,128)(2,1)S(1)} %get-tuple-element.146), channel_id=1, source_target_pairs={{0,16},{4,20},{8,24},{12,28},{16,0},{20,4},{24,8},{28,12},{1,17},{... | collective-permute-start | bytes 1474568 | tf_op jit(solution)/shard_map/ppermute | solution.py:75
  146.4 21.6 %collective-permute-start.31 = (bf16[3,80,1024]{2,1,0:T(8,128)(2,1)S(1)}, bf16[3,80,1024]{2,1,0:T(8,128)(2,1)S(1)}, u32[]{:S(2)}, u32[]{:S(2)}) collective-permute-start(bf16[3,80,1024]{2,1,0:T(8,128)(2,1)S(1)} %get-tuple-element.147), channel_id=1, source_target_pairs={{0,8},{4,12},{8,0},{12,4},{16,24},{20,28},{24,16},{28,20},{1,9},{5... | collective-permute-start | bytes 1474568 | tf_op jit(solution)/shard_map/ppermute | solution.py:75
  168.0 5.2 %collective-permute-start.34 = (bf16[4,4,2,64,512]{4,3,2,1,0:T(8,128)(2,1)}, bf16[4,4,2,64,512]{4,3,2,1,0:T(8,128)(2,1)}, u32[]{:S(2)}, u32[]{:S(2)}) collective-permute-start(bf16[4,4,2,64,512]{4,3,2,1,0:T(8,128)(2,1)} %get-tuple-element.77), channel_id=1, source_target_pairs={{0,4},{4,0},{8,12},{12,8},{16,20},{20,16},{24,28},{28,24},{1,5},{5... | collective-permute-start | bytes 6291464 | tf_op jit(solution)/shard_map/ppermute | solution.py:75
  172.1 14.4 %collective-permute-start.53 = (bf16[3,80,512]{2,1,0:T(8,128)(2,1)S(1)}, bf16[3,80,512]{2,1,0:T(8,128)(2,1)S(1)}, u32[]{:S(2)}, u32[]{:S(2)}) collective-permute-start(bf16[3,80,512]{2,1,0:T(8,128)(2,1)S(1)} %split.210), channel_id=1, source_target_pairs={{0,2},{1,3},{2,0},{3,1},{4,6},{5,7},{6,4},{7,5},{8,10},{9,11},{10,... | collective-permute-start | bytes 737288 | tf_op jit(solution)/shard_map/ppermute | solution.py:75
  177.3 32.0 %collective-permute-start.41 = (bf16[2,4,80,1024]{3,2,1,0:T(8,128)(2,1)S(1)}, bf16[2,4,80,1024]{3,2,1,0:T(8,128)(2,1)S(1)}, u32[]{:S(2)}, u32[]{:S(2)}) collective-permute-start(bf16[2,4,80,1024]{3,2,1,0:T(8,128)(2,1)S(1)} %fusion.13), channel_id=1, source_target_pairs={{0,4},{4,0},{8,12},{12,8},{16,20},{20,16},{24,28},{28,24},{1,5},{5... | collective-permute-start | bytes 3932168 | tf_op jit(solution)/shard_map/ppermute | solution.py:75
  177.7 14.8 %collective-permute-start.35 = (bf16[1,4,2,64,512]{4,3,2,1,0:T(8,128)(2,1)S(1)}, bf16[1,4,2,64,512]{4,3,2,1,0:T(8,128)(2,1)S(1)}, u32[]{:S(2)}, u32[]{:S(2)}) collective-permute-start(bf16[1,4,2,64,512]{4,3,2,1,0:T(8,128)(2,1)S(1)} %get-tuple-element.140), channel_id=1, source_target_pairs={{0,8},{4,12},{8,0},{12,4},{16,24},{20,28},{24,16},{28,20},{1,9},{5... | collective-permute-start | bytes 1572872 | tf_op jit(solution)/shard_map/ppermute | solution.py:75
  179.0 25.1 %collective-permute-start.37 = (bf16[1,4,2,64,512]{4,3,2,1,0:T(8,128)(2,1)S(1)}, bf16[1,4,2,64,512]{4,3,2,1,0:T(8,128)(2,1)S(1)}, u32[]{:S(2)}, u32[]{:S(2)}) collective-permute-start(bf16[1,4,2,64,512]{4,3,2,1,0:T(8,128)(2,1)S(1)} %get-tuple-element.141), channel_id=1, source_target_pairs={{0,24},{4,28},{8,16},{12,20},{16,8},{20,12},{24,0},{28,4},{1,25},{... | collective-permute-start | bytes 1572872 | tf_op jit(solution)/shard_map/ppermute | solution.py:75
  180.6 24.8 %collective-permute-start.36 = (bf16[1,4,2,64,512]{4,3,2,1,0:T(8,128)(2,1)S(1)}, bf16[1,4,2,64,512]{4,3,2,1,0:T(8,128)(2,1)S(1)}, u32[]{:S(2)}, u32[]{:S(2)}) collective-permute-start(bf16[1,4,2,64,512]{4,3,2,1,0:T(8,128)(2,1)S(1)} %get-tuple-element.142), channel_id=1, source_target_pairs={{0,16},{4,20},{8,24},{12,28},{16,0},{20,4},{24,8},{28,12},{1,17},{... | collective-permute-start | bytes 1572872 | tf_op jit(solution)/shard_map/ppermute | solution.py:75
  205.8 6.6 %collective-permute-start.38 = (bf16[1,2,64,512]{3,2,1,0:T(8,128)(2,1)S(1)}, bf16[1,2,64,512]{3,2,1,0:T(8,128)(2,1)S(1)}, u32[]{:S(2)}, u32[]{:S(2)}) collective-permute-start(bf16[1,2,64,512]{3,2,1,0:T(8,128)(2,1)S(1)} %get-tuple-element.153), channel_id=1, source_target_pairs={{0,1},{1,0},{2,3},{3,2},{4,5},{5,4},{6,7},{7,6},{8,9},{9,8},{10,11... | collective-permute-start | bytes 393224 | tf_op jit(solution)/shard_map/ppermute | solution.py:75
  207.4 8.7 %collective-permute-start.40 = (bf16[1,2,64,512]{3,2,1,0:T(8,128)(2,1)S(1)}, bf16[1,2,64,512]{3,2,1,0:T(8,128)(2,1)S(1)}, u32[]{:S(2)}, u32[]{:S(2)}) collective-permute-start(bf16[1,2,64,512]{3,2,1,0:T(8,128)(2,1)S(1)} %get-tuple-element.154), channel_id=1, source_target_pairs={{0,3},{1,2},{2,1},{3,0},{4,7},{5,6},{6,5},{7,4},{8,11},{9,10},{10,... | collective-permute-start | bytes 393224 | tf_op jit(solution)/shard_map/ppermute | solution.py:75
  209.2 11.1 %collective-permute-start.39 = (bf16[1,2,64,512]{3,2,1,0:T(8,128)(2,1)S(1)}, bf16[1,2,64,512]{3,2,1,0:T(8,128)(2,1)S(1)}, u32[]{:S(2)}, u32[]{:S(2)}) collective-permute-start(bf16[1,2,64,512]{3,2,1,0:T(8,128)(2,1)S(1)} %get-tuple-element.155), channel_id=1, source_target_pairs={{0,2},{1,3},{2,0},{3,1},{4,6},{5,7},{6,4},{7,5},{8,10},{9,11},{10,... | collective-permute-start | bytes 393224 | tf_op jit(solution)/shard_map/ppermute | solution.py:75
  210.0 11.6 %collective-permute-start.44 = (bf16[2,80,1024]{2,1,0:T(8,128)(2,1)S(1)}, bf16[2,80,1024]{2,1,0:T(8,128)(2,1)S(1)}, u32[]{:S(2)}, u32[]{:S(2)}) collective-permute-start(bf16[2,80,1024]{2,1,0:T(8,128)(2,1)S(1)} %get-tuple-element.148), channel_id=1, source_target_pairs={{0,24},{4,28},{8,16},{12,20},{16,8},{20,12},{24,0},{28,4},{1,25},{... | collective-permute-start | bytes 983048 | tf_op jit(solution)/shard_map/ppermute | solution.py:75
  211.4 14.4 %collective-permute-start.43 = (bf16[2,80,1024]{2,1,0:T(8,128)(2,1)S(1)}, bf16[2,80,1024]{2,1,0:T(8,128)(2,1)S(1)}, u32[]{:S(2)}, u32[]{:S(2)}) collective-permute-start(bf16[2,80,1024]{2,1,0:T(8,128)(2,1)S(1)} %get-tuple-element.149), channel_id=1, source_target_pairs={{0,16},{4,20},{8,24},{12,28},{16,0},{20,4},{24,8},{28,12},{1,17},{... | collective-permute-start | bytes 983048 | tf_op jit(solution)/shard_map/ppermute | solution.py:75
  212.4 13.4 %collective-permute-start.42 = (bf16[2,80,1024]{2,1,0:T(8,128)(2,1)S(1)}, bf16[2,80,1024]{2,1,0:T(8,128)(2,1)S(1)}, u32[]{:S(2)}, u32[]{:S(2)}) collective-permute-start(bf16[2,80,1024]{2,1,0:T(8,128)(2,1)S(1)} %get-tuple-element.150), channel_id=1, source_target_pairs={{0,8},{4,12},{8,0},{12,4},{16,24},{20,28},{24,16},{28,20},{1,9},{5... | collective-permute-start | bytes 983048 | tf_op jit(solution)/shard_map/ppermute | solution.py:75
  236.0 1.2 collective-permute-start.46
  236.5 1.7 collective-permute-start.45
  238.4 5.4 %collective-permute-start.47 = (bf16[92,512]{1,0:T(8,128)(2,1)S(1)}, bf16[92,512]{1,0:T(8,128)(2,1)S(1)}, u32[]{:S(2)}, u32[]{:S(2)}) collective-permute-start(bf16[92,512]{1,0:T(8,128)(2,1)S(1)} %get-tuple-element.187), channel_id=1, source_target_pairs={{0,8},{4,12},{8,0},{12,4},{16,24},{20,28},{24,16},{28,20},{1,9},{5... | collective-permute-start | bytes 282632 | tf_op jit(solution)/shard_map/ppermute | solution.py:75
  239.3 6.9 %collective-permute-start.48 = (bf16[92,512]{1,0:T(8,128)(2,1)S(1)}, bf16[92,512]{1,0:T(8,128)(2,1)S(1)}, u32[]{:S(2)}, u32[]{:S(2)}) collective-permute-start(bf16[92,512]{1,0:T(8,128)(2,1)S(1)} %get-tuple-element.188), channel_id=1, source_target_pairs={{0,16},{4,20},{8,24},{12,28},{16,0},{20,4},{24,8},{28,12},{1,17},{... | collective-permute-start | bytes 282632 | tf_op jit(solution)/shard_map/ppermute | solution.py:75
  240.3 5.9 %collective-permute-start.49 = (bf16[92,512]{1,0:T(8,128)(2,1)S(1)}, bf16[92,512]{1,0:T(8,128)(2,1)S(1)}, u32[]{:S(2)}, u32[]{:S(2)}) collective-permute-start(bf16[92,512]{1,0:T(8,128)(2,1)S(1)} %get-tuple-element.189), channel_id=1, source_target_pairs={{0,24},{4,28},{8,16},{12,20},{16,8},{20,12},{24,0},{28,4},{1,25},{... | collective-permute-start | bytes 282632 | tf_op jit(solution)/shard_map/ppermute | solution.py:75
  246.5 7.1 %collective-permute-start.50 = (bf16[224,256]{1,0:T(8,128)(2,1)S(1)}, bf16[224,256]{1,0:T(8,128)(2,1)S(1)}, u32[]{:S(2)}, u32[]{:S(2)}) collective-permute-start(bf16[224,256]{1,0:T(8,128)(2,1)S(1)} %get-tuple-element.190), channel_id=1, source_target_pairs={{0,1},{1,0},{2,3},{3,2},{4,5},{5,4},{6,7},{7,6},{8,9},{9,8},{10,11... | collective-permute-start | bytes 344072 | tf_op jit(solution)/shard_map/ppermute | solution.py:75
  251.2 9.8 %collective-permute-start.51 = (bf16[224,256]{1,0:T(8,128)(2,1)S(1)}, bf16[224,256]{1,0:T(8,128)(2,1)S(1)}, u32[]{:S(2)}, u32[]{:S(2)}) collective-permute-start(bf16[224,256]{1,0:T(8,128)(2,1)S(1)} %get-tuple-element.191), channel_id=1, source_target_pairs={{0,2},{1,3},{2,0},{3,1},{4,6},{5,7},{6,4},{7,5},{8,10},{9,11},{10,... | collective-permute-start | bytes 344072 | tf_op jit(solution)/shard_map/ppermute | solution.py:75
  251.6 9.4 %collective-permute-start.52 = (bf16[224,256]{1,0:T(8,128)(2,1)S(1)}, bf16[224,256]{1,0:T(8,128)(2,1)S(1)}, u32[]{:S(2)}, u32[]{:S(2)}) collective-permute-start(bf16[224,256]{1,0:T(8,128)(2,1)S(1)} %get-tuple-element.192), channel_id=1, source_target_pairs={{0,3},{1,2},{2,1},{3,0},{4,7},{5,6},{6,5},{7,4},{8,11},{9,10},{10,... | collective-permute-start | bytes 344072 | tf_op jit(solution)/shard_map/ppermute | solution.py:75
  (63 other events, 333.5 us)

commit v2 on v1

--- a/solution.py
+++ b/solution.py
@@ -614,9 +614,8 @@
     kv_own = jnp.concatenate([keys_own, values_own], axis=-1).reshape(
         shard_size, 2, half_len, 2 * HEAD
     )
-    attn_own = after(
-        jnp.stack([side_by_side(2 * slice_len, HEAD), side_by_side(2 * slice_len + HEAD, HEAD)]),
-        keyval_marks,
+    attn_own = jnp.stack(
+        [side_by_side(2 * slice_len, HEAD), side_by_side(2 * slice_len + HEAD, HEAD)]
     )
     attn_got = [attn_own] + [swap(attn_own, "ctx", 2 * k) for k in range(1, chip_count())]
     kv_marks = [swap(kv_own, "ctx", 2 * k) for k in range(1, chip_count())]
@@ -624,12 +623,16 @@
     attn_full = core_rows(jnp.concatenate(attn_got, axis=-2))
     query_full, output_full = (attn_full[0], attn_full[1])
     query_proj = nn(attn_in, query_full)
-    query_normed, query_inverse = rms_forward(query_proj.reshape(row_count, HEADS, HEAD))
-    query_scaled = query_normed * (1.0 + head_scales[0])
-    query_rows = (
-        (query_scaled * cosine[:, None, :] + rotate(query_scaled) * sine[:, None, :])
-        .astype(bfloat)
-        .reshape(row_count, HEADS * HEAD)
+    query_heads = [
+        rms_forward(query_proj[:, h * HEAD : (h + 1) * HEAD]) for h in range(HEADS)
+    ]
+
+    def turn(values):
+        return values * cosine + rotate(values) * sine
+
+    query_rows = jnp.concatenate(
+        [turn(normed * (1.0 + head_scales[0])).astype(bfloat) for normed, _ in query_heads],
+        axis=1,
     )
     kv_pieces = [
         piece
@@ -692,15 +695,19 @@
     kv_core = kv_terms
     kv_terms, kv_marks = scatter_chips(kv_terms, 0)
     kv_grad = scatter_shard(kv_terms.astype(bfloat)[0], 0).reshape(row_count, 2 * HEAD)
-    query_rot_grad = query_parts.reshape(row_count, HEADS, HEAD)
-    query_rope_grad = query_rot_grad * cosine[:, None, :] + rotate_back(
-        query_rot_grad * sine[:, None, :]
-    )
-    grad_head0 = jnp.sum(query_rope_grad * query_normed, axis=(0, 1))
-    query_proj_grad = (
-        rms_backward(query_normed, query_inverse, query_rope_grad * (1.0 + head_scales[0]))
-        .reshape(row_count, HEADS * HEAD)
-        .astype(bfloat)
+    query_rope_grads = []
+    for h in range(HEADS):
+        part = query_parts[:, h * HEAD : (h + 1) * HEAD]
+        query_rope_grads.append(part * cosine + rotate_back(part * sine))
+    grad_head0 = sum(
+        jnp.sum(part * normed, axis=0) for part, (normed, _) in zip(query_rope_grads, query_heads)
+    )
+    query_proj_grad = jnp.concatenate(
+        [
+            rms_backward(normed, inverse, part * (1.0 + head_scales[0])).astype(bfloat)
+            for part, (normed, inverse) in zip(query_rope_grads, query_heads)
+        ],
+        axis=1,
     )
     late_grad, late_out_grad = after((query_proj_grad, attn_out_grad), kv_core)
     query_wgrad = tn(attn_in, late_grad).astype(bfloat)

time: 266 us -> 263 us (0.989)
  waiting for transfers between devices: 120 us -> 134 us
  local copies, waits for them, and re-layouts: 13.5 us -> 4.69 us
  other arithmetic: 31.7 us -> 25.2 us
    ppermute x54, waiting for transfers between devices: 120 us -> 134 us  [swap(): lax.ppermute(piece, axis, [(i, i ^ distance) for i in range(lax.axis_size...]
    unnamed x146 -> x110, local copies, waits for them, and re-layouts: 5.88 us -> 2.8 us
  transfers between devices with their start and end apart: 54 -> 54, of which waited for: 26 -> 32; matrix products, arithmetic and copies ran while one was open for 14% -> 10% of each run, Pallas kernels for 6% -> 5%
where the time goes in v2:
time: 263 us; the launch traced here: 262 us
  waiting for transfers between devices  134 us (51%)
  starting transfers between devices  59.5 us (23%)
  other arithmetic  25.2 us (10%)
  matrix products  22.5 us (9%)
  Pallas kernels  13.9 us (5%)
  local copies, waits for them, and re-layouts  4.69 us (2%)
    ppermute x54, waiting for transfers between devices, swap(): lax.ppermute(piece, axis, [(i, i ^ distance) for i in range(lax.axis_size...  134 us
    ppermute x54, starting transfers between devices, swap(): lax.ppermute(piece, axis, [(i, i ^ distance) for i in range(lax.axis_size...  59.5 us
    dot_general x9, matrix products, nt(): lax.dot_general(left, right, (((1,), (1,)), ((), ())), preferred_element_...  12 us
    pallas_call x1, Pallas kernels, attention_backward(): pl.pallas_call(backward_kernel, out_shape=(jax.ShapeDtypeStruct(queries.s...  9.3 us
    dot_general x9, matrix products, nn(): return jnp.dot(left, right, preferred_element_type=jnp.float32)  5.71 us
    sub x7, other arithmetic, adam_update(): weight - learn_rate * (first_hat / (jnp.sqrt(second_hat) + adam_eps) + we...  5.43 us
  transfers between devices with their start and end apart: 54, of which 32 were waited for; matrix products, arithmetic and copies ran while one was open for 10% of the time, Pallas kernels for 5%

profile of v2, /device:TPU:0, one launch (start us, length us, event | category | flops | bytes accessed | tf_op | source)
XLA Modules:
  0.0 262.0 jit_solution(13002684204625591166)
XLA Ops:
  3.6 5.1 %collective-permute-start.5 = (bf16[1,80,640]{2,1,0:T(8,128)(2,1)S(1)}, bf16[1,80,640]{2,1,0:T(8,128)(2,1)S(1)}, u32[]{:S(2)}, u32[]{:S(2)}) collective-permute-start(bf16[1,80,640]{2,1,0:T(8,128)(2,1)S(1)} %maximum_bitcast_fusion.2), channel_id=1, source_target_pairs={{0,3},{1,2},{2,1},{3,0},{4,7},{5,6},{6,5},{7,4},{8,11},{9,10},{10,... | collective-permute-start | bytes 307208 | tf_op jit(solution)/shard_map/ppermute | solution.py:75
  9.4 2.3 collective-permute-start.1
  11.6 2.0 collective-permute-start
  15.4 1.3 fusion.17
  18.1 3.7 %collective-permute-done.4 = bf16[1,80,640]{2,1,0:T(8,128)(2,1)S(1)} collective-permute-done((bf16[1,80,640]{2,1,0:T(8,128)(2,1)S(1)}, bf16[1,80,640]{2,1,0:T(8,128)(2,1)S(1)}, u32[]{:S(2)}, u32[]{:S(2)}) %collective-permute-start.4) | collective-permute-done | bytes 102432 | tf_op jit(solution)/shard_map/ppermute | solution.py:75
  21.8 2.5 collective-permute-start.11
  25.0 3.9 %collective-permute-done.1 = bf16[128,640]{1,0:T(8,128)(2,1)S(1)} collective-permute-done((bf16[128,640]{1,0:T(8,128)(2,1)}, bf16[128,640]{1,0:T(8,128)(2,1)S(1)}, u32[]{:S(2)}, u32[]{:S(2)}) %collective-permute-start.1) | collective-permute-done | bytes 163872 | tf_op jit(solution)/shard_map/ppermute | solution.py:75
  28.8 1.5 collective-permute-start.9
  30.3 1.5 collective-permute-start.8
  34.2 1.3 multiply_convert_fusion
  38.5 2.6 %collective-permute-start.15 = (bf16[4,2,64,512]{3,2,1,0:T(8,128)(2,1)S(1)}, bf16[4,2,64,512]{3,2,1,0:T(8,128)(2,1)S(1)}, u32[]{:S(2)}, u32[]{:S(2)}) collective-permute-start(bf16[4,2,64,512]{3,2,1,0:T(8,128)(2,1)S(1)} %bitcast.166), channel_id=1, source_target_pairs={{0,24},{4,28},{8,16},{12,20},{16,8},{20,12},{24,0},{28,4},{1,25},{... | collective-permute-start | bytes 1572872 | tf_op jit(solution)/shard_map/ppermute | solution.py:75
  42.0 1.4 collective-permute-done.16
  43.5 1.3 collective-permute-start.7
  44.8 1.5 collective-permute-start.6
  46.4 25.3 %collective-permute-done.7 = bf16[2,80,1024]{2,1,0:T(8,128)(2,1)S(1)} collective-permute-done((bf16[2,80,1024]{2,1,0:T(8,128)(2,1)S(1)}, bf16[2,80,1024]{2,1,0:T(8,128)(2,1)S(1)}, u32[]{:S(2)}, u32[]{:S(2)}) %collective-permute-start.7) | collective-permute-done | bytes 327712 | tf_op jit(solution)/shard_map/ppermute | solution.py:75
  72.0 1.2 pad_maximum_fusion.5
  74.2 1.5 collective-permute-start.25
  75.7 1.4 collective-permute-start.24
  77.7 1.9 fusion.10
  81.6 1.3 collective-permute-done.20.refs_5_
  83.6 4.6 %attention_forward.1 = (f32[128,1024]{1,0:T(8,128)S(1)}, f32[512,1]{1,0:T(8,128)S(1)}) custom-call(s32[10]{0:T(128)S(1)} %pad_add_fusion.table_ref, bf16[128,1024]{1,0:T(8,128)(2,1)S(1)} %pad_maximum_fusion.14.query_ref, bf16[4,2,64,512]{3,2,1,0:T(8,128)(2,1)S(1)} %bitcast.170, bf16[4,2,64,512]{3,2,1,0:T(8,128)(2,1)S(1)} %collective-permute-done.18.refs_1_, ...), custom_call_target="tpu_custom_call" | custom-call | tf_op jit(solution)/shard_map/attention_forward/pallas_call | solution.py:437
  88.2 1.2 collective-permute-done.25
  89.4 9.6 %collective-permute-done.24 = bf16[3,80,1024]{2,1,0:T(8,128)(2,1)S(1)} collective-permute-done((bf16[3,80,1024]{2,1,0:T(8,128)(2,1)}, bf16[3,80,1024]{2,1,0:T(8,128)(2,1)S(1)}, u32[]{:S(2)}, u32[]{:S(2)}) %collective-permute-start.24) | collective-permute-done | bytes 491552 | tf_op jit(solution)/shard_map/ppermute | solution.py:75
  99.9 1.2 multiply_reduce_fusion.11
  101.3 1.7 collective-permute-start.22
  103.6 4.3 %collective-permute-done.22 = bf16[128,640]{1,0:T(8,128)(2,1)S(1)} collective-permute-done((bf16[128,640]{1,0:T(8,128)(2,1)S(1)}, bf16[128,640]{1,0:T(8,128)(2,1)S(1)}, u32[]{:S(2)}, u32[]{:S(2)}) %collective-permute-start.22) | collective-permute-done | bytes 163872 | tf_op jit(solution)/shard_map/ppermute | solution.py:75
  109.9 1.7 collective-permute-start.27
  111.6 4.2 %collective-permute-done.27 = bf16[128,640]{1,0:T(8,128)(2,1)S(1)} collective-permute-done((bf16[128,640]{1,0:T(8,128)(2,1)S(1)}, bf16[128,640]{1,0:T(8,128)(2,1)S(1)}, u32[]{:S(2)}, u32[]{:S(2)}) %collective-permute-start.27) | collective-permute-done | bytes 163872 | tf_op jit(solution)/shard_map/ppermute | solution.py:75
  116.6 1.7 collective-permute-start.28
  118.4 3.6 %collective-permute-done.28 = bf16[128,640]{1,0:T(8,128)(2,1)S(1)} collective-permute-done((bf16[128,640]{1,0:T(8,128)(2,1)S(1)}, bf16[128,640]{1,0:T(8,128)(2,1)S(1)}, u32[]{:S(2)}, u32[]{:S(2)}) %collective-permute-start.28) | collective-permute-done | bytes 163872 | tf_op jit(solution)/shard_map/ppermute | solution.py:75
  126.8 1.7 collective-permute-start.29
  128.5 1.2 fusion.15
  129.7 3.7 %collective-permute-done.29 = bf16[128,640]{1,0:T(8,128)(2,1)S(1)} collective-permute-done((bf16[128,640]{1,0:T(8,128)(2,1)S(1)}, bf16[128,640]{1,0:T(8,128)(2,1)S(1)}, u32[]{:S(2)}, u32[]{:S(2)}) %collective-permute-start.29) | collective-permute-done | bytes 163872 | tf_op jit(solution)/shard_map/ppermute | solution.py:75
  134.8 9.3 %attention_backward.1 = (f32[128,1024]{1,0:T(8,128)S(1)}, bf16[4,4,2,64,512]{4,3,2,1,0:T(8,128)(2,1)S(1)}, bf16[4,4,2,64,512]{4,3,2,1,0:T(8,128)(2,1)S(1)}) custom-call(s32[10]{0:T(128)S(1)} %pad_add_fusion.table_ref, bf16[128,1024]{1,0:T(8,128)(2,1)S(1)} %pad_maximum_fusion.14.query_ref, f32[128,1024]{1,0:T(8,128)S(1)} %get-tuple-element.64.out_ref, ...), custom_call_target="tpu_custom_call" | custom-call | tf_op jit(solution)/shard_map/attention_backward/pallas_call | solution.py:461
  145.3 1.6 collective-permute-start.33
  146.8 1.3 collective-permute-start.32
  148.9 11.5 %collective-permute-done.33 = bf16[3,80,1024]{2,1,0:T(8,128)(2,1)S(1)} collective-permute-done((bf16[3,80,1024]{2,1,0:T(8,128)(2,1)S(1)}, bf16[3,80,1024]{2,1,0:T(8,128)(2,1)S(1)}, u32[]{:S(2)}, u32[]{:S(2)}) %collective-permute-start.33) | collective-permute-done | bytes 491552 | tf_op jit(solution)/shard_map/ppermute | solution.py:75
  160.4 9.1 %collective-permute-done.32 = bf16[3,80,1024]{2,1,0:T(8,128)(2,1)S(1)} collective-permute-done((bf16[3,80,1024]{2,1,0:T(8,128)(2,1)S(1)}, bf16[3,80,1024]{2,1,0:T(8,128)(2,1)S(1)}, u32[]{:S(2)}, u32[]{:S(2)}) %collective-permute-start.32) | collective-permute-done | bytes 491552 | tf_op jit(solution)/shard_map/ppermute | solution.py:75
  170.9 1.4 collective-permute-start.53
  172.3 1.4 collective-permute-done.34
  176.0 1.5 collective-permute-start.35
  177.4 1.4 collective-permute-start.37
  179.5 5.9 %collective-permute-done.53 = bf16[3,80,512]{2,1,0:T(8,128)(2,1)S(1)} collective-permute-done((bf16[3,80,512]{2,1,0:T(8,128)(2,1)S(1)}, bf16[3,80,512]{2,1,0:T(8,128)(2,1)S(1)}, u32[]{:S(2)}, u32[]{:S(2)}) %collective-permute-start.53) | collective-permute-done | bytes 245792 | tf_op jit(solution)/shard_map/ppermute | solution.py:75
  186.7 4.1 %collective-permute-done.35 = bf16[1,4,2,64,512]{4,3,2,1,0:T(8,128)(2,1)S(1)} collective-permute-done((bf16[1,4,2,64,512]{4,3,2,1,0:T(8,128)(2,1)S(1)}, bf16[1,4,2,64,512]{4,3,2,1,0:T(8,128)(2,1)S(1)}, u32[]{:S(2)}, u32[]{:S(2)}) %collective-permute-start.35) | collective-permute-done | bytes 524320 | tf_op jit(solution)/shard_map/ppermute | solution.py:75
  190.8 11.6 %collective-permute-done.37 = bf16[1,4,2,64,512]{4,3,2,1,0:T(8,128)(2,1)S(1)} collective-permute-done((bf16[1,4,2,64,512]{4,3,2,1,0:T(8,128)(2,1)S(1)}, bf16[1,4,2,64,512]{4,3,2,1,0:T(8,128)(2,1)S(1)}, u32[]{:S(2)}, u32[]{:S(2)}) %collective-permute-start.37) | collective-permute-done | bytes 524320 | tf_op jit(solution)/shard_map/ppermute | solution.py:75
  202.4 1.4 collective-permute-done.36
  206.2 1.4 collective-permute-start.39
  208.3 1.6 collective-permute-start.44
  210.7 1.2 collective-permute-done.38
  213.3 4.8 %collective-permute-done.39 = bf16[1,2,64,512]{3,2,1,0:T(8,128)(2,1)S(1)} collective-permute-done((bf16[1,2,64,512]{3,2,1,0:T(8,128)(2,1)S(1)}, bf16[1,2,64,512]{3,2,1,0:T(8,128)(2,1)S(1)}, u32[]{:S(2)}, u32[]{:S(2)}) %collective-permute-start.39) | collective-permute-done | bytes 131104 | tf_op jit(solution)/shard_map/ppermute | solution.py:75
  218.1 1.8 collective-permute-done.44
  219.9 4.1 %collective-permute-done.43 = bf16[2,80,1024]{2,1,0:T(8,128)(2,1)S(1)} collective-permute-done((bf16[2,80,1024]{2,1,0:T(8,128)(2,1)S(1)}, bf16[2,80,1024]{2,1,0:T(8,128)(2,1)S(1)}, u32[]{:S(2)}, u32[]{:S(2)}) %collective-permute-start.43) | collective-permute-done | bytes 327712 | tf_op jit(solution)/shard_map/ppermute | solution.py:75
  225.9 2.4 convolution_convert_fusion.6
  228.3 2.6 multiply_reduce_fusion.5
  231.9 1.4 add_convert_fusion.3
  233.9 1.2 collective-permute-done.45
  236.3 1.2 collective-permute-start.48
  237.5 1.4 collective-permute-start.49
  238.9 1.9 collective-permute-done.47
  240.8 2.4 collective-permute-done.48
  243.5 2.6 collective-permute-start.50
  246.1 2.2 fusion.16
  248.7 2.1 collective-permute-start.52
  250.9 6.9 %collective-permute-done.51 = bf16[224,256]{1,0:T(8,128)(2,1)S(1)} collective-permute-done((bf16[224,256]{1,0:T(8,128)(2,1)S(1)}, bf16[224,256]{1,0:T(8,128)(2,1)S(1)}, u32[]{:S(2)}, u32[]{:S(2)}) %collective-permute-start.51) | collective-permute-done | bytes 114720 | tf_op jit(solution)/shard_map/ppermute | solution.py:75
  (354 shorter events, 49.8 us)
Async XLA Ops:
  0.7 115.2 %copy-start = (bf16[128,640]{1,0:T(8,128)(2,1)S(1)}, bf16[128,640]{1,0:T(8,128)(2,1)}, u32[]{:S(2)}) copy-start(bf16[128,640]{1,0:T(8,128)(2,1)} %param.26) | copy-start | bytes 491524
  0.7 16.1 %copy-start.14 = (f32[512,80]{0,1:T(8,128)S(1)}, f32[512,80]{0,1:T(8,128)}, u32[]{:S(2)}) copy-start(f32[512,80]{0,1:T(8,128)} %param.39) | copy-start | bytes 491524
  0.7 16.1 %copy-start.7 = (f32[2,80,512]{2,1,0:T(8,128)S(1)}, f32[2,80,512]{2,1,0:T(8,128)}, u32[]{:S(2)}) copy-start(f32[2,80,512]{2,1,0:T(8,128)} %param.36) | copy-start | bytes 983044
  3.5 14.4 %copy-start.51 = (bf16[128,640]{1,0:T(8,128)(2,1)S(1)}, bf16[128,640]{1,0:T(8,128)(2,1)}, u32[]{:S(2)}) copy-start(bf16[128,640]{1,0:T(8,128)(2,1)} %param.24) | copy-start | bytes 491524
  3.6 14.3 %collective-permute-start.5 = (bf16[1,80,640]{2,1,0:T(8,128)(2,1)S(1)}, bf16[1,80,640]{2,1,0:T(8,128)(2,1)S(1)}, u32[]{:S(2)}, u32[]{:S(2)}) collective-permute-start(bf16[1,80,640]{2,1,0:T(8,128)(2,1)S(1)} %maximum_bitcast_fusion.2), channel_id=1, source_target_pairs={{0,3},{1,2},{2,1},{3,0},{4,7},{5,6},{6,5},{7,4},{8,11},{9,10},{10,... | collective-permute-start | bytes 307208 | tf_op jit(solution)/shard_map/ppermute | solution.py:75
  8.7 13.1 %collective-permute-start.4 = (bf16[1,80,640]{2,1,0:T(8,128)(2,1)S(1)}, bf16[1,80,640]{2,1,0:T(8,128)(2,1)S(1)}, u32[]{:S(2)}, u32[]{:S(2)}) collective-permute-start(bf16[1,80,640]{2,1,0:T(8,128)(2,1)S(1)} %maximum_bitcast_fusion.2), channel_id=1, source_target_pairs={{0,2},{1,3},{2,0},{3,1},{4,6},{5,7},{6,4},{7,5},{8,10},{9,11},{10,... | collective-permute-start | bytes 307208 | tf_op jit(solution)/shard_map/ppermute | solution.py:75
  8.7 13.1 %collective-permute-start.3 = (bf16[1,80,640]{2,1,0:T(8,128)(2,1)S(1)}, bf16[1,80,640]{2,1,0:T(8,128)(2,1)S(1)}, u32[]{:S(2)}, u32[]{:S(2)}) collective-permute-start(bf16[1,80,640]{2,1,0:T(8,128)(2,1)S(1)} %maximum_bitcast_fusion.2), channel_id=1, source_target_pairs={{0,1},{1,0},{2,3},{3,2},{4,5},{5,4},{6,7},{7,6},{8,9},{9,8},{10,11... | collective-permute-start | bytes 307208 | tf_op jit(solution)/shard_map/ppermute | solution.py:75
  9.4 19.5 %collective-permute-start.1 = (bf16[128,640]{1,0:T(8,128)(2,1)}, bf16[128,640]{1,0:T(8,128)(2,1)S(1)}, u32[]{:S(2)}, u32[]{:S(2)}) collective-permute-start(bf16[128,640]{1,0:T(8,128)(2,1)} %param.24), channel_id=1, source_target_pairs={{0,2},{1,3},{2,0},{3,1},{4,6},{5,7},{6,4},{7,5},{8,10},{9,11},{10,... | collective-permute-start | bytes 491528 | tf_op jit(solution)/shard_map/ppermute | solution.py:75
  11.6 18.7 %collective-permute-start = (bf16[128,640]{1,0:T(8,128)(2,1)}, bf16[128,640]{1,0:T(8,128)(2,1)S(1)}, u32[]{:S(2)}, u32[]{:S(2)}) collective-permute-start(bf16[128,640]{1,0:T(8,128)(2,1)} %param.24), channel_id=1, source_target_pairs={{0,1},{1,0},{2,3},{3,2},{4,5},{5,4},{6,7},{7,6},{8,9},{9,8},{10,11... | collective-permute-start | bytes 491528 | tf_op jit(solution)/shard_map/ppermute | solution.py:75
  17.9 13.9 %collective-permute-start.2 = (bf16[128,640]{1,0:T(8,128)(2,1)S(1)}, bf16[128,640]{1,0:T(8,128)(2,1)S(1)}, u32[]{:S(2)}, u32[]{:S(2)}) collective-permute-start(bf16[128,640]{1,0:T(8,128)(2,1)S(1)} %copy-done.51), channel_id=1, source_target_pairs={{0,3},{1,2},{2,1},{3,0},{4,7},{5,6},{6,5},{7,4},{8,11},{9,10},{10,... | collective-permute-start | bytes 491528 | tf_op jit(solution)/shard_map/ppermute | solution.py:75
  21.8 12.0 %collective-permute-start.11 = (bf16[80,512]{1,0:T(8,128)(2,1)S(1)}, bf16[80,512]{1,0:T(8,128)(2,1)S(1)}, u32[]{:S(2)}, u32[]{:S(2)}) collective-permute-start(bf16[80,512]{1,0:T(8,128)(2,1)S(1)} %pad_maximum_fusion.29), channel_id=1, source_target_pairs={{0,24},{4,28},{8,16},{12,20},{16,8},{20,12},{24,0},{28,4},{1,25},{... | collective-permute-start | bytes 245768 | tf_op jit(solution)/shard_map/ppermute | solution.py:75
  24.4 9.5 %collective-permute-start.10 = (bf16[80,512]{1,0:T(8,128)(2,1)S(1)}, bf16[80,512]{1,0:T(8,128)(2,1)S(1)}, u32[]{:S(2)}, u32[]{:S(2)}) collective-permute-start(bf16[80,512]{1,0:T(8,128)(2,1)S(1)} %pad_maximum_fusion.29), channel_id=1, source_target_pairs={{0,16},{4,20},{8,24},{12,28},{16,0},{20,4},{24,8},{28,12},{1,17},{... | collective-permute-start | bytes 245768 | tf_op jit(solution)/shard_map/ppermute | solution.py:75
  28.8 5.3 %collective-permute-start.9 = (bf16[80,512]{1,0:T(8,128)(2,1)S(1)}, bf16[80,512]{1,0:T(8,128)(2,1)S(1)}, u32[]{:S(2)}, u32[]{:S(2)}) collective-permute-start(bf16[80,512]{1,0:T(8,128)(2,1)S(1)} %pad_maximum_fusion.29), channel_id=1, source_target_pairs={{0,8},{4,12},{8,0},{12,4},{16,24},{20,28},{24,16},{28,20},{1,9},{5... | collective-permute-start | bytes 245768 | tf_op jit(solution)/shard_map/ppermute | solution.py:75
  30.3 14.5 %collective-permute-start.8 = (bf16[2,80,1024]{2,1,0:T(8,128)(2,1)S(1)}, bf16[2,80,1024]{2,1,0:T(8,128)(2,1)S(1)}, u32[]{:S(2)}, u32[]{:S(2)}) collective-permute-start(bf16[2,80,1024]{2,1,0:T(8,128)(2,1)S(1)} %pad_maximum_fusion.10), channel_id=1, source_target_pairs={{0,24},{4,28},{8,16},{12,20},{16,8},{20,12},{24,0},{28,4},{1,25},{... | collective-permute-start | bytes 983048 | tf_op jit(solution)/shard_map/ppermute | solution.py:75
  31.8 11.7 %collective-permute-start.16 = (bf16[3,80,512]{2,1,0:T(8,128)(2,1)S(1)}, bf16[3,80,512]{2,1,0:T(8,128)(2,1)S(1)}, u32[]{:S(2)}, u32[]{:S(2)}) collective-permute-start(bf16[3,80,512]{2,1,0:T(8,128)(2,1)S(1)} %pad_maximum_fusion.16), channel_id=1, source_target_pairs={{0,2},{1,3},{2,0},{3,1},{4,6},{5,7},{6,4},{7,5},{8,10},{9,11},{10,... | collective-permute-start | bytes 737288 | tf_op jit(solution)/shard_map/ppermute | solution.py:75
  34.1 1.7 collective-permute-start.12
  34.2 84.1 %copy-start.48 = (f32[512]{0:T(512)}, f32[512]{0:T(512)S(1)}, u32[]{:S(2)}) copy-start(f32[512]{0:T(512)S(1)} %add_rsqrt_fusion.1) | copy-start | bytes 6148
  37.3 81.1 %copy-start.45 = (f32[512]{0:T(512)}, f32[512]{0:T(512)S(1)}, u32[]{:S(2)}) copy-start(f32[512]{0:T(512)S(1)} %add_rsqrt_fusion) | copy-start | bytes 6148
  38.5 33.5 %collective-permute-start.15 = (bf16[4,2,64,512]{3,2,1,0:T(8,128)(2,1)S(1)}, bf16[4,2,64,512]{3,2,1,0:T(8,128)(2,1)S(1)}, u32[]{:S(2)}, u32[]{:S(2)}) collective-permute-start(bf16[4,2,64,512]{3,2,1,0:T(8,128)(2,1)S(1)} %bitcast.166), channel_id=1, source_target_pairs={{0,24},{4,28},{8,16},{12,20},{16,8},{20,12},{24,0},{28,4},{1,25},{... | collective-permute-start | bytes 1572872 | tf_op jit(solution)/shard_map/ppermute | solution.py:75
  41.1 30.8 %collective-permute-start.14 = (bf16[4,2,64,512]{3,2,1,0:T(8,128)(2,1)S(1)}, bf16[4,2,64,512]{3,2,1,0:T(8,128)(2,1)S(1)}, u32[]{:S(2)}, u32[]{:S(2)}) collective-permute-start(bf16[4,2,64,512]{3,2,1,0:T(8,128)(2,1)S(1)} %bitcast.167), channel_id=1, source_target_pairs={{0,16},{4,20},{8,24},{12,28},{16,0},{20,4},{24,8},{28,12},{1,17},{... | collective-permute-start | bytes 1572872 | tf_op jit(solution)/shard_map/ppermute | solution.py:75
  41.6 30.3 %collective-permute-start.13 = (bf16[4,2,64,512]{3,2,1,0:T(8,128)(2,1)S(1)}, bf16[4,2,64,512]{3,2,1,0:T(8,128)(2,1)S(1)}, u32[]{:S(2)}, u32[]{:S(2)}) collective-permute-start(bf16[4,2,64,512]{3,2,1,0:T(8,128)(2,1)S(1)} %bitcast.168), channel_id=1, source_target_pairs={{0,8},{4,12},{8,0},{12,4},{16,24},{20,28},{24,16},{28,20},{1,9},{5... | collective-permute-start | bytes 1572872 | tf_op jit(solution)/shard_map/ppermute | solution.py:75
  43.5 28.2 %collective-permute-start.7 = (bf16[2,80,1024]{2,1,0:T(8,128)(2,1)S(1)}, bf16[2,80,1024]{2,1,0:T(8,128)(2,1)S(1)}, u32[]{:S(2)}, u32[]{:S(2)}) collective-permute-start(bf16[2,80,1024]{2,1,0:T(8,128)(2,1)S(1)} %pad_maximum_fusion.10), channel_id=1, source_target_pairs={{0,16},{4,20},{8,24},{12,28},{16,0},{20,4},{24,8},{28,12},{1,17},{... | collective-permute-start | bytes 983048 | tf_op jit(solution)/shard_map/ppermute | solution.py:75
  44.8 27.1 %collective-permute-start.6 = (bf16[2,80,1024]{2,1,0:T(8,128)(2,1)S(1)}, bf16[2,80,1024]{2,1,0:T(8,128)(2,1)S(1)}, u32[]{:S(2)}, u32[]{:S(2)}) collective-permute-start(bf16[2,80,1024]{2,1,0:T(8,128)(2,1)S(1)} %pad_maximum_fusion.10), channel_id=1, source_target_pairs={{0,8},{4,12},{8,0},{12,4},{16,24},{20,28},{24,16},{28,20},{1,9},{5... | collective-permute-start | bytes 983048 | tf_op jit(solution)/shard_map/ppermute | solution.py:75
  46.4 25.6 %copy-start.12 = (bf16[3,80,1024]{2,1,0:T(8,128)(2,1)}, bf16[3,80,1024]{2,1,0:T(8,128)(2,1)S(1)}, u32[]{:S(2)}) copy-start(bf16[3,80,1024]{2,1,0:T(8,128)(2,1)S(1)} %constant_dynamic-update-slice_fusion) | copy-start | bytes 1474564
  46.4 26.7 %copy-start.41 = (s32[4096]{0:T(1024)S(1)}, s32[4096]{0:T(1024)}, u32[]{:S(2)}) copy-start(s32[4096]{0:T(1024)} %param.25) | copy-start | bytes 49156
  73.1 4.6 %collective-permute-start.17 = (bf16[2,4,1,80,1024]{4,3,2,1,0:T(8,128)(2,1)}, bf16[2,4,1,80,1024]{4,3,2,1,0:T(8,128)(2,1)}, u32[]{:S(2)}, u32[]{:S(2)}) collective-permute-start(bf16[2,4,1,80,1024]{4,3,2,1,0:T(8,128)(2,1)} %bitcast.28), channel_id=1, source_target_pairs={{0,4},{4,0},{8,12},{12,8},{16,20},{20,16},{24,28},{28,24},{1,5},{5... | collective-permute-start | bytes 3932168 | tf_op jit(solution)/shard_map/ppermute | solution.py:75
  73.7 7.1 %collective-permute-start.18 = (bf16[4,2,64,512]{3,2,1,0:T(8,128)(2,1)S(1)}, bf16[4,2,64,512]{3,2,1,0:T(8,128)(2,1)S(1)}, u32[]{:S(2)}, u32[]{:S(2)}) collective-permute-start(bf16[4,2,64,512]{3,2,1,0:T(8,128)(2,1)S(1)} %bitcast.169), channel_id=1, source_target_pairs={{0,4},{4,0},{8,12},{12,8},{16,20},{20,16},{24,28},{28,24},{1,5},{5... | collective-permute-start | bytes 1572872 | tf_op jit(solution)/shard_map/ppermute | solution.py:75
  74.2 15.2 %collective-permute-start.25 = (bf16[3,80,1024]{2,1,0:T(8,128)(2,1)}, bf16[3,80,1024]{2,1,0:T(8,128)(2,1)S(1)}, u32[]{:S(2)}, u32[]{:S(2)}) collective-permute-start(bf16[3,80,1024]{2,1,0:T(8,128)(2,1)} %copy-done.12), channel_id=1, source_target_pairs={{0,24},{4,28},{8,16},{12,20},{16,8},{20,12},{24,0},{28,4},{1,25},{... | collective-permute-start | bytes 1474568 | tf_op jit(solution)/shard_map/ppermute | solution.py:75
  75.7 23.3 %collective-permute-start.24 = (bf16[3,80,1024]{2,1,0:T(8,128)(2,1)}, bf16[3,80,1024]{2,1,0:T(8,128)(2,1)S(1)}, u32[]{:S(2)}, u32[]{:S(2)}) collective-permute-start(bf16[3,80,1024]{2,1,0:T(8,128)(2,1)} %copy-done.12), channel_id=1, source_target_pairs={{0,16},{4,20},{8,24},{12,28},{16,0},{20,4},{24,8},{28,12},{1,17},{... | collective-permute-start | bytes 1474568 | tf_op jit(solution)/shard_map/ppermute | solution.py:75
  77.2 21.9 %collective-permute-start.23 = (bf16[3,80,1024]{2,1,0:T(8,128)(2,1)}, bf16[3,80,1024]{2,1,0:T(8,128)(2,1)S(1)}, u32[]{:S(2)}, u32[]{:S(2)}) collective-permute-start(bf16[3,80,1024]{2,1,0:T(8,128)(2,1)} %copy-done.12), channel_id=1, source_target_pairs={{0,8},{4,12},{8,0},{12,4},{16,24},{20,28},{24,16},{28,20},{1,9},{5... | collective-permute-start | bytes 1474568 | tf_op jit(solution)/shard_map/ppermute | solution.py:75
  77.7 3.7 %collective-permute-start.21 = (bf16[4,2,64,512]{3,2,1,0:T(8,128)(2,1)S(1)}, bf16[4,2,64,512]{3,2,1,0:T(8,128)(2,1)S(1)}, u32[]{:S(2)}, u32[]{:S(2)}) collective-permute-start(bf16[4,2,64,512]{3,2,1,0:T(8,128)(2,1)S(1)} %collective-permute-done.15.refs_6_), channel_id=1, source_target_pairs={{0,4},{4,0},{8,12},{12,8},{16,20},{20,16},{24,28},{28,24},{1,5},{5... | collective-permute-start | bytes 1572872 | tf_op jit(solution)/shard_map/ppermute | solution.py:75
  80.8 2.1 collective-permute-start.20
  81.4 2.3 collective-permute-start.19
  81.5 17.5 %copy-start.13 = (bf16[3,80,1024]{2,1,0:T(8,128)(2,1)S(1)}, bf16[3,80,1024]{2,1,0:T(8,128)(2,1)}, u32[]{:S(2)}) copy-start(bf16[3,80,1024]{2,1,0:T(8,128)(2,1)} %copy-done.12) | copy-start | bytes 1474564
  99.2 4.0 %collective-permute-start.26 = (bf16[3,4,1,80,1024]{4,3,2,1,0:T(8,128)(2,1)S(1)}, bf16[3,4,1,80,1024]{4,3,2,1,0:T(8,128)(2,1)S(1)}, u32[]{:S(2)}, u32[]{:S(2)}) collective-permute-start(bf16[3,4,1,80,1024]{4,3,2,1,0:T(8,128)(2,1)S(1)} %bitcast.182), channel_id=1, source_target_pairs={{0,4},{4,0},{8,12},{12,8},{16,20},{20,16},{24,28},{28,24},{1,5},{5... | collective-permute-start | bytes 5898248 | tf_op jit(solution)/shard_map/ppermute | solution.py:75
  101.3 6.7 %collective-permute-start.22 = (bf16[128,640]{1,0:T(8,128)(2,1)S(1)}, bf16[128,640]{1,0:T(8,128)(2,1)S(1)}, u32[]{:S(2)}, u32[]{:S(2)}) collective-permute-start(bf16[128,640]{1,0:T(8,128)(2,1)S(1)} %multiply_convert_fusion.5), channel_id=1, source_target_pairs={{0,1},{1,0},{2,3},{3,2},{4,5},{5,4},{6,7},{7,6},{8,9},{9,8},{10,11... | collective-permute-start | bytes 491528 | tf_op jit(solution)/shard_map/ppermute | solution.py:75
  109.9 5.9 %collective-permute-start.27 = (bf16[128,640]{1,0:T(8,128)(2,1)S(1)}, bf16[128,640]{1,0:T(8,128)(2,1)S(1)}, u32[]{:S(2)}, u32[]{:S(2)}) collective-permute-start(bf16[128,640]{1,0:T(8,128)(2,1)S(1)} %split.269), channel_id=1, source_target_pairs={{0,1},{1,0},{2,3},{3,2},{4,5},{5,4},{6,7},{7,6},{8,9},{9,8},{10,11... | collective-permute-start | bytes 491528 | tf_op jit(solution)/shard_map/ppermute | solution.py:75
  116.6 5.4 %collective-permute-start.28 = (bf16[128,640]{1,0:T(8,128)(2,1)S(1)}, bf16[128,640]{1,0:T(8,128)(2,1)S(1)}, u32[]{:S(2)}, u32[]{:S(2)}) collective-permute-start(bf16[128,640]{1,0:T(8,128)(2,1)S(1)} %multiply_convert_fusion.4), channel_id=1, source_target_pairs={{0,1},{1,0},{2,3},{3,2},{4,5},{5,4},{6,7},{7,6},{8,9},{9,8},{10,11... | collective-permute-start | bytes 491528 | tf_op jit(solution)/shard_map/ppermute | solution.py:75
  126.1 18.1 %collective-permute-start.30 = (bf16[3,4,80,1024]{3,2,1,0:T(8,128)(2,1)S(1)}, bf16[3,4,80,1024]{3,2,1,0:T(8,128)(2,1)S(1)}, u32[]{:S(2)}, u32[]{:S(2)}) collective-permute-start(bf16[3,4,80,1024]{3,2,1,0:T(8,128)(2,1)S(1)} %slice_bitcast_fusion), channel_id=1, source_target_pairs={{0,4},{4,0},{8,12},{12,8},{16,20},{20,16},{24,28},{28,24},{1,5},{5... | collective-permute-start | bytes 5898248 | tf_op jit(solution)/shard_map/ppermute | solution.py:75
  126.8 6.7 %collective-permute-start.29 = (bf16[128,640]{1,0:T(8,128)(2,1)S(1)}, bf16[128,640]{1,0:T(8,128)(2,1)S(1)}, u32[]{:S(2)}, u32[]{:S(2)}) collective-permute-start(bf16[128,640]{1,0:T(8,128)(2,1)S(1)} %split.268), channel_id=1, source_target_pairs={{0,1},{1,0},{2,3},{3,2},{4,5},{5,4},{6,7},{7,6},{8,9},{9,8},{10,11... | collective-permute-start | bytes 491528 | tf_op jit(solution)/shard_map/ppermute | solution.py:75
  145.3 15.1 %collective-permute-start.33 = (bf16[3,80,1024]{2,1,0:T(8,128)(2,1)S(1)}, bf16[3,80,1024]{2,1,0:T(8,128)(2,1)S(1)}, u32[]{:S(2)}, u32[]{:S(2)}) collective-permute-start(bf16[3,80,1024]{2,1,0:T(8,128)(2,1)S(1)} %get-tuple-element.165), channel_id=1, source_target_pairs={{0,24},{4,28},{8,16},{12,20},{16,8},{20,12},{24,0},{28,4},{1,25},{... | collective-permute-start | bytes 1474568 | tf_op jit(solution)/shard_map/ppermute | solution.py:75
  146.8 22.7 %collective-permute-start.32 = (bf16[3,80,1024]{2,1,0:T(8,128)(2,1)S(1)}, bf16[3,80,1024]{2,1,0:T(8,128)(2,1)S(1)}, u32[]{:S(2)}, u32[]{:S(2)}) collective-permute-start(bf16[3,80,1024]{2,1,0:T(8,128)(2,1)S(1)} %get-tuple-element.166), channel_id=1, source_target_pairs={{0,16},{4,20},{8,24},{12,28},{16,0},{20,4},{24,8},{28,12},{1,17},{... | collective-permute-start | bytes 1474568 | tf_op jit(solution)/shard_map/ppermute | solution.py:75
  148.2 21.3 %collective-permute-start.31 = (bf16[3,80,1024]{2,1,0:T(8,128)(2,1)S(1)}, bf16[3,80,1024]{2,1,0:T(8,128)(2,1)S(1)}, u32[]{:S(2)}, u32[]{:S(2)}) collective-permute-start(bf16[3,80,1024]{2,1,0:T(8,128)(2,1)S(1)} %get-tuple-element.167), channel_id=1, source_target_pairs={{0,8},{4,12},{8,0},{12,4},{16,24},{20,28},{24,16},{28,20},{1,9},{5... | collective-permute-start | bytes 1474568 | tf_op jit(solution)/shard_map/ppermute | solution.py:75
  169.5 4.2 %collective-permute-start.34 = (bf16[4,4,2,64,512]{4,3,2,1,0:T(8,128)(2,1)S(1)}, bf16[4,4,2,64,512]{4,3,2,1,0:T(8,128)(2,1)S(1)}, u32[]{:S(2)}, u32[]{:S(2)}) collective-permute-start(bf16[4,4,2,64,512]{4,3,2,1,0:T(8,128)(2,1)S(1)} %get-tuple-element.75), channel_id=1, source_target_pairs={{0,4},{4,0},{8,12},{12,8},{16,20},{20,16},{24,28},{28,24},{1,5},{5... | collective-permute-start | bytes 6291464 | tf_op jit(solution)/shard_map/ppermute | solution.py:75
  170.9 14.6 %collective-permute-start.53 = (bf16[3,80,512]{2,1,0:T(8,128)(2,1)S(1)}, bf16[3,80,512]{2,1,0:T(8,128)(2,1)S(1)}, u32[]{:S(2)}, u32[]{:S(2)}) collective-permute-start(bf16[3,80,512]{2,1,0:T(8,128)(2,1)S(1)} %split.210), channel_id=1, source_target_pairs={{0,2},{1,3},{2,0},{3,1},{4,6},{5,7},{6,4},{7,5},{8,10},{9,11},{10,... | collective-permute-start | bytes 737288 | tf_op jit(solution)/shard_map/ppermute | solution.py:75
  175.7 32.0 %collective-permute-start.41 = (bf16[2,4,80,1024]{3,2,1,0:T(8,128)(2,1)S(1)}, bf16[2,4,80,1024]{3,2,1,0:T(8,128)(2,1)S(1)}, u32[]{:S(2)}, u32[]{:S(2)}) collective-permute-start(bf16[2,4,80,1024]{3,2,1,0:T(8,128)(2,1)S(1)} %fusion.13), channel_id=1, source_target_pairs={{0,4},{4,0},{8,12},{12,8},{16,20},{20,16},{24,28},{28,24},{1,5},{5... | collective-permute-start | bytes 3932168 | tf_op jit(solution)/shard_map/ppermute | solution.py:75
  176.0 14.8 %collective-permute-start.35 = (bf16[1,4,2,64,512]{4,3,2,1,0:T(8,128)(2,1)S(1)}, bf16[1,4,2,64,512]{4,3,2,1,0:T(8,128)(2,1)S(1)}, u32[]{:S(2)}, u32[]{:S(2)}) collective-permute-start(bf16[1,4,2,64,512]{4,3,2,1,0:T(8,128)(2,1)S(1)} %get-tuple-element.160), channel_id=1, source_target_pairs={{0,8},{4,12},{8,0},{12,4},{16,24},{20,28},{24,16},{28,20},{1,9},{5... | collective-permute-start | bytes 1572872 | tf_op jit(solution)/shard_map/ppermute | solution.py:75
  177.4 24.9 %collective-permute-start.37 = (bf16[1,4,2,64,512]{4,3,2,1,0:T(8,128)(2,1)S(1)}, bf16[1,4,2,64,512]{4,3,2,1,0:T(8,128)(2,1)S(1)}, u32[]{:S(2)}, u32[]{:S(2)}) collective-permute-start(bf16[1,4,2,64,512]{4,3,2,1,0:T(8,128)(2,1)S(1)} %get-tuple-element.161), channel_id=1, source_target_pairs={{0,24},{4,28},{8,16},{12,20},{16,8},{20,12},{24,0},{28,4},{1,25},{... | collective-permute-start | bytes 1572872 | tf_op jit(solution)/shard_map/ppermute | solution.py:75
  178.9 24.9 %collective-permute-start.36 = (bf16[1,4,2,64,512]{4,3,2,1,0:T(8,128)(2,1)S(1)}, bf16[1,4,2,64,512]{4,3,2,1,0:T(8,128)(2,1)S(1)}, u32[]{:S(2)}, u32[]{:S(2)}) collective-permute-start(bf16[1,4,2,64,512]{4,3,2,1,0:T(8,128)(2,1)S(1)} %get-tuple-element.162), channel_id=1, source_target_pairs={{0,16},{4,20},{8,24},{12,28},{16,0},{20,4},{24,8},{28,12},{1,17},{... | collective-permute-start | bytes 1572872 | tf_op jit(solution)/shard_map/ppermute | solution.py:75
  204.1 7.8 %collective-permute-start.38 = (bf16[1,2,64,512]{3,2,1,0:T(8,128)(2,1)S(1)}, bf16[1,2,64,512]{3,2,1,0:T(8,128)(2,1)S(1)}, u32[]{:S(2)}, u32[]{:S(2)}) collective-permute-start(bf16[1,2,64,512]{3,2,1,0:T(8,128)(2,1)S(1)} %get-tuple-element.183), channel_id=1, source_target_pairs={{0,1},{1,0},{2,3},{3,2},{4,5},{5,4},{6,7},{7,6},{8,9},{9,8},{10,11... | collective-permute-start | bytes 393224 | tf_op jit(solution)/shard_map/ppermute | solution.py:75
  205.0 8.2 %collective-permute-start.40 = (bf16[1,2,64,512]{3,2,1,0:T(8,128)(2,1)S(1)}, bf16[1,2,64,512]{3,2,1,0:T(8,128)(2,1)S(1)}, u32[]{:S(2)}, u32[]{:S(2)}) collective-permute-start(bf16[1,2,64,512]{3,2,1,0:T(8,128)(2,1)S(1)} %get-tuple-element.184), channel_id=1, source_target_pairs={{0,3},{1,2},{2,1},{3,0},{4,7},{5,6},{6,5},{7,4},{8,11},{9,10},{10,... | collective-permute-start | bytes 393224 | tf_op jit(solution)/shard_map/ppermute | solution.py:75
  206.2 11.9 %collective-permute-start.39 = (bf16[1,2,64,512]{3,2,1,0:T(8,128)(2,1)S(1)}, bf16[1,2,64,512]{3,2,1,0:T(8,128)(2,1)S(1)}, u32[]{:S(2)}, u32[]{:S(2)}) collective-permute-start(bf16[1,2,64,512]{3,2,1,0:T(8,128)(2,1)S(1)} %get-tuple-element.185), channel_id=1, source_target_pairs={{0,2},{1,3},{2,0},{3,1},{4,6},{5,7},{6,4},{7,5},{8,10},{9,11},{10,... | collective-permute-start | bytes 393224 | tf_op jit(solution)/shard_map/ppermute | solution.py:75
  208.3 11.6 %collective-permute-start.44 = (bf16[2,80,1024]{2,1,0:T(8,128)(2,1)S(1)}, bf16[2,80,1024]{2,1,0:T(8,128)(2,1)S(1)}, u32[]{:S(2)}, u32[]{:S(2)}) collective-permute-start(bf16[2,80,1024]{2,1,0:T(8,128)(2,1)S(1)} %get-tuple-element.168), channel_id=1, source_target_pairs={{0,24},{4,28},{8,16},{12,20},{16,8},{20,12},{24,0},{28,4},{1,25},{... | collective-permute-start | bytes 983048 | tf_op jit(solution)/shard_map/ppermute | solution.py:75
  209.9 14.1 %collective-permute-start.43 = (bf16[2,80,1024]{2,1,0:T(8,128)(2,1)S(1)}, bf16[2,80,1024]{2,1,0:T(8,128)(2,1)S(1)}, u32[]{:S(2)}, u32[]{:S(2)}) collective-permute-start(bf16[2,80,1024]{2,1,0:T(8,128)(2,1)S(1)} %get-tuple-element.169), channel_id=1, source_target_pairs={{0,16},{4,20},{8,24},{12,28},{16,0},{20,4},{24,8},{28,12},{1,17},{... | collective-permute-start | bytes 983048 | tf_op jit(solution)/shard_map/ppermute | solution.py:75
  211.9 12.1 %collective-permute-start.42 = (bf16[2,80,1024]{2,1,0:T(8,128)(2,1)S(1)}, bf16[2,80,1024]{2,1,0:T(8,128)(2,1)S(1)}, u32[]{:S(2)}, u32[]{:S(2)}) collective-permute-start(bf16[2,80,1024]{2,1,0:T(8,128)(2,1)S(1)} %get-tuple-element.170), channel_id=1, source_target_pairs={{0,8},{4,12},{8,0},{12,4},{16,24},{20,28},{24,16},{28,20},{1,9},{5... | collective-permute-start | bytes 983048 | tf_op jit(solution)/shard_map/ppermute | solution.py:75
  231.8 2.1 collective-permute-start.46
  233.3 1.8 collective-permute-start.45
  235.3 5.5 %collective-permute-start.47 = (bf16[92,512]{1,0:T(8,128)(2,1)S(1)}, bf16[92,512]{1,0:T(8,128)(2,1)S(1)}, u32[]{:S(2)}, u32[]{:S(2)}) collective-permute-start(bf16[92,512]{1,0:T(8,128)(2,1)S(1)} %get-tuple-element.234), channel_id=1, source_target_pairs={{0,8},{4,12},{8,0},{12,4},{16,24},{20,28},{24,16},{28,20},{1,9},{5... | collective-permute-start | bytes 282632 | tf_op jit(solution)/shard_map/ppermute | solution.py:75
  236.3 6.9 %collective-permute-start.48 = (bf16[92,512]{1,0:T(8,128)(2,1)S(1)}, bf16[92,512]{1,0:T(8,128)(2,1)S(1)}, u32[]{:S(2)}, u32[]{:S(2)}) collective-permute-start(bf16[92,512]{1,0:T(8,128)(2,1)S(1)} %get-tuple-element.235), channel_id=1, source_target_pairs={{0,16},{4,20},{8,24},{12,28},{16,0},{20,4},{24,8},{28,12},{1,17},{... | collective-permute-start | bytes 282632 | tf_op jit(solution)/shard_map/ppermute | solution.py:75
  237.5 5.7 %collective-permute-start.49 = (bf16[92,512]{1,0:T(8,128)(2,1)S(1)}, bf16[92,512]{1,0:T(8,128)(2,1)S(1)}, u32[]{:S(2)}, u32[]{:S(2)}) collective-permute-start(bf16[92,512]{1,0:T(8,128)(2,1)S(1)} %get-tuple-element.236), channel_id=1, source_target_pairs={{0,24},{4,28},{8,16},{12,20},{16,8},{20,12},{24,0},{28,4},{1,25},{... | collective-permute-start | bytes 282632 | tf_op jit(solution)/shard_map/ppermute | solution.py:75
  243.5 7.4 %collective-permute-start.50 = (bf16[224,256]{1,0:T(8,128)(2,1)S(1)}, bf16[224,256]{1,0:T(8,128)(2,1)S(1)}, u32[]{:S(2)}, u32[]{:S(2)}) collective-permute-start(bf16[224,256]{1,0:T(8,128)(2,1)S(1)} %get-tuple-element.237), channel_id=1, source_target_pairs={{0,1},{1,0},{2,3},{3,2},{4,5},{5,4},{6,7},{7,6},{8,9},{9,8},{10,11... | collective-permute-start | bytes 344072 | tf_op jit(solution)/shard_map/ppermute | solution.py:75
  246.1 12.2 %copy-start.34 = (f32[256,80]{0,1:T(8,128)S(1)}, f32[256,80]{0,1:T(8,128)}, u32[]{:S(2)}) copy-start(f32[256,80]{0,1:T(8,128)} %param.34) | copy-start | bytes 245764
  248.4 9.4 %collective-permute-start.51 = (bf16[224,256]{1,0:T(8,128)(2,1)S(1)}, bf16[224,256]{1,0:T(8,128)(2,1)S(1)}, u32[]{:S(2)}, u32[]{:S(2)}) collective-permute-start(bf16[224,256]{1,0:T(8,128)(2,1)S(1)} %get-tuple-element.238), channel_id=1, source_target_pairs={{0,2},{1,3},{2,0},{3,1},{4,6},{5,7},{6,4},{7,5},{8,10},{9,11},{10,... | collective-permute-start | bytes 344072 | tf_op jit(solution)/shard_map/ppermute | solution.py:75
  248.7 9.0 %collective-permute-start.52 = (bf16[224,256]{1,0:T(8,128)(2,1)S(1)}, bf16[224,256]{1,0:T(8,128)(2,1)S(1)}, u32[]{:S(2)}, u32[]{:S(2)}) collective-permute-start(bf16[224,256]{1,0:T(8,128)(2,1)S(1)} %get-tuple-element.239), channel_id=1, source_target_pairs={{0,3},{1,2},{2,1},{3,0},{4,7},{5,6},{6,5},{7,4},{8,11},{9,10},{10,... | collective-permute-start | bytes 344072 | tf_op jit(solution)/shard_map/ppermute | solution.py:75
  (45 other events, 225.9 us)
